TPU v7x, 32 devices: a whole 2x2x4 slice. The times are simulated.
32 devices in a mesh: groups: 2 (over y), ctx: 4 (over z), chan: 2 (over x), sub: 2 (over core).
Axes of the slice: x: 2, y: 2, z: 4, core: 2. Of those that a mesh axis runs over, the one named last changes fastest.
Arguments:
- sequence: bfloat16 [2048, 4096], P(('groups', 'ctx'), ('chan', 'sub')), parts along dimension 0, may hold values from -6 to 6
- gate: bfloat16 [2048, 4096], P(('groups', 'ctx'), ('chan', 'sub')), parts along dimension 0, may hold values from -6 to 6
- filters: float32 [32, 768], P(('chan', 'sub')), may hold values from -0.21875 to 0.21875
- lengths: int32 [32], P(('chan', 'sub')), may hold values from 1 to 3, as said below
- gain: float32 [4096], P(('chan', 'sub')), may hold values from 0.5 to 2
- permutation: int32 [128], replicated, may hold values from 0 to 127, each once
Outputs:
- mixed: bfloat16 [2048, 4096], P(('groups', 'ctx'), ('chan', 'sub')), parts along dimension 0
There are 2 independent parts, one for each index of `groups`. A program takes and returns all parts, laid end to end along the dimension named above; an argument that names none is the same for every part. Nothing has to cross between parts.
Inputs may be any that keep to these rules, and one draw needn't show every extreme that they name: Filter lengths in blocks of 256 taps; some group has length 3 and some group length 1. A permutation of the 128 channel indices of a group, the same for every group.
All inputs are finite; a program needn't handle non-finite values.
Results may differ from a plain program's by a relative error of at most 0.0065.
Values may be sent and summed in bfloat16 or wider, within the bound.
No kernel may reach another device: no remote copies, remote signals or barrier semaphores. Data moves between devices by JAX's collectives and lax.ppermute only.
A program may use at most 64 MiB of HBM per device.

v0:
```python
import jax
import jax.numpy as jnp
from jax import lax
from jax.sharding import PartitionSpec as P

LMAX = 3


def shifted(array, axis, by):
    count = lax.axis_size(axis)
    pairs = [(i, i + by) for i in range(count) if 0 <= i + by < count]
    return lax.ppermute(array, axis, pairs)


def build_blocks(kernel, rows):
    groups_dev = kernel.shape[0]
    padded = jnp.pad(kernel, ((0, 0), (rows, rows)))
    blocks = []
    for lag in range(LMAX + 1):
        window = padded[:, lag * rows : lag * rows + 2 * rows][:, ::-1]
        tiled = jnp.tile(window, (1, rows))[:, : rows * (2 * rows - 1)]
        skewed = tiled.reshape(groups_dev, rows, 2 * rows - 1)
        blocks.append(skewed[:, :, rows - 1 : 2 * rows - 1])
    return blocks


def block_product(matrix, inputs, forward):
    if forward:
        return jnp.einsum("gst,tgc->sgc", matrix, inputs, preferred_element_type=jnp.float32)
    return jnp.einsum("gts,tgc->sgc", matrix, inputs, preferred_element_type=jnp.float32)


def convolve(inputs, blocks, sign):
    forward = sign > 0
    result = block_product(blocks[0], inputs, forward)
    for lag in range(1, LMAX + 1):
        result = result + shifted(block_product(blocks[lag], inputs, forward), "ctx", sign * lag)
    return result


def body(sequence, gate, filters, lengths, gain, permutation):
    rows, width = sequence.shape
    groups_dev = filters.shape[0]
    group_w = permutation.shape[0]
    tap_ids = lax.broadcasted_iota(jnp.int32, filters.shape, 1)
    kernel = jnp.where(tap_ids < lengths[:, None] * rows, filters, jnp.float32(0.0)).astype(
        jnp.bfloat16
    )
    blocks = build_blocks(kernel, rows)
    seq3 = sequence.reshape(rows, groups_dev, group_w)
    gain3 = gain.reshape(groups_dev, group_w)
    gated = (seq3.astype(jnp.float32) * gain3[None]).astype(jnp.bfloat16)
    ahead = convolve(gated, blocks, 1)
    target_ids = lax.broadcasted_iota(jnp.int32, (group_w, group_w), 1)
    match = permutation[:, None] == target_ids
    gain_rc = jnp.sum(jnp.where(match[None], gain3[:, :, None], jnp.float32(0.0)), axis=1)
    rc_input = (seq3.astype(jnp.float32) * gain_rc[None]).astype(jnp.bfloat16)
    behind = convolve(rc_input, blocks, -1).astype(jnp.bfloat16)
    mixed = gate.reshape(rows, groups_dev, group_w).astype(jnp.float32) * (
        ahead + behind.astype(jnp.float32)
    )
    return mixed.astype(jnp.bfloat16).reshape(rows, width)


def solution(mesh):
    in_specs = (
        P(("groups", "ctx"), ("chan", "sub")),
        P(("groups", "ctx"), ("chan", "sub")),
        P(("chan", "sub"), None),
        P(("chan", "sub")),
        P(("chan", "sub")),
        P(),
    )
    out_specs = P(("groups", "ctx"), ("chan", "sub"))
    return jax.shard_map(body, mesh=mesh, in_specs=in_specs, out_specs=out_specs, check_vma=False)
```

profile of v0, /device:TPU:27, one launch (start us, length us, event | category | flops | bytes accessed | tf_op | source)
XLA Modules:
  0.0 136.6 jit_solution(18327637480622777534)
XLA Ops:
  0.0 0.7 broadcast_multiply_fusion
  0.7 0.7 iota_compare_fusion
  1.4 0.8 select_convert_fusion
  2.5 2.2 %copy.19 = f32[256,1024]{0,1:T(8,128)} copy(bf16[256,1024]{1,0:T(8,128)(2,1)} %param.6) | data formatting | bytes 1572864 | tf_op jit(solution)/shard_map/convert_element_type | solution.py:52
  5.0 4.5 %reshape.68 = bf16[1046528]{0:T(1024)(128)(2,1)} reshape(bf16[8,130816]{1,0:T(8,128)(2,1)S(1)} %slice.53) | data formatting | bytes 4186112
  9.5 5.0 %reshape.58 = bf16[8,256,511]{2,1,0:T(8,128)(2,1)S(1)} reshape(bf16[1046528]{0:T(1024)(128)(2,1)} %reshape.68) | data formatting | bytes 4186112 | tf_op jit(solution)/shard_map/reshape | solution.py:22
  14.8 1.6 %multiply_convert_fusion.1 = (bf16[256,8,128]{0,2,1:T(8,128)(2,1)S(1)}, bf16[256,8,128]{0,2,1:T(8,128)(2,1)S(1)}) fusion(f32[256,8,128]{0,2,1:T(8,128)} %bitcast.59, f32[8,128]{1,0:T(8,128)S(1)} %bitcast.62, f32[8,128]{1,0:T(8,128)S(1)} %select_reduce_fusion), kind=kLoop, calls=%fused_computation.20 | loop fusion | flops 1048576 | bytes 2105344 | tf_op jit(solution)/shard_map/convert_element_type | solution.py:52
  16.3 1.6 %convolution_bitcast_fusion.6 = f32[256,8,128]{0,2,1:T(8,128)} fusion(bf16[256,8,128]{0,2,1:T(8,128)(2,1)S(1)} %get-tuple-element.5, bf16[8,256,511]{2,1,0:T(8,128)(2,1)S(1)} %reshape.58), kind=kOutput, calls=%fused_computation.9 | convolution fusion | flops 134217728 | bytes 2621440 | tf_op jit(solution)/shard_map/gst,tgc->sgc/dot_general | solution.py:29
  17.9 1.3 collective-permute-start
  19.2 1.5 %convolution_bitcast_fusion.2 = f32[256,8,128]{0,2,1:T(8,128)} fusion(bf16[256,8,128]{0,2,1:T(8,128)(2,1)S(1)} %get-tuple-element.6, bf16[8,256,511]{2,1,0:T(8,128)(2,1)S(1)} %reshape.58), kind=kOutput, calls=%fused_computation.2 | convolution fusion | flops 134217728 | bytes 2621440 | tf_op jit(solution)/shard_map/gts,tgc->sgc/dot_general | solution.py:30
  20.7 5.0 %collective-permute-start.3 = (f32[256,8,128]{0,2,1:T(8,128)}, f32[256,8,128]{0,2,1:T(8,128)}, u32[]{:S(2)}, u32[]{:S(2)}) collective-permute-start(f32[256,8,128]{0,2,1:T(8,128)} %convolution_bitcast_fusion.2), channel_id=1, source_target_pairs={{4,0},{8,4},{12,8},{5,1},{9,5},{13,9},{6,2},{10,6},{14,10},{7,3},{... | collective-permute-start | bytes 3145736 | tf_op jit(solution)/shard_map/ppermute | solution.py:12
  26.3 4.5 %reshape.66 = bf16[1046528]{0:T(1024)(128)(2,1)} reshape(bf16[8,130816]{1,0:T(8,128)(2,1)S(1)} %slice.56) | data formatting | bytes 4186112
  30.7 5.0 %reshape.59 = bf16[8,256,511]{2,1,0:T(8,128)(2,1)S(1)} reshape(bf16[1046528]{0:T(1024)(128)(2,1)} %reshape.66) | data formatting | bytes 4186112 | tf_op jit(solution)/shard_map/reshape | solution.py:22
  35.8 1.5 %convolution_bitcast_fusion.1 = f32[256,8,128]{0,2,1:T(8,128)} fusion(bf16[256,8,128]{0,2,1:T(8,128)(2,1)S(1)} %get-tuple-element.6, bf16[8,256,511]{2,1,0:T(8,128)(2,1)S(1)} %reshape.59), kind=kOutput, calls=%fused_computation.1 | convolution fusion | flops 134217728 | bytes 2621440 | tf_op jit(solution)/shard_map/gts,tgc->sgc/dot_general | solution.py:30
  37.3 3.1 %collective-permute-start.4 = (f32[256,8,128]{0,2,1:T(8,128)}, f32[256,8,128]{0,2,1:T(8,128)}, u32[]{:S(2)}, u32[]{:S(2)}) collective-permute-start(f32[256,8,128]{0,2,1:T(8,128)} %convolution_bitcast_fusion.1), channel_id=1, source_target_pairs={{8,0},{12,4},{9,1},{13,5},{10,2},{14,6},{11,3},{15,7},{24,16},{28,... | collective-permute-start | bytes 3145736 | tf_op jit(solution)/shard_map/ppermute | solution.py:12
  40.8 1.4 %slice.58 = bf16[8,130816]{1,0:T(8,128)(2,1)} slice(bf16[8,131072]{1,0:T(8,128)(2,1)S(1)} %bitcast.56), slice={[0:8], [0:130816]} | slice | bytes 4186112 | tf_op jit(solution)/shard_map/slice | solution.py:21
  42.3 6.1 %reshape.64 = bf16[1046528]{0:T(1024)(128)(2,1)} reshape(bf16[8,130816]{1,0:T(8,128)(2,1)} %slice.58) | data formatting | bytes 4186112
  48.4 6.0 %reshape.60 = bf16[8,256,511]{2,1,0:T(8,128)(2,1)} reshape(bf16[1046528]{0:T(1024)(128)(2,1)} %reshape.64) | data formatting | bytes 4186112 | tf_op jit(solution)/shard_map/reshape | solution.py:22
  54.5 3.1 %convolution_bitcast_fusion = f32[256,8,128]{0,2,1:T(8,128)} fusion(bf16[256,8,128]{0,2,1:T(8,128)(2,1)S(1)} %get-tuple-element.6, bf16[8,256,511]{2,1,0:T(8,128)(2,1)} %reshape.60), kind=kOutput, calls=%fused_computation | convolution fusion | flops 134217728 | bytes 2621440 | tf_op jit(solution)/shard_map/gts,tgc->sgc/dot_general | solution.py:30
  57.5 2.3 %collective-permute-start.5 = (f32[256,8,128]{0,2,1:T(8,128)}, f32[256,8,128]{0,2,1:T(8,128)}, u32[]{:S(2)}, u32[]{:S(2)}) collective-permute-start(f32[256,8,128]{0,2,1:T(8,128)} %convolution_bitcast_fusion), channel_id=1, source_target_pairs={{12,0},{13,1},{14,2},{15,3},{28,16},{29,17},{30,18},{31,19}} | collective-permute-start | bytes 3145736 | tf_op jit(solution)/shard_map/ppermute | solution.py:12
  59.9 1.5 %convolution_bitcast_fusion.5 = f32[256,8,128]{0,2,1:T(8,128)} fusion(bf16[256,8,128]{0,2,1:T(8,128)(2,1)S(1)} %get-tuple-element.5, bf16[8,256,511]{2,1,0:T(8,128)(2,1)S(1)} %reshape.59), kind=kOutput, calls=%fused_computation.8 | convolution fusion | flops 134217728 | bytes 2621440 | tf_op jit(solution)/shard_map/gst,tgc->sgc/dot_general | solution.py:29
  61.4 1.3 collective-permute-start.1
  62.7 1.5 %convolution_bitcast_fusion.4 = f32[256,8,128]{0,2,1:T(8,128)} fusion(bf16[256,8,128]{0,2,1:T(8,128)(2,1)S(1)} %get-tuple-element.5, bf16[8,256,511]{2,1,0:T(8,128)(2,1)S(1)} %copy-done), kind=kOutput, calls=%fused_computation.7 | convolution fusion | flops 134217728 | bytes 2621440 | tf_op jit(solution)/shard_map/gst,tgc->sgc/dot_general | solution.py:29
  64.2 1.3 collective-permute-start.2
  65.8 2.2 %copy.15 = f32[256,1024]{0,1:T(8,128)} copy(bf16[256,1024]{1,0:T(8,128)(2,1)} %param.7) | data formatting | bytes 1572864 | tf_op jit(solution)/shard_map/convert_element_type | solution.py:59
  68.4 4.4 %reshape.70 = bf16[1046528]{0:T(1024)(128)(2,1)} reshape(bf16[8,130816]{1,0:T(8,128)(2,1)S(1)} %slice.50) | data formatting | bytes 4186112
  72.8 5.0 %reshape.57 = bf16[8,256,511]{2,1,0:T(8,128)(2,1)S(1)} reshape(bf16[1046528]{0:T(1024)(128)(2,1)} %reshape.70) | data formatting | bytes 4186112 | tf_op jit(solution)/shard_map/reshape | solution.py:22
  77.8 13.6 %collective-permute-done.5 = f32[256,8,128]{0,2,1:T(8,128)} collective-permute-done((f32[256,8,128]{0,2,1:T(8,128)}, f32[256,8,128]{0,2,1:T(8,128)}, u32[]{:S(2)}, u32[]{:S(2)}) %collective-permute-start.5) | collective-permute-done | bytes 1048608 | tf_op jit(solution)/shard_map/ppermute | solution.py:12
  91.5 2.4 %fusion.10 = f32[256,8,128]{0,2,1:T(8,128)S(1)} fusion(f32[256,8,128]{0,2,1:T(8,128)} %collective-permute-done.5, f32[256,8,128]{0,2,1:T(8,128)} %collective-permute-done.4, f32[256,8,128]{0,2,1:T(8,128)} %collective-permute-done.3, bf16[256,8,128]{0,2,1:T(8,128)(2,1)S(1)} %get-tuple-element.6, bf16[8,256,511]{2,1,0:T(8,128)(2,1)S(1)} %reshape.57), kind=kOutput, calls=%fused_computation.18 | convolution fusion | flops 135528448 | bytes 5767168 | tf_op jit(solution)/shard_map/gts,tgc->sgc/dot_general | solution.py:30
  93.9 39.1 %collective-permute-done.1 = f32[256,8,128]{0,2,1:T(8,128)} collective-permute-done((f32[256,8,128]{0,2,1:T(8,128)}, f32[256,8,128]{0,2,1:T(8,128)}, u32[]{:S(2)}, u32[]{:S(2)}) %collective-permute-start.1) | collective-permute-done | bytes 1048608 | tf_op jit(solution)/shard_map/ppermute | solution.py:12
  133.0 2.5 %fusion.8 = bf16[256,8,128]{0,2,1:T(8,128)(2,1)S(1)} fusion(f32[256,8,128]{0,2,1:T(8,128)S(1)} %bitcast.58, f32[256,8,128]{0,2,1:T(8,128)S(1)} %fusion.10, f32[256,8,128]{0,2,1:T(8,128)} %collective-permute-done.2, f32[256,8,128]{0,2,1:T(8,128)} %collective-permute-done.1, f32[256,8,128]{0,2,1:T(8,128)} %collective-permute-done, ...), kind=kOutput, calls=%fused_computation.16 | convolution fusion | flops 135790592 | bytes 7340032 | tf_op jit(solution)/shard_map/gst,tgc->sgc/dot_general | solution.py:29
  135.6 1.0 copy.18
  (23 shorter events, 2.5 us)
Async XLA Ops:
  9.5 5.0 %copy-start.2 = (f32[1024]{0:T(1024)S(1)}, f32[1024]{0:T(1024)}, u32[]{:S(2)}) copy-start(f32[1024]{0:T(1024)} %param.10) | copy-start | bytes 12292
  17.9 76.0 %collective-permute-start = (f32[256,8,128]{0,2,1:T(8,128)}, f32[256,8,128]{0,2,1:T(8,128)}, u32[]{:S(2)}, u32[]{:S(2)}) collective-permute-start(f32[256,8,128]{0,2,1:T(8,128)} %convolution_bitcast_fusion.6), channel_id=1, source_target_pairs={{0,4},{4,8},{8,12},{1,5},{5,9},{9,13},{2,6},{6,10},{10,14},{3,7},{... | collective-permute-start | bytes 3145736 | tf_op jit(solution)/shard_map/ppermute | solution.py:12
  20.7 43.5 %collective-permute-start.3 = (f32[256,8,128]{0,2,1:T(8,128)}, f32[256,8,128]{0,2,1:T(8,128)}, u32[]{:S(2)}, u32[]{:S(2)}) collective-permute-start(f32[256,8,128]{0,2,1:T(8,128)} %convolution_bitcast_fusion.2), channel_id=1, source_target_pairs={{4,0},{8,4},{12,8},{5,1},{9,5},{13,9},{6,2},{10,6},{14,10},{7,3},{... | collective-permute-start | bytes 3145736 | tf_op jit(solution)/shard_map/ppermute | solution.py:12
  37.3 40.6 %collective-permute-start.4 = (f32[256,8,128]{0,2,1:T(8,128)}, f32[256,8,128]{0,2,1:T(8,128)}, u32[]{:S(2)}, u32[]{:S(2)}) collective-permute-start(f32[256,8,128]{0,2,1:T(8,128)} %convolution_bitcast_fusion.1), channel_id=1, source_target_pairs={{8,0},{12,4},{9,1},{13,5},{10,2},{14,6},{11,3},{15,7},{24,16},{28,... | collective-permute-start | bytes 3145736 | tf_op jit(solution)/shard_map/ppermute | solution.py:12
  54.5 8.3 %copy-start = (bf16[8,256,511]{2,1,0:T(8,128)(2,1)S(1)}, bf16[8,256,511]{2,1,0:T(8,128)(2,1)}, u32[]{:S(2)}) copy-start(bf16[8,256,511]{2,1,0:T(8,128)(2,1)} %reshape.60) | copy-start | bytes 6279172
  57.5 34.0 %collective-permute-start.5 = (f32[256,8,128]{0,2,1:T(8,128)}, f32[256,8,128]{0,2,1:T(8,128)}, u32[]{:S(2)}, u32[]{:S(2)}) collective-permute-start(f32[256,8,128]{0,2,1:T(8,128)} %convolution_bitcast_fusion), channel_id=1, source_target_pairs={{12,0},{13,1},{14,2},{15,3},{28,16},{29,17},{30,18},{31,19}} | collective-permute-start | bytes 3145736 | tf_op jit(solution)/shard_map/ppermute | solution.py:12
  61.4 71.6 %collective-permute-start.1 = (f32[256,8,128]{0,2,1:T(8,128)}, f32[256,8,128]{0,2,1:T(8,128)}, u32[]{:S(2)}, u32[]{:S(2)}) collective-permute-start(f32[256,8,128]{0,2,1:T(8,128)} %convolution_bitcast_fusion.5), channel_id=1, source_target_pairs={{0,8},{4,12},{1,9},{5,13},{2,10},{6,14},{3,11},{7,15},{16,24},{20,... | collective-permute-start | bytes 3145736 | tf_op jit(solution)/shard_map/ppermute | solution.py:12
  64.2 68.8 %collective-permute-start.2 = (f32[256,8,128]{0,2,1:T(8,128)}, f32[256,8,128]{0,2,1:T(8,128)}, u32[]{:S(2)}, u32[]{:S(2)}) collective-permute-start(f32[256,8,128]{0,2,1:T(8,128)} %convolution_bitcast_fusion.4), channel_id=1, source_target_pairs={{0,12},{1,13},{2,14},{3,15},{16,28},{17,29},{18,30},{19,31}} | collective-permute-start | bytes 3145736 | tf_op jit(solution)/shard_map/ppermute | solution.py:12
  77.8 55.2 %copy-start.1 = (f32[256,1024]{0,1:T(8,128)S(1)}, f32[256,1024]{0,1:T(8,128)}, u32[]{:S(2)}) copy-start(f32[256,1024]{0,1:T(8,128)} %copy.15) | copy-start | bytes 3145732
where the time goes:
time: 137 us
  waiting for transfers between devices  52.8 us (39%)
  local copies, waits for them, and re-layouts  49.8 us (36%)
  matrix products  15.6 us (11%)
  starting transfers between devices  14.3 us (10%)
  other arithmetic  3.97 us (3%)
    ppermute x6, waiting for transfers between devices, shifted(): return lax.ppermute(array, axis, pairs)  52.8 us
    reshape x4, local copies, waits for them, and re-layouts, build_blocks(): skewed = tiled.reshape(groups_dev, rows, 2 * rows - 1)  21.1 us
    unnamed x10, local copies, waits for them, and re-layouts  19.5 us
    ppermute x6, starting transfers between devices, shifted(): return lax.ppermute(array, axis, pairs)  14.3 us
    dot_general x4, matrix products, block_product(): jnp.einsum('gts,tgc->sgc', matrix, inputs, preferred_element_type=jnp.flo...  8.49 us
    dot_general x4, matrix products, block_product(): jnp.einsum('gst,tgc->sgc', matrix, inputs, preferred_element_type=jnp.flo...  7.13 us
  transfers between devices with their start and end apart: 6, of which 2 were waited for; matrix products, arithmetic and copies ran while one was open for 35% of the time, Pallas kernels for 0%

commit v1 on v0

v1 whole, which is shorter than its diff:
```python
import functools

import jax
import jax.numpy as jnp
from jax import lax
from jax.experimental import pallas as pl
from jax.experimental.pallas import tpu as pltpu
from jax.sharding import PartitionSpec as P

F32, BF16 = jnp.float32, jnp.bfloat16
VMEM, SMEM = pltpu.VMEM, pltpu.SMEM


def shifted(array, by):
    count = lax.axis_size("ctx")
    return lax.ppermute(array, "ctx", [(i, i + by) for i in range(count) if 0 <= i + by < count])


def rotated(array, by):
    count = lax.axis_size("ctx")
    return lax.ppermute(array, "ctx", [(i, (i + by) % count) for i in range(count)])


def held(array):
    return pltpu.with_memory_space_constraint(array, VMEM)


def build_kernel(rows, lags, owned, filters_ref, lengths_ref, gain_ref, perm_ref, fwd_ref, bwd_ref, gains_ref):
    first = lax.axis_index("ctx") * owned
    group_w = perm_ref.shape[1]
    taps = filters_ref.shape[1]
    span = lags * rows
    target = lax.broadcasted_iota(jnp.int32, (group_w, group_w), 0)
    match = perm_ref[...] == target
    for own in range(owned):
        group = first + own
        taps_row = filters_ref[pl.ds(group, 1), :]
        tap_ids = lax.broadcasted_iota(jnp.int32, (1, taps), 1)
        taps_row = jnp.where(tap_ids < lengths_ref[group] * rows, taps_row, 0.0)
        taps_row = jnp.concatenate([taps_row, jnp.zeros((1, span - taps), F32)], axis=1)
        strip = pltpu.roll(jnp.broadcast_to(taps_row, (rows, span)), 0, 1, stride=1, stride_axis=0)
        for lag in range(lags):
            block = strip[:, lag * rows : (lag + 1) * rows]
            bwd_ref[own, lag] = block.astype(BF16)
            fwd_ref[own, lag] = block.T.astype(BF16)
        gain_row = gain_ref[pl.ds(group, 1), :]
        spread = jnp.where(match, gain_row, 0.0)
        gains_ref[own, 0:1, :] = gain_row
        gains_ref[own, 1:2, :] = jnp.sum(spread.T, axis=0, keepdims=True)


def mix_kernel(count, lags, owned, *refs):
    blocks, (fwd_ref, bwd_ref, gains_ref) = refs[:count], refs[count : count + 3]
    outs, (inputs, sums) = refs[count + 3 : 2 * count + 3], refs[2 * count + 3 :]
    me = lax.axis_index("ctx")
    group_w = gains_ref.shape[2]
    places = [lax.rem(me - k + count, count) for k in range(count)]
    for k in range(count):
        inputs[places[k]] = blocks[k][...]
    for own in range(owned):
        lanes = slice(own * group_w, (own + 1) * group_w)
        values = jnp.concatenate([inputs[i, :, lanes] for i in range(count)], axis=1).astype(F32)
        gated = (values * jnp.tile(gains_ref[own, 0:1, :], (1, count))).astype(BF16)
        flipped = (values * jnp.tile(gains_ref[own, 1:2, :], (1, count))).astype(BF16)
        ahead = [None] * count
        behind = [None] * count

        def add(total, at, value):
            total[at] = value if total[at] is None else total[at] + value

        for lag in range(min(lags, count)):
            kept = (count - lag) * group_w
            up = jnp.dot(fwd_ref[own, lag], gated[:, :kept], preferred_element_type=F32)
            down = jnp.dot(bwd_ref[own, lag], flipped[:, count * group_w - kept :], preferred_element_type=F32)
            for i in range(count - lag):
                piece = slice(i * group_w, (i + 1) * group_w)
                add(ahead, i + lag, up[:, piece])
                add(behind, i, down[:, piece])
        for i in range(count):
            sums[i, :, lanes] = (ahead[i] + behind[i].astype(BF16).astype(F32)).astype(BF16)
    for k in range(count):
        outs[k][...] = sums[places[k]]


def gate_kernel(count, gate_ref, *refs):
    blocks, out_ref = refs[:count], refs[count]
    me = lax.axis_index("ctx")
    width = blocks[0].shape[1]
    for k in range(count):
        place = pl.ds(pl.multiple_of(lax.rem(me + k, count) * width, width), width)
        out_ref[:, place] = (gate_ref[:, place].astype(F32) * blocks[k][...].astype(F32)).astype(BF16)


def dealt(sequence, gate, filters, lengths, gain, permutation):
    rows, width = sequence.shape
    count = lax.axis_size("ctx")
    groups_dev, taps = filters.shape
    group_w = permutation.shape[0]
    owned = groups_dev // count
    lags = taps // rows + 1
    chunk = owned * group_w
    me = lax.axis_index("ctx")
    vmem = pl.BlockSpec(memory_space=VMEM)

    def part(k):
        return lax.dynamic_slice(sequence, (0, lax.rem(me + k, count) * chunk), (rows, chunk))

    blocks = [part(0)] + [rotated(part(k), k) for k in range(1, count)]
    fwd, bwd, gains = pl.pallas_call(
        functools.partial(build_kernel, rows, lags, owned),
        in_specs=[vmem, pl.BlockSpec(memory_space=SMEM), vmem, vmem],
        out_specs=[vmem] * 3,
        out_shape=[VMEM((owned, lags, rows, rows), BF16)] * 2 + [VMEM((owned, 8, group_w), F32)],
        name="build",
    )(filters, lengths, gain.reshape(groups_dev, group_w), permutation.reshape(1, group_w))
    outs = pl.pallas_call(
        functools.partial(mix_kernel, count, lags, owned),
        in_specs=[vmem] * (count + 3),
        out_specs=[vmem] * count,
        out_shape=[VMEM((rows, chunk), BF16)] * count,
        scratch_shapes=[VMEM((count, rows, chunk), BF16)] * 2,
        name="mix",
    )(*map(held, [*blocks, fwd, bwd, gains]))
    back = [outs[0]] + [rotated(outs[k], -k) for k in range(1, count)]
    return pl.pallas_call(
        functools.partial(gate_kernel, count),
        in_specs=[vmem] * (count + 1),
        out_specs=vmem,
        out_shape=jax.ShapeDtypeStruct((rows, width), BF16),
        name="gate",
    )(gate, *map(held, back))


def build_blocks(kernel, rows):
    groups_dev, taps = kernel.shape
    padded = jnp.pad(kernel, ((0, 0), (rows, rows)))
    blocks = []
    for lag in range(taps // rows + 1):
        window = padded[:, lag * rows : lag * rows + 2 * rows][:, ::-1]
        tiled = jnp.tile(window, (1, rows))[:, : rows * (2 * rows - 1)]
        skewed = tiled.reshape(groups_dev, rows, 2 * rows - 1)
        blocks.append(skewed[:, :, rows - 1 : 2 * rows - 1])
    return blocks


def halos(sequence, gate, filters, lengths, gain, permutation):
    rows, width = sequence.shape
    groups_dev = filters.shape[0]
    group_w = permutation.shape[0]
    tap_ids = lax.broadcasted_iota(jnp.int32, filters.shape, 1)
    kernel = jnp.where(tap_ids < lengths[:, None] * rows, filters, 0.0).astype(BF16)
    blocks = build_blocks(kernel, rows)
    gain3 = gain.reshape(groups_dev, group_w)
    target_ids = lax.broadcasted_iota(jnp.int32, (group_w, group_w), 1)
    match = permutation[:, None] == target_ids
    gain_rc = jnp.sum(jnp.where(match[None], gain3[:, :, None], 0.0), axis=1)

    def scaled(block, gains):
        return (block.reshape(rows, groups_dev, group_w).astype(F32) * gains[None]).astype(BF16)

    ahead, behind = 0.0, 0.0
    for lag, matrix in enumerate(blocks):
        past = scaled(shifted(sequence, lag) if lag else sequence, gain3)
        later = scaled(shifted(sequence, -lag) if lag else sequence, gain_rc)
        ahead = ahead + jnp.einsum("gst,tgc->sgc", matrix, past, preferred_element_type=F32)
        behind = behind + jnp.einsum("gts,tgc->sgc", matrix, later, preferred_element_type=F32)
    gate3 = gate.reshape(rows, groups_dev, group_w).astype(F32)
    mixed = gate3 * (ahead + behind.astype(BF16).astype(F32))
    return mixed.astype(BF16).reshape(rows, width)


def body(*args):
    count = lax.axis_size("ctx")
    groups_dev = args[2].shape[0]
    if count <= 8 and groups_dev % count == 0:
        return dealt(*args)
    return halos(*args)


def solution(mesh):
    in_specs = (
        P(("groups", "ctx"), ("chan", "sub")),
        P(("groups", "ctx"), ("chan", "sub")),
        P(("chan", "sub"), None),
        P(("chan", "sub")),
        P(("chan", "sub")),
        P(),
    )
    out_specs = P(("groups", "ctx"), ("chan", "sub"))
    return jax.shard_map(body, mesh=mesh, in_specs=in_specs, out_specs=out_specs, check_vma=False)
```

time: 137 us -> 34.1 us (0.25)
  the two profiles are of different devices: /device:TPU:27 before, /device:TPU:0 now
where the time goes in v1:
time: 34.1 us; the launch traced here: 33.8 us
  waiting for transfers between devices  19.3 us (57%)
  starting transfers between devices  9.06 us (27%)
  Pallas kernels  4.33 us (13%)
  local copies, waits for them, and re-layouts  1.13 us (3%)
    ppermute x6, waiting for transfers between devices, rotated(): lax.ppermute(array, 'ctx', [(i, (i + by) % count) for i in range(count)])  19.3 us
    ppermute x6, starting transfers between devices, rotated(): lax.ppermute(array, 'ctx', [(i, (i + by) % count) for i in range(count)])  9.06 us
    pallas_call x1, Pallas kernels, dealt(): pl.pallas_call(functools.partial(gate_kernel, count), in_specs=[vmem] * (...  1.98 us
    pallas_call x1, Pallas kernels, dealt(): pl.pallas_call(functools.partial(build_kernel, rows, lags, owned), in_spe...  1.22 us
    dynamic_slice x1, local copies, waits for them, and re-layouts, part(): lax.dynamic_slice(sequence, (0, lax.rem(me + k, count) * chunk), (rows, c...  1.13 us
    pallas_call x1, Pallas kernels, dealt(): pl.pallas_call(functools.partial(mix_kernel, count, lags, owned), in_spec...  1.13 us
  transfers between devices with their start and end apart: 6, of which 5 were waited for; matrix products, arithmetic and copies ran while one was open for 0% of the time, Pallas kernels for 4%

profile of v1, /device:TPU:0, one launch (start us, length us, event | category | flops | bytes accessed | tf_op | source)
XLA Modules:
  0.0 33.8 jit_solution(9665369579491454642)
XLA Ops:
  0.0 1.1 %constant_dynamic-slice_fusion = (bf16[256,256]{1,0:T(8,128)(2,1)S(1)}, bf16[256,256]{1,0:T(8,128)(2,1)S(1)}, bf16[256,256]{1,0:T(8,128)(2,1)S(1)}, bf16[256,256]{1,0:T(8,128)(2,1)S(1)}) fusion(bf16[256,1024]{1,0:T(8,128)(2,1)} %param.6, s32[]{:T(128)S(6)} %select_n.15, s32[]{:T(128)S(6)} %select_n.13, s32[]{:T(128)S(6)} %select_n.12, s32[]{:T(128)S(6)} %select_n.14), kind=kLoop, calls=%fused_computation | loop fusion | bytes 1048592 | tf_op jit(solution)/shard_map/dynamic_slice | solution.py:106
  1.1 5.1 %collective-permute-start.2 = (bf16[256,256]{1,0:T(8,128)(2,1)S(1)}, bf16[256,256]{1,0:T(8,128)(2,1)S(1)}, u32[]{:S(2)}, u32[]{:S(2)}) collective-permute-start(bf16[256,256]{1,0:T(8,128)(2,1)S(1)} %get-tuple-element.19), channel_id=1, source_target_pairs={{0,12},{4,0},{8,4},{12,8},{1,13},{5,1},{9,5},{13,9},{2,14},{6,2},{... | collective-permute-start | bytes 393224 | tf_op jit(solution)/shard_map/ppermute | solution.py:21
  6.2 0.0 collective-permute-start
  6.2 1.0 %collective-permute-start.1 = (bf16[256,256]{1,0:T(8,128)(2,1)S(1)}, bf16[256,256]{1,0:T(8,128)(2,1)S(1)}, u32[]{:S(2)}, u32[]{:S(2)}) collective-permute-start(bf16[256,256]{1,0:T(8,128)(2,1)S(1)} %get-tuple-element.22), channel_id=1, source_target_pairs={{0,8},{4,12},{8,0},{12,4},{1,9},{5,13},{9,1},{13,5},{2,10},{6,14},... | collective-permute-start | bytes 393224 | tf_op jit(solution)/shard_map/ppermute | solution.py:21
  7.3 1.2 %build.1 = (bf16[2,4,256,256]{3,2,1,0:T(8,128)(2,1)S(1)}, bf16[2,4,256,256]{3,2,1,0:T(8,128)(2,1)S(1)}, f32[2,8,128]{2,1,0:T(8,128)S(1)}) custom-call(f32[8,768]{1,0:T(8,128)} %filters_ref.1, s32[8]{0:T(128)} %lengths_ref.1, f32[8,128]{1,0:T(8,128)} %bitcast.2, s32[1,128]{1,0:T(1,128)} %bitcast.3), custom_call_target="tpu_custom_call" | custom-call | tf_op jit(solution)/shard_map/build/pallas_call | solution.py:109
  8.5 1.7 %collective-permute-done.2.refs_3_ = bf16[256,256]{1,0:T(8,128)(2,1)S(1)} collective-permute-done((bf16[256,256]{1,0:T(8,128)(2,1)S(1)}, bf16[256,256]{1,0:T(8,128)(2,1)S(1)}, u32[]{:S(2)}, u32[]{:S(2)}) %collective-permute-start.2) | collective-permute-done | bytes 131104 | tf_op jit(solution)/shard_map/ppermute | solution.py:21
  10.1 4.4 %collective-permute-done.refs_1_ = bf16[256,256]{1,0:T(8,128)(2,1)S(1)} collective-permute-done((bf16[256,256]{1,0:T(8,128)(2,1)S(1)}, bf16[256,256]{1,0:T(8,128)(2,1)S(1)}, u32[]{:S(2)}, u32[]{:S(2)}) %collective-permute-start) | collective-permute-done | bytes 131104 | tf_op jit(solution)/shard_map/ppermute | solution.py:21
  14.5 3.2 %collective-permute-done.1.refs_2_ = bf16[256,256]{1,0:T(8,128)(2,1)S(1)} collective-permute-done((bf16[256,256]{1,0:T(8,128)(2,1)S(1)}, bf16[256,256]{1,0:T(8,128)(2,1)S(1)}, u32[]{:S(2)}, u32[]{:S(2)}) %collective-permute-start.1) | collective-permute-done | bytes 131104 | tf_op jit(solution)/shard_map/ppermute | solution.py:21
  17.7 1.1 %mix.1 = (bf16[256,256]{1,0:T(8,128)(2,1)S(1)}, bf16[256,256]{1,0:T(8,128)(2,1)S(1)}, bf16[256,256]{1,0:T(8,128)(2,1)S(1)}, bf16[256,256]{1,0:T(8,128)(2,1)S(1)}) custom-call(bf16[256,256]{1,0:T(8,128)(2,1)S(1)} %get-tuple-element.21.refs_0_, bf16[256,256]{1,0:T(8,128)(2,1)S(1)} %collective-permute-done.refs_1_, ...), custom_call_target="tpu_custom_call" | custom-call | tf_op jit(solution)/shard_map/mix/pallas_call | solution.py:116
  18.8 2.3 %collective-permute-start.3 = (bf16[256,256]{1,0:T(8,128)(2,1)S(1)}, bf16[256,256]{1,0:T(8,128)(2,1)S(1)}, u32[]{:S(2)}, u32[]{:S(2)}) collective-permute-start(bf16[256,256]{1,0:T(8,128)(2,1)S(1)} %get-tuple-element.16), channel_id=1, source_target_pairs={{0,12},{4,0},{8,4},{12,8},{1,13},{5,1},{9,5},{13,9},{2,14},{6,2},{... | collective-permute-start | bytes 393224 | tf_op jit(solution)/shard_map/ppermute | solution.py:21
  21.2 0.0 collective-permute-start.4
  21.2 0.6 %collective-permute-start.5 = (bf16[256,256]{1,0:T(8,128)(2,1)S(1)}, bf16[256,256]{1,0:T(8,128)(2,1)S(1)}, u32[]{:S(2)}, u32[]{:S(2)}) collective-permute-start(bf16[256,256]{1,0:T(8,128)(2,1)S(1)} %get-tuple-element.18), channel_id=1, source_target_pairs={{0,4},{4,8},{8,12},{12,0},{1,5},{5,9},{9,13},{13,1},{2,6},{6,10},{... | collective-permute-start | bytes 393224 | tf_op jit(solution)/shard_map/ppermute | solution.py:21
  21.8 3.3 %collective-permute-done.3.refs_1_ = bf16[256,256]{1,0:T(8,128)(2,1)S(1)} collective-permute-done((bf16[256,256]{1,0:T(8,128)(2,1)S(1)}, bf16[256,256]{1,0:T(8,128)(2,1)S(1)}, u32[]{:S(2)}, u32[]{:S(2)}) %collective-permute-start.3) | collective-permute-done | bytes 131104 | tf_op jit(solution)/shard_map/ppermute | solution.py:21
  25.1 6.7 %collective-permute-done.4.refs_2_ = bf16[256,256]{1,0:T(8,128)(2,1)S(1)} collective-permute-done((bf16[256,256]{1,0:T(8,128)(2,1)S(1)}, bf16[256,256]{1,0:T(8,128)(2,1)S(1)}, u32[]{:S(2)}, u32[]{:S(2)}) %collective-permute-start.4) | collective-permute-done | bytes 131104 | tf_op jit(solution)/shard_map/ppermute | solution.py:21
  31.8 0.0 collective-permute-done.5.refs_3_
  31.8 2.0 %gate.1 = bf16[256,1024]{1,0:T(8,128)(2,1)} custom-call(bf16[256,1024]{1,0:T(8,128)(2,1)} %gate_ref.1, bf16[256,256]{1,0:T(8,128)(2,1)S(1)} %get-tuple-element.15.refs_0_, bf16[256,256]{1,0:T(8,128)(2,1)S(1)} %collective-permute-done.3.refs_1_, bf16[256,256]{1,0:T(8,128)(2,1)S(1)} %collective-permute-done.4.refs_2_, ...), custom_call_target="tpu_custom_call" | custom-call | tf_op jit(solution)/shard_map/gate/pallas_call | solution.py:125
Async XLA Ops:
  1.1 9.0 %collective-permute-start.2 = (bf16[256,256]{1,0:T(8,128)(2,1)S(1)}, bf16[256,256]{1,0:T(8,128)(2,1)S(1)}, u32[]{:S(2)}, u32[]{:S(2)}) collective-permute-start(bf16[256,256]{1,0:T(8,128)(2,1)S(1)} %get-tuple-element.19), channel_id=1, source_target_pairs={{0,12},{4,0},{8,4},{12,8},{1,13},{5,1},{9,5},{13,9},{2,14},{6,2},{... | collective-permute-start | bytes 393224 | tf_op jit(solution)/shard_map/ppermute | solution.py:21
  6.2 8.3 %collective-permute-start = (bf16[256,256]{1,0:T(8,128)(2,1)S(1)}, bf16[256,256]{1,0:T(8,128)(2,1)S(1)}, u32[]{:S(2)}, u32[]{:S(2)}) collective-permute-start(bf16[256,256]{1,0:T(8,128)(2,1)S(1)} %get-tuple-element.20), channel_id=1, source_target_pairs={{0,4},{4,8},{8,12},{12,0},{1,5},{5,9},{9,13},{13,1},{2,6},{6,10},{... | collective-permute-start | bytes 393224 | tf_op jit(solution)/shard_map/ppermute | solution.py:21
  6.2 11.5 %collective-permute-start.1 = (bf16[256,256]{1,0:T(8,128)(2,1)S(1)}, bf16[256,256]{1,0:T(8,128)(2,1)S(1)}, u32[]{:S(2)}, u32[]{:S(2)}) collective-permute-start(bf16[256,256]{1,0:T(8,128)(2,1)S(1)} %get-tuple-element.22), channel_id=1, source_target_pairs={{0,8},{4,12},{8,0},{12,4},{1,9},{5,13},{9,1},{13,5},{2,10},{6,14},... | collective-permute-start | bytes 393224 | tf_op jit(solution)/shard_map/ppermute | solution.py:21
  18.8 6.3 %collective-permute-start.3 = (bf16[256,256]{1,0:T(8,128)(2,1)S(1)}, bf16[256,256]{1,0:T(8,128)(2,1)S(1)}, u32[]{:S(2)}, u32[]{:S(2)}) collective-permute-start(bf16[256,256]{1,0:T(8,128)(2,1)S(1)} %get-tuple-element.16), channel_id=1, source_target_pairs={{0,12},{4,0},{8,4},{12,8},{1,13},{5,1},{9,5},{13,9},{2,14},{6,2},{... | collective-permute-start | bytes 393224 | tf_op jit(solution)/shard_map/ppermute | solution.py:21
  21.2 10.7 %collective-permute-start.4 = (bf16[256,256]{1,0:T(8,128)(2,1)S(1)}, bf16[256,256]{1,0:T(8,128)(2,1)S(1)}, u32[]{:S(2)}, u32[]{:S(2)}) collective-permute-start(bf16[256,256]{1,0:T(8,128)(2,1)S(1)} %get-tuple-element.17), channel_id=1, source_target_pairs={{0,8},{4,12},{8,0},{12,4},{1,9},{5,13},{9,1},{13,5},{2,10},{6,14},... | collective-permute-start | bytes 393224 | tf_op jit(solution)/shard_map/ppermute | solution.py:21
  21.2 10.7 %collective-permute-start.5 = (bf16[256,256]{1,0:T(8,128)(2,1)S(1)}, bf16[256,256]{1,0:T(8,128)(2,1)S(1)}, u32[]{:S(2)}, u32[]{:S(2)}) collective-permute-start(bf16[256,256]{1,0:T(8,128)(2,1)S(1)} %get-tuple-element.18), channel_id=1, source_target_pairs={{0,4},{4,8},{8,12},{12,0},{1,5},{5,9},{9,13},{13,1},{2,6},{6,10},{... | collective-permute-start | bytes 393224 | tf_op jit(solution)/shard_map/ppermute | solution.py:21

commit v2 on v1

--- a/solution.py
+++ b/solution.py
@@ -49,7 +49,7 @@
         gains_ref[own, 1:2, :] = jnp.sum(spread.T, axis=0, keepdims=True)
 
 
-def mix_kernel(count, lags, owned, *refs):
+def mix_kernel(count, lags, own, *refs):
     blocks, (fwd_ref, bwd_ref, gains_ref) = refs[:count], refs[count : count + 3]
     outs, (inputs, sums) = refs[count + 3 : 2 * count + 3], refs[2 * count + 3 :]
     me = lax.axis_index("ctx")
@@ -57,38 +57,42 @@
     places = [lax.rem(me - k + count, count) for k in range(count)]
     for k in range(count):
         inputs[places[k]] = blocks[k][...]
-    for own in range(owned):
-        lanes = slice(own * group_w, (own + 1) * group_w)
-        values = jnp.concatenate([inputs[i, :, lanes] for i in range(count)], axis=1).astype(F32)
-        gated = (values * jnp.tile(gains_ref[own, 0:1, :], (1, count))).astype(BF16)
-        flipped = (values * jnp.tile(gains_ref[own, 1:2, :], (1, count))).astype(BF16)
-        ahead = [None] * count
-        behind = [None] * count
-
-        def add(total, at, value):
-            total[at] = value if total[at] is None else total[at] + value
-
-        for lag in range(min(lags, count)):
-            kept = (count - lag) * group_w
-            up = jnp.dot(fwd_ref[own, lag], gated[:, :kept], preferred_element_type=F32)
-            down = jnp.dot(bwd_ref[own, lag], flipped[:, count * group_w - kept :], preferred_element_type=F32)
-            for i in range(count - lag):
-                piece = slice(i * group_w, (i + 1) * group_w)
-                add(ahead, i + lag, up[:, piece])
-                add(behind, i, down[:, piece])
-        for i in range(count):
-            sums[i, :, lanes] = (ahead[i] + behind[i].astype(BF16).astype(F32)).astype(BF16)
+    values = jnp.concatenate([inputs[i] for i in range(count)], axis=1).astype(F32)
+    gated = (values * jnp.tile(gains_ref[own, 0:1, :], (1, count))).astype(BF16)
+    flipped = (values * jnp.tile(gains_ref[own, 1:2, :], (1, count))).astype(BF16)
+    ahead = [None] * count
+    behind = [None] * count
+
+    def add(total, at, value):
+        total[at] = value if total[at] is None else total[at] + value
+
+    for lag in range(min(lags, count)):
+        kept = (count - lag) * group_w
+        up = jnp.dot(fwd_ref[own, lag], gated[:, :kept], preferred_element_type=F32)
+        down = jnp.dot(bwd_ref[own, lag], flipped[:, count * group_w - kept :], preferred_element_type=F32)
+        for i in range(count - lag):
+            piece = slice(i * group_w, (i + 1) * group_w)
+            add(ahead, i + lag, up[:, piece])
+            add(behind, i, down[:, piece])
+    for i in range(count):
+        sums[i] = (ahead[i] + behind[i].astype(BF16).astype(F32)).astype(BF16)
     for k in range(count):
         outs[k][...] = sums[places[k]]
 
 
-def gate_kernel(count, gate_ref, *refs):
-    blocks, out_ref = refs[:count], refs[count]
+def gate_kernel(count, owned, own, gate_ref, *refs):
+    blocks, out_ref, (pieces, sems) = refs[:count], refs[-3], refs[-2:]
     me = lax.axis_index("ctx")
-    width = blocks[0].shape[1]
+    group_w = blocks[0].shape[1]
+    copies = []
     for k in range(count):
-        place = pl.ds(pl.multiple_of(lax.rem(me + k, count) * width, width), width)
-        out_ref[:, place] = (gate_ref[:, place].astype(F32) * blocks[k][...].astype(F32)).astype(BF16)
+        at = (lax.rem(me + k, count) * owned + own) * group_w
+        place = pl.ds(pl.multiple_of(at, group_w), group_w)
+        pieces[k] = (gate_ref[:, place].astype(F32) * blocks[k][...].astype(F32)).astype(BF16)
+        copies.append(pltpu.make_async_copy(pieces.at[k], out_ref.at[:, place], sems.at[k]))
+        copies[k].start()
+    for copy in copies:
+        copy.wait()
 
 
 def dealt(sequence, gate, filters, lengths, gain, permutation):
@@ -98,37 +102,50 @@
     group_w = permutation.shape[0]
     owned = groups_dev // count
     lags = taps // rows + 1
-    chunk = owned * group_w
     me = lax.axis_index("ctx")
-    vmem = pl.BlockSpec(memory_space=VMEM)
-
-    def part(k):
-        return lax.dynamic_slice(sequence, (0, lax.rem(me + k, count) * chunk), (rows, chunk))
-
-    blocks = [part(0)] + [rotated(part(k), k) for k in range(1, count)]
-    fwd, bwd, gains = pl.pallas_call(
+    vmem, anywhere = pl.BlockSpec(memory_space=VMEM), pl.BlockSpec(memory_space=pl.ANY)
+
+    def part(k, own):
+        group = lax.rem(me + k, count) * owned + own
+        return lax.dynamic_slice(sequence, (0, group * group_w), (rows, group_w))
+
+    def deal(own):
+        return [part(0, own)] + [rotated(part(k, own), k) for k in range(1, count)]
+
+    blocks = [deal(own) for own in range(owned)]
+    toeplitz = pl.pallas_call(
         functools.partial(build_kernel, rows, lags, owned),
         in_specs=[vmem, pl.BlockSpec(memory_space=SMEM), vmem, vmem],
         out_specs=[vmem] * 3,
         out_shape=[VMEM((owned, lags, rows, rows), BF16)] * 2 + [VMEM((owned, 8, group_w), F32)],
         name="build",
     )(filters, lengths, gain.reshape(groups_dev, group_w), permutation.reshape(1, group_w))
-    outs = pl.pallas_call(
-        functools.partial(mix_kernel, count, lags, owned),
-        in_specs=[vmem] * (count + 3),
-        out_specs=[vmem] * count,
-        out_shape=[VMEM((rows, chunk), BF16)] * count,
-        scratch_shapes=[VMEM((count, rows, chunk), BF16)] * 2,
-        name="mix",
-    )(*map(held, [*blocks, fwd, bwd, gains]))
-    back = [outs[0]] + [rotated(outs[k], -k) for k in range(1, count)]
-    return pl.pallas_call(
-        functools.partial(gate_kernel, count),
-        in_specs=[vmem] * (count + 1),
-        out_specs=vmem,
-        out_shape=jax.ShapeDtypeStruct((rows, width), BF16),
-        name="gate",
-    )(gate, *map(held, back))
+    back = []
+    for own in range(owned):
+        outs = pl.pallas_call(
+            functools.partial(mix_kernel, count, lags, own),
+            in_specs=[vmem] * (count + 3),
+            out_specs=[vmem] * count,
+            out_shape=[VMEM((rows, group_w), BF16)] * count,
+            scratch_shapes=[VMEM((count, rows, group_w), BF16)] * 2,
+            name=f"mix{own}",
+        )(*map(held, [*blocks[own], *toeplitz]))
+        back.append([outs[0]] + [rotated(outs[k], -k) for k in range(1, count)])
+    gate = held(gate)
+    out = []
+    for own in range(owned):
+        out = [
+            pl.pallas_call(
+                functools.partial(gate_kernel, count, owned, own),
+                in_specs=[vmem] * (count + 1) + [anywhere] * len(out),
+                out_specs=anywhere,
+                out_shape=jax.ShapeDtypeStruct((rows, width), BF16),
+                scratch_shapes=[VMEM((count, rows, group_w), BF16), pltpu.SemaphoreType.DMA((count,))],
+                input_output_aliases={count + 1: 0} if out else {},
+                name=f"gate{own}",
+            )(gate, *map(held, back[own]), *out)
+        ]
+    return out[0]
 
 
 def build_blocks(kernel, rows):

time: 34.1 us -> 33.6 us (0.985)
  waiting for transfers between devices: 19.3 us -> 6.88 us
  starting transfers between devices: 9.06 us -> 19.9 us
  Pallas kernels: 4.33 us -> 5.39 us
    ppermute x6 -> x12, waiting for transfers between devices: 19.3 us -> 6.88 us  [rotated(): lax.ppermute(array, 'ctx', [(i, (i + by) % count) for i in range(count)])]
    ppermute x6 -> x12, starting transfers between devices: 9.06 us -> 19.9 us  [rotated(): lax.ppermute(array, 'ctx', [(i, (i + by) % count) for i in range(count)])]
    pallas_call x2 -> x4, Pallas kernels: 3.11 us -> 4.17 us  [the longest x2 2.64 us: dealt(): pl.pallas_call(functools.partial(mix_kernel, count, lags, own), in_specs=...]
  transfers between devices with their start and end apart: 6 -> 12, of which waited for: 5 -> 4; matrix products, arithmetic and copies ran while one was open for 0% -> 0% of each run, Pallas kernels for 4% -> 14%
where the time goes in v2:
time: 33.6 us; the launch traced here: 33.4 us
  starting transfers between devices  19.9 us (59%)
  waiting for transfers between devices  6.88 us (20%)
  Pallas kernels  5.39 us (16%)
  local copies, waits for them, and re-layouts  1.11 us (3%)
    ppermute x12, starting transfers between devices, rotated(): lax.ppermute(array, 'ctx', [(i, (i + by) % count) for i in range(count)])  19.9 us
    ppermute x12, waiting for transfers between devices, rotated(): lax.ppermute(array, 'ctx', [(i, (i + by) % count) for i in range(count)])  6.88 us
    pallas_call x2, Pallas kernels, dealt(): pl.pallas_call(functools.partial(mix_kernel, count, lags, own), in_specs=...  2.64 us
    pallas_call x2, Pallas kernels, dealt(): pl.pallas_call(functools.partial(gate_kernel, count, owned, own), in_spec...  1.53 us
    pallas_call x1, Pallas kernels, dealt(): pl.pallas_call(functools.partial(build_kernel, rows, lags, owned), in_spe...  1.22 us
    dynamic_slice x1, local copies, waits for them, and re-layouts, part(): return lax.dynamic_slice(sequence, (0, group * group_w), (rows, group_w))  1.11 us
  transfers between devices with their start and end apart: 12, of which 4 were waited for; matrix products, arithmetic and copies ran while one was open for 0% of the time, Pallas kernels for 14%

profile of v2, /device:TPU:0, one launch (start us, length us, event | category | flops | bytes accessed | tf_op | source)
XLA Modules:
  0.0 33.4 jit_solution(16816474517620886502)
XLA Ops:
  0.0 1.1 %constant_dynamic-slice_fusion = (bf16[256,128]{1,0:T(8,128)(2,1)S(1)}, bf16[256,128]{1,0:T(8,128)(2,1)S(1)}, bf16[256,128]{1,0:T(8,128)(2,1)S(1)}, bf16[256,128...) fusion(bf16[256,1024]{1,0:T(8,128)(2,1)} %param.6, ...), kind=kLoop, calls=%fused_computation | loop fusion | bytes 1048608 | tf_op jit(solution)/shard_map/dynamic_slice | solution.py:110
  1.1 5.1 %collective-permute-start.8 = (bf16[256,128]{1,0:T(8,128)(2,1)S(1)}, bf16[256,128]{1,0:T(8,128)(2,1)S(1)}, u32[]{:S(2)}, u32[]{:S(2)}) collective-permute-start(bf16[256,128]{1,0:T(8,128)(2,1)S(1)} %get-tuple-element.27), channel_id=1, source_target_pairs={{0,12},{4,0},{8,4},{12,8},{1,13},{5,1},{9,5},{13,9},{2,14},{6,2},{... | collective-permute-start | bytes 196616 | tf_op jit(solution)/shard_map/ppermute | solution.py:21
  6.2 0.0 collective-permute-start.6
  6.2 1.0 %collective-permute-start.7 = (bf16[256,128]{1,0:T(8,128)(2,1)S(1)}, bf16[256,128]{1,0:T(8,128)(2,1)S(1)}, u32[]{:S(2)}, u32[]{:S(2)}) collective-permute-start(bf16[256,128]{1,0:T(8,128)(2,1)S(1)} %get-tuple-element.34), channel_id=1, source_target_pairs={{0,8},{4,12},{8,0},{12,4},{1,9},{5,13},{9,1},{13,5},{2,10},{6,14},... | collective-permute-start | bytes 196616 | tf_op jit(solution)/shard_map/ppermute | solution.py:21
  7.2 2.8 %collective-permute-start.2 = (bf16[256,128]{1,0:T(8,128)(2,1)S(1)}, bf16[256,128]{1,0:T(8,128)(2,1)S(1)}, u32[]{:S(2)}, u32[]{:S(2)}) collective-permute-start(bf16[256,128]{1,0:T(8,128)(2,1)S(1)} %get-tuple-element.30), channel_id=1, source_target_pairs={{0,12},{4,0},{8,4},{12,8},{1,13},{5,1},{9,5},{13,9},{2,14},{6,2},{... | collective-permute-start | bytes 196616 | tf_op jit(solution)/shard_map/ppermute | solution.py:21
  10.0 2.0 %collective-permute-start.1 = (bf16[256,128]{1,0:T(8,128)(2,1)S(1)}, bf16[256,128]{1,0:T(8,128)(2,1)S(1)}, u32[]{:S(2)}, u32[]{:S(2)}) collective-permute-start(bf16[256,128]{1,0:T(8,128)(2,1)S(1)} %get-tuple-element.31), channel_id=1, source_target_pairs={{0,8},{4,12},{8,0},{12,4},{1,9},{5,13},{9,1},{13,5},{2,10},{6,14},... | collective-permute-start | bytes 196616 | tf_op jit(solution)/shard_map/ppermute | solution.py:21
  12.1 1.2 %build.1 = (bf16[2,4,256,256]{3,2,1,0:T(8,128)(2,1)S(1)}, bf16[2,4,256,256]{3,2,1,0:T(8,128)(2,1)S(1)}, f32[2,8,128]{2,1,0:T(8,128)S(1)}) custom-call(f32[8,768]{1,0:T(8,128)} %filters_ref.1, s32[8]{0:T(128)} %lengths_ref.1, f32[8,128]{1,0:T(8,128)} %bitcast.2, s32[1,128]{1,0:T(1,128)} %bitcast.3), custom_call_target="tpu_custom_call" | custom-call | tf_op jit(solution)/shard_map/build/pallas_call | solution.py:116
  13.3 0.0 collective-permute-done.8.refs_3_
  13.3 0.1 collective-permute-start
  13.4 0.0 collective-permute-done.6.refs_1_
  13.4 1.6 %collective-permute-done.7.refs_2_ = bf16[256,128]{1,0:T(8,128)(2,1)S(1)} collective-permute-done((bf16[256,128]{1,0:T(8,128)(2,1)S(1)}, bf16[256,128]{1,0:T(8,128)(2,1)S(1)}, u32[]{:S(2)}, u32[]{:S(2)}) %collective-permute-start.7) | collective-permute-done | bytes 65568 | tf_op jit(solution)/shard_map/ppermute | solution.py:21
  15.0 1.3 %mix0.1 = (bf16[256,128]{1,0:T(8,128)(2,1)S(1)}, bf16[256,128]{1,0:T(8,128)(2,1)}, bf16[256,128]{1,0:T(8,128)(2,1)}, bf16[256,128]{1,0:T(8,128)(2,1)S(1)}) custom-call(bf16[256,128]{1,0:T(8,128)(2,1)S(1)} %get-tuple-element.29.refs_0_, bf16[256,128]{1,0:T(8,128)(2,1)S(1)} %collective-permute-done.6.refs_1_, ...), custom_call_target="tpu_custom_call" | custom-call | tf_op jit(solution)/shard_map/mix0/pallas_call | solution.py:125
  16.3 4.0 %collective-permute-start.9 = (bf16[256,128]{1,0:T(8,128)(2,1)}, bf16[256,128]{1,0:T(8,128)(2,1)S(1)}, u32[]{:S(2)}, u32[]{:S(2)}) collective-permute-start(bf16[256,128]{1,0:T(8,128)(2,1)} %get-tuple-element.24), channel_id=1, source_target_pairs={{0,12},{4,0},{8,4},{12,8},{1,13},{5,1},{9,5},{13,9},{2,14},{6,2},{... | collective-permute-start | bytes 196616 | tf_op jit(solution)/shard_map/ppermute | solution.py:21
  20.3 0.0 collective-permute-start.10
  20.3 0.0 collective-permute-done.2.refs_3_
  20.3 0.6 %collective-permute-start.11 = (bf16[256,128]{1,0:T(8,128)(2,1)S(1)}, bf16[256,128]{1,0:T(8,128)(2,1)S(1)}, u32[]{:S(2)}, u32[]{:S(2)}) collective-permute-start(bf16[256,128]{1,0:T(8,128)(2,1)S(1)} %get-tuple-element.26), channel_id=1, source_target_pairs={{0,4},{4,8},{8,12},{12,0},{1,5},{5,9},{9,13},{13,1},{2,6},{6,10},{... | collective-permute-start | bytes 196616 | tf_op jit(solution)/shard_map/ppermute | solution.py:21
  20.8 0.0 collective-permute-done.1.refs_2_
  20.9 0.0 collective-permute-done.refs_1_
  20.9 0.0 copy-start
  20.9 1.3 %mix1.1 = (bf16[256,128]{1,0:T(8,128)(2,1)S(1)}, bf16[256,128]{1,0:T(8,128)(2,1)}, bf16[256,128]{1,0:T(8,128)(2,1)S(1)}, bf16[256,128]{1,0:T(8,128)(2,1)S(1)}) custom-call(bf16[256,128]{1,0:T(8,128)(2,1)S(1)} %get-tuple-element.33.refs_0_, bf16[256,128]{1,0:T(8,128)(2,1)S(1)} %collective-permute-done.refs_1_, ...), custom_call_target="tpu_custom_call" | custom-call | tf_op jit(solution)/shard_map/mix1/pallas_call | solution.py:125
  22.2 3.2 %collective-permute-start.3 = (bf16[256,128]{1,0:T(8,128)(2,1)}, bf16[256,128]{1,0:T(8,128)(2,1)S(1)}, u32[]{:S(2)}, u32[]{:S(2)}) collective-permute-start(bf16[256,128]{1,0:T(8,128)(2,1)} %get-tuple-element.20), channel_id=1, source_target_pairs={{0,12},{4,0},{8,4},{12,8},{1,13},{5,1},{9,5},{13,9},{2,14},{6,2},{... | collective-permute-start | bytes 196616 | tf_op jit(solution)/shard_map/ppermute | solution.py:21
  25.4 1.1 %collective-permute-start.4 = (bf16[256,128]{1,0:T(8,128)(2,1)S(1)}, bf16[256,128]{1,0:T(8,128)(2,1)S(1)}, u32[]{:S(2)}, u32[]{:S(2)}) collective-permute-start(bf16[256,128]{1,0:T(8,128)(2,1)S(1)} %get-tuple-element.21), channel_id=1, source_target_pairs={{0,8},{4,12},{8,0},{12,4},{1,9},{5,13},{9,1},{13,5},{2,10},{6,14},... | collective-permute-start | bytes 196616 | tf_op jit(solution)/shard_map/ppermute | solution.py:21
  26.5 0.0 collective-permute-done.9.refs_1_
  26.6 0.0 collective-permute-start.5
  26.6 1.3 %collective-permute-done.10.refs_2_ = bf16[256,128]{1,0:T(8,128)(2,1)S(1)} collective-permute-done((bf16[256,128]{1,0:T(8,128)(2,1)}, bf16[256,128]{1,0:T(8,128)(2,1)S(1)}, u32[]{:S(2)}, u32[]{:S(2)}) %collective-permute-start.10) | collective-permute-done | bytes 65568 | tf_op jit(solution)/shard_map/ppermute | solution.py:21
  27.9 0.0 collective-permute-done.11.refs_3_
  27.9 0.0 copy-done
  27.9 0.8 %gate0.1.refs_4_ = bf16[256,1024]{1,0:T(8,128)(2,1)} custom-call(bf16[256,1024]{1,0:T(8,128)(2,1)S(1)} %copy-done, bf16[256,128]{1,0:T(8,128)(2,1)S(1)} %get-tuple-element.23.refs_0_, bf16[256,128]{1,0:T(8,128)(2,1)S(1)} %collective-permute-done.9.refs_1_, bf16[256,128]{1,0:T(8,128)(2,1)S(1)} %collective-permute-done.10.refs_2_, ...), custom_call_target="tpu_custom_call" | custom-call | tf_op jit(solution)/shard_map/gate0/pallas_call | solution.py:138
  28.6 0.0 collective-permute-done.3.refs_1_
  28.7 1.9 %collective-permute-done.4.refs_2_ = bf16[256,128]{1,0:T(8,128)(2,1)S(1)} collective-permute-done((bf16[256,128]{1,0:T(8,128)(2,1)S(1)}, bf16[256,128]{1,0:T(8,128)(2,1)S(1)}, u32[]{:S(2)}, u32[]{:S(2)}) %collective-permute-start.4) | collective-permute-done | bytes 65568 | tf_op jit(solution)/shard_map/ppermute | solution.py:21
  30.6 2.0 %collective-permute-done.5.refs_3_ = bf16[256,128]{1,0:T(8,128)(2,1)S(1)} collective-permute-done((bf16[256,128]{1,0:T(8,128)(2,1)S(1)}, bf16[256,128]{1,0:T(8,128)(2,1)S(1)}, u32[]{:S(2)}, u32[]{:S(2)}) %collective-permute-start.5) | collective-permute-done | bytes 65568 | tf_op jit(solution)/shard_map/ppermute | solution.py:21
  32.6 0.8 %gate1.1 = bf16[256,1024]{1,0:T(8,128)(2,1)} custom-call(bf16[256,1024]{1,0:T(8,128)(2,1)S(1)} %copy-done, bf16[256,128]{1,0:T(8,128)(2,1)S(1)} %get-tuple-element.19.refs_0_, bf16[256,128]{1,0:T(8,128)(2,1)S(1)} %collective-permute-done.3.refs_1_, bf16[256,128]{1,0:T(8,128)(2,1)S(1)} %collective-permute-done.4.refs_2_, ...), custom_call_target="tpu_custom_call", output_to_operand_aliasing={{}: (5, {})} | custom-call | tf_op jit(solution)/shard_map/gate1/pallas_call | solution.py:138
Async XLA Ops:
  1.1 12.2 %collective-permute-start.8 = (bf16[256,128]{1,0:T(8,128)(2,1)S(1)}, bf16[256,128]{1,0:T(8,128)(2,1)S(1)}, u32[]{:S(2)}, u32[]{:S(2)}) collective-permute-start(bf16[256,128]{1,0:T(8,128)(2,1)S(1)} %get-tuple-element.27), channel_id=1, source_target_pairs={{0,12},{4,0},{8,4},{12,8},{1,13},{5,1},{9,5},{13,9},{2,14},{6,2},{... | collective-permute-start | bytes 196616 | tf_op jit(solution)/shard_map/ppermute | solution.py:21
  6.2 7.2 %collective-permute-start.6 = (bf16[256,128]{1,0:T(8,128)(2,1)S(1)}, bf16[256,128]{1,0:T(8,128)(2,1)S(1)}, u32[]{:S(2)}, u32[]{:S(2)}) collective-permute-start(bf16[256,128]{1,0:T(8,128)(2,1)S(1)} %get-tuple-element.28), channel_id=1, source_target_pairs={{0,4},{4,8},{8,12},{12,0},{1,5},{5,9},{9,13},{13,1},{2,6},{6,10},{... | collective-permute-start | bytes 196616 | tf_op jit(solution)/shard_map/ppermute | solution.py:21
  6.2 8.8 %collective-permute-start.7 = (bf16[256,128]{1,0:T(8,128)(2,1)S(1)}, bf16[256,128]{1,0:T(8,128)(2,1)S(1)}, u32[]{:S(2)}, u32[]{:S(2)}) collective-permute-start(bf16[256,128]{1,0:T(8,128)(2,1)S(1)} %get-tuple-element.34), channel_id=1, source_target_pairs={{0,8},{4,12},{8,0},{12,4},{1,9},{5,13},{9,1},{13,5},{2,10},{6,14},... | collective-permute-start | bytes 196616 | tf_op jit(solution)/shard_map/ppermute | solution.py:21
  7.2 13.1 %collective-permute-start.2 = (bf16[256,128]{1,0:T(8,128)(2,1)S(1)}, bf16[256,128]{1,0:T(8,128)(2,1)S(1)}, u32[]{:S(2)}, u32[]{:S(2)}) collective-permute-start(bf16[256,128]{1,0:T(8,128)(2,1)S(1)} %get-tuple-element.30), channel_id=1, source_target_pairs={{0,12},{4,0},{8,4},{12,8},{1,13},{5,1},{9,5},{13,9},{2,14},{6,2},{... | collective-permute-start | bytes 196616 | tf_op jit(solution)/shard_map/ppermute | solution.py:21
  10.0 10.8 %collective-permute-start.1 = (bf16[256,128]{1,0:T(8,128)(2,1)S(1)}, bf16[256,128]{1,0:T(8,128)(2,1)S(1)}, u32[]{:S(2)}, u32[]{:S(2)}) collective-permute-start(bf16[256,128]{1,0:T(8,128)(2,1)S(1)} %get-tuple-element.31), channel_id=1, source_target_pairs={{0,8},{4,12},{8,0},{12,4},{1,9},{5,13},{9,1},{13,5},{2,10},{6,14},... | collective-permute-start | bytes 196616 | tf_op jit(solution)/shard_map/ppermute | solution.py:21
  13.3 7.5 %collective-permute-start = (bf16[256,128]{1,0:T(8,128)(2,1)S(1)}, bf16[256,128]{1,0:T(8,128)(2,1)S(1)}, u32[]{:S(2)}, u32[]{:S(2)}) collective-permute-start(bf16[256,128]{1,0:T(8,128)(2,1)S(1)} %get-tuple-element.32), channel_id=1, source_target_pairs={{0,4},{4,8},{8,12},{12,0},{1,5},{5,9},{9,13},{13,1},{2,6},{6,10},{... | collective-permute-start | bytes 196616 | tf_op jit(solution)/shard_map/ppermute | solution.py:21
  16.3 10.2 %collective-permute-start.9 = (bf16[256,128]{1,0:T(8,128)(2,1)}, bf16[256,128]{1,0:T(8,128)(2,1)S(1)}, u32[]{:S(2)}, u32[]{:S(2)}) collective-permute-start(bf16[256,128]{1,0:T(8,128)(2,1)} %get-tuple-element.24), channel_id=1, source_target_pairs={{0,12},{4,0},{8,4},{12,8},{1,13},{5,1},{9,5},{13,9},{2,14},{6,2},{... | collective-permute-start | bytes 196616 | tf_op jit(solution)/shard_map/ppermute | solution.py:21
  20.3 7.6 %collective-permute-start.10 = (bf16[256,128]{1,0:T(8,128)(2,1)}, bf16[256,128]{1,0:T(8,128)(2,1)S(1)}, u32[]{:S(2)}, u32[]{:S(2)}) collective-permute-start(bf16[256,128]{1,0:T(8,128)(2,1)} %get-tuple-element.25), channel_id=1, source_target_pairs={{0,8},{4,12},{8,0},{12,4},{1,9},{5,13},{9,1},{13,5},{2,10},{6,14},... | collective-permute-start | bytes 196616 | tf_op jit(solution)/shard_map/ppermute | solution.py:21
  20.3 7.6 %collective-permute-start.11 = (bf16[256,128]{1,0:T(8,128)(2,1)S(1)}, bf16[256,128]{1,0:T(8,128)(2,1)S(1)}, u32[]{:S(2)}, u32[]{:S(2)}) collective-permute-start(bf16[256,128]{1,0:T(8,128)(2,1)S(1)} %get-tuple-element.26), channel_id=1, source_target_pairs={{0,4},{4,8},{8,12},{12,0},{1,5},{5,9},{9,13},{13,1},{2,6},{6,10},{... | collective-permute-start | bytes 196616 | tf_op jit(solution)/shard_map/ppermute | solution.py:21
  20.9 7.0 %copy-start = (bf16[256,1024]{1,0:T(8,128)(2,1)S(1)}, bf16[256,1024]{1,0:T(8,128)(2,1)}, u32[]{:S(2)}) copy-start(bf16[256,1024]{1,0:T(8,128)(2,1)} %gate_ref.3) | copy-start | bytes 1572868
  22.2 6.5 %collective-permute-start.3 = (bf16[256,128]{1,0:T(8,128)(2,1)}, bf16[256,128]{1,0:T(8,128)(2,1)S(1)}, u32[]{:S(2)}, u32[]{:S(2)}) collective-permute-start(bf16[256,128]{1,0:T(8,128)(2,1)} %get-tuple-element.20), channel_id=1, source_target_pairs={{0,12},{4,0},{8,4},{12,8},{1,13},{5,1},{9,5},{13,9},{2,14},{6,2},{... | collective-permute-start | bytes 196616 | tf_op jit(solution)/shard_map/ppermute | solution.py:21
  25.4 5.2 %collective-permute-start.4 = (bf16[256,128]{1,0:T(8,128)(2,1)S(1)}, bf16[256,128]{1,0:T(8,128)(2,1)S(1)}, u32[]{:S(2)}, u32[]{:S(2)}) collective-permute-start(bf16[256,128]{1,0:T(8,128)(2,1)S(1)} %get-tuple-element.21), channel_id=1, source_target_pairs={{0,8},{4,12},{8,0},{12,4},{1,9},{5,13},{9,1},{13,5},{2,10},{6,14},... | collective-permute-start | bytes 196616 | tf_op jit(solution)/shard_map/ppermute | solution.py:21
  26.6 6.1 %collective-permute-start.5 = (bf16[256,128]{1,0:T(8,128)(2,1)S(1)}, bf16[256,128]{1,0:T(8,128)(2,1)S(1)}, u32[]{:S(2)}, u32[]{:S(2)}) collective-permute-start(bf16[256,128]{1,0:T(8,128)(2,1)S(1)} %get-tuple-element.22), channel_id=1, source_target_pairs={{0,4},{4,8},{8,12},{12,0},{1,5},{5,9},{9,13},{13,1},{2,6},{6,10},{... | collective-permute-start | bytes 196616 | tf_op jit(solution)/shard_map/ppermute | solution.py:21

commit v3 on v1

--- a/solution.py
+++ b/solution.py
@@ -49,16 +49,30 @@
         gains_ref[own, 1:2, :] = jnp.sum(spread.T, axis=0, keepdims=True)
 
 
-def mix_kernel(count, lags, owned, *refs):
-    blocks, (fwd_ref, bwd_ref, gains_ref) = refs[:count], refs[count : count + 3]
+def deal_kernel(count, chunks, group_w, owned, x_ref, *refs):
+    outs, sems = refs[:-1], refs[-1]
+    me = lax.axis_index("ctx")
+    copies = []
+    for c, chunk in enumerate(chunks):
+        for k in range(count):
+            at = (lax.rem(me + k, count) * owned + chunk[0]) * group_w
+            place = pl.ds(pl.multiple_of(at, group_w), len(chunk) * group_w)
+            copies.append(pltpu.make_async_copy(x_ref.at[:, place], outs[c * count + k], sems.at[c * count + k]))
+            copies[-1].start()
+    for copy in copies:
+        copy.wait()
+
+
+def mix_kernel(count, lags, chunk, order, *refs):
+    blocks, (fwd_ref, bwd_ref, gains_ref) = dict(zip(order, refs[:count])), refs[count : count + 3]
     outs, (inputs, sums) = refs[count + 3 : 2 * count + 3], refs[2 * count + 3 :]
     me = lax.axis_index("ctx")
     group_w = gains_ref.shape[2]
     places = [lax.rem(me - k + count, count) for k in range(count)]
     for k in range(count):
         inputs[places[k]] = blocks[k][...]
-    for own in range(owned):
-        lanes = slice(own * group_w, (own + 1) * group_w)
+    for j, own in enumerate(chunk):
+        lanes = slice(j * group_w, (j + 1) * group_w)
         values = jnp.concatenate([inputs[i, :, lanes] for i in range(count)], axis=1).astype(F32)
         gated = (values * jnp.tile(gains_ref[own, 0:1, :], (1, count))).astype(BF16)
         flipped = (values * jnp.tile(gains_ref[own, 1:2, :], (1, count))).astype(BF16)
@@ -82,13 +96,18 @@
         outs[k][...] = sums[places[k]]
 
 
-def gate_kernel(count, gate_ref, *refs):
-    blocks, out_ref = refs[:count], refs[count]
+def gate_kernel(count, owned, chunk, order, group_w, gate_ref, *refs):
+    blocks, out_ref, (pieces, sems) = dict(zip(order, refs[:count])), refs[-3], refs[-2:]
     me = lax.axis_index("ctx")
-    width = blocks[0].shape[1]
+    copies = []
     for k in range(count):
-        place = pl.ds(pl.multiple_of(lax.rem(me + k, count) * width, width), width)
-        out_ref[:, place] = (gate_ref[:, place].astype(F32) * blocks[k][...].astype(F32)).astype(BF16)
+        at = (lax.rem(me + k, count) * owned + chunk[0]) * group_w
+        place = pl.ds(pl.multiple_of(at, group_w), len(chunk) * group_w)
+        pieces[k] = (gate_ref[:, place].astype(F32) * blocks[k][...].astype(F32)).astype(BF16)
+        copies.append(pltpu.make_async_copy(pieces.at[k], out_ref.at[:, place], sems.at[k]))
+        copies[k].start()
+    for copy in copies:
+        copy.wait()
 
 
 def dealt(sequence, gate, filters, lengths, gain, permutation):
@@ -98,37 +117,62 @@
     group_w = permutation.shape[0]
     owned = groups_dev // count
     lags = taps // rows + 1
-    chunk = owned * group_w
-    me = lax.axis_index("ctx")
-    vmem = pl.BlockSpec(memory_space=VMEM)
-
-    def part(k):
-        return lax.dynamic_slice(sequence, (0, lax.rem(me + k, count) * chunk), (rows, chunk))
-
-    blocks = [part(0)] + [rotated(part(k), k) for k in range(1, count)]
-    fwd, bwd, gains = pl.pallas_call(
+    vmem, anywhere = pl.BlockSpec(memory_space=VMEM), pl.BlockSpec(memory_space=pl.ANY)
+    params = pltpu.CompilerParams(vmem_limit_bytes=24 << 20)
+    chunks = [(own,) for own in range(owned)]
+    order = (0, 1, 2, 3)
+
+    dealt_out = pl.pallas_call(
+        functools.partial(deal_kernel, count, chunks, group_w, owned),
+        in_specs=[anywhere],
+        out_specs=[vmem] * (count * len(chunks)),
+        out_shape=[VMEM((rows, len(chunk) * group_w), BF16) for chunk in chunks for _ in range(count)],
+        scratch_shapes=[pltpu.SemaphoreType.DMA((count * len(chunks),))],
+        compiler_params=params,
+        name="deal",
+    )(sequence)
+    blocks = [
+        [part if k == 0 else rotated(part, k) for k, part in enumerate(dealt_out[c * count : (c + 1) * count])]
+        for c in range(len(chunks))
+    ]
+    toeplitz = pl.pallas_call(
         functools.partial(build_kernel, rows, lags, owned),
         in_specs=[vmem, pl.BlockSpec(memory_space=SMEM), vmem, vmem],
         out_specs=[vmem] * 3,
         out_shape=[VMEM((owned, lags, rows, rows), BF16)] * 2 + [VMEM((owned, 8, group_w), F32)],
+        compiler_params=params,
         name="build",
     )(filters, lengths, gain.reshape(groups_dev, group_w), permutation.reshape(1, group_w))
-    outs = pl.pallas_call(
-        functools.partial(mix_kernel, count, lags, owned),
-        in_specs=[vmem] * (count + 3),
-        out_specs=[vmem] * count,
-        out_shape=[VMEM((rows, chunk), BF16)] * count,
-        scratch_shapes=[VMEM((count, rows, chunk), BF16)] * 2,
-        name="mix",
-    )(*map(held, [*blocks, fwd, bwd, gains]))
-    back = [outs[0]] + [rotated(outs[k], -k) for k in range(1, count)]
-    return pl.pallas_call(
-        functools.partial(gate_kernel, count),
-        in_specs=[vmem] * (count + 1),
-        out_specs=vmem,
-        out_shape=jax.ShapeDtypeStruct((rows, width), BF16),
-        name="gate",
-    )(gate, *map(held, back))
+    back = []
+    for c, chunk in enumerate(chunks):
+        chunk_w = len(chunk) * group_w
+        outs = pl.pallas_call(
+            functools.partial(mix_kernel, count, lags, chunk, order),
+            in_specs=[vmem] * (count + 3),
+            out_specs=[vmem] * count,
+            out_shape=[VMEM((rows, chunk_w), BF16)] * count,
+            scratch_shapes=[VMEM((count, rows, chunk_w), BF16)] * 2,
+            compiler_params=params,
+            name=f"mix{c}",
+        )(*map(held, [*[blocks[c][k] for k in order], *toeplitz]))
+        back.append([outs[0]] + [rotated(outs[k], -k) for k in range(1, count)])
+    gate = held(gate)
+    order = (0, 3, 2, 1)
+    out = []
+    for c, chunk in enumerate(chunks):
+        out = [
+            pl.pallas_call(
+                functools.partial(gate_kernel, count, owned, chunk, order, group_w),
+                in_specs=[vmem] * (count + 1) + [anywhere] * len(out),
+                out_specs=anywhere,
+                out_shape=jax.ShapeDtypeStruct((rows, width), BF16),
+                scratch_shapes=[VMEM((count, rows, len(chunk) * group_w), BF16), pltpu.SemaphoreType.DMA((count,))],
+                input_output_aliases={count + 1: 0} if out else {},
+                compiler_params=params,
+                name=f"gate{c}",
+            )(gate, *map(held, [back[c][k] for k in order]), *out)
+        ]
+    return out[0]
 
 
 def build_blocks(kernel, rows):

time: 34.1 us -> 29.7 us (0.87)
  waiting for transfers between devices: 19.3 us -> 3.87 us
  starting transfers between devices: 9.06 us -> 19.8 us
  local copies, waits for them, and re-layouts: 1.13 us -> 1.71 us
    ppermute x6 -> x12, waiting for transfers between devices: 19.3 us -> 3.87 us  [rotated(): lax.ppermute(array, 'ctx', [(i, (i + by) % count) for i in range(count)])]
    ppermute x6 -> x12, starting transfers between devices: 9.06 us -> 19.8 us  [rotated(): lax.ppermute(array, 'ctx', [(i, (i + by) % count) for i in range(count)])]
    unnamed x0 -> x12, local copies, waits for them, and re-layouts: none -> 1.71 us
    dynamic_slice x1 -> x0, local copies, waits for them, and re-layouts: 1.13 us -> none  [part(): lax.dynamic_slice(sequence, (0, lax.rem(me + k, count) * chunk), (rows, c...]
    pallas_call x2 -> x5, Pallas kernels: 3.11 us -> 3.17 us  [the longest x2 1.53 us: dealt(): pl.pallas_call(functools.partial(gate_kernel, count, owned, chunk, order,...]
  transfers between devices with their start and end apart: 6 -> 12, of which waited for: 5 -> 3; matrix products, arithmetic and copies ran while one was open for 0% -> 0% of each run, Pallas kernels for 4% -> 11%
where the time goes in v3:
time: 29.7 us; the launch traced here: 29.5 us
  starting transfers between devices  19.8 us (67%)
  Pallas kernels  4.13 us (14%)
  waiting for transfers between devices  3.87 us (13%)
  local copies, waits for them, and re-layouts  1.71 us (6%)
    ppermute x12, starting transfers between devices, rotated(): lax.ppermute(array, 'ctx', [(i, (i + by) % count) for i in range(count)])  19.8 us
    ppermute x12, waiting for transfers between devices, rotated(): lax.ppermute(array, 'ctx', [(i, (i + by) % count) for i in range(count)])  3.87 us
    unnamed x12, local copies, waits for them, and re-layouts  1.71 us
    pallas_call x2, Pallas kernels, dealt(): pl.pallas_call(functools.partial(gate_kernel, count, owned, chunk, order,...  1.53 us
    pallas_call x2, Pallas kernels, dealt(): pl.pallas_call(functools.partial(mix_kernel, count, lags, chunk, order),...  1.4 us
    pallas_call x1, Pallas kernels, dealt(): pl.pallas_call(functools.partial(build_kernel, rows, lags, owned), in_spe...  0.96 us
  transfers between devices with their start and end apart: 12, of which 3 were waited for; matrix products, arithmetic and copies ran while one was open for 0% of the time, Pallas kernels for 11%

profile of v3, /device:TPU:0, one launch (start us, length us, event | category | flops | bytes accessed | tf_op | source)
XLA Modules:
  0.0 29.5 jit_solution(7697512869632930938)
XLA Ops:
  0.0 1.0 %copy-done.1 = bf16[256,1024]{1,0:T(8,128)(2,1)S(1)} copy-done((bf16[256,1024]{1,0:T(8,128)(2,1)S(1)}, bf16[256,1024]{1,0:T(8,128)(2,1)}, u32[]{:S(2)}) %copy-start.1) | copy-done | bytes 524312
  1.0 0.2 deal.1
  1.3 3.1 %collective-permute-start.6 = (bf16[256,128]{1,0:T(8,128)(2,1)S(1)}, bf16[256,128]{1,0:T(8,128)(2,1)S(1)}, u32[]{:S(2)}, u32[]{:S(2)}) collective-permute-start(bf16[256,128]{1,0:T(8,128)(2,1)S(1)} %get-tuple-element.36), channel_id=1, source_target_pairs={{0,4},{4,8},{8,12},{12,0},{1,5},{5,9},{9,13},{13,1},{2,6},{6,10},{... | collective-permute-start | bytes 196616 | tf_op jit(solution)/shard_map/ppermute | solution.py:21
  4.4 2.6 %collective-permute-start.7 = (bf16[256,128]{1,0:T(8,128)(2,1)S(1)}, bf16[256,128]{1,0:T(8,128)(2,1)S(1)}, u32[]{:S(2)}, u32[]{:S(2)}) collective-permute-start(bf16[256,128]{1,0:T(8,128)(2,1)S(1)} %get-tuple-element.37), channel_id=1, source_target_pairs={{0,8},{4,12},{8,0},{12,4},{1,9},{5,13},{9,1},{13,5},{2,10},{6,14},... | collective-permute-start | bytes 196616 | tf_op jit(solution)/shard_map/ppermute | solution.py:21
  7.0 1.3 %collective-permute-start.8 = (bf16[256,128]{1,0:T(8,128)(2,1)S(1)}, bf16[256,128]{1,0:T(8,128)(2,1)S(1)}, u32[]{:S(2)}, u32[]{:S(2)}) collective-permute-start(bf16[256,128]{1,0:T(8,128)(2,1)S(1)} %get-tuple-element.38), channel_id=1, source_target_pairs={{0,12},{4,0},{8,4},{12,8},{1,13},{5,1},{9,5},{13,9},{2,14},{6,2},{... | collective-permute-start | bytes 196616 | tf_op jit(solution)/shard_map/ppermute | solution.py:21
  8.3 0.7 %collective-permute-start = (bf16[256,128]{1,0:T(8,128)(2,1)S(1)}, bf16[256,128]{1,0:T(8,128)(2,1)S(1)}, u32[]{:S(2)}, u32[]{:S(2)}) collective-permute-start(bf16[256,128]{1,0:T(8,128)(2,1)S(1)} %get-tuple-element.25), channel_id=1, source_target_pairs={{0,4},{4,8},{8,12},{12,0},{1,5},{5,9},{9,13},{13,1},{2,6},{6,10},{... | collective-permute-start | bytes 196616 | tf_op jit(solution)/shard_map/ppermute | solution.py:21
  9.0 0.3 %collective-permute-start.1 = (bf16[256,128]{1,0:T(8,128)(2,1)S(1)}, bf16[256,128]{1,0:T(8,128)(2,1)S(1)}, u32[]{:S(2)}, u32[]{:S(2)}) collective-permute-start(bf16[256,128]{1,0:T(8,128)(2,1)S(1)} %get-tuple-element.26), channel_id=1, source_target_pairs={{0,8},{4,12},{8,0},{12,4},{1,9},{5,13},{9,1},{13,5},{2,10},{6,14},... | collective-permute-start | bytes 196616 | tf_op jit(solution)/shard_map/ppermute | solution.py:21
  9.3 0.6 %copy-done.4 = s32[8]{0:T(128)S(1)} copy-done((s32[8]{0:T(128)S(1)}, s32[8]{0:T(128)}, u32[]{:S(2)}) %copy-start.4) | copy-done | bytes 56
  10.0 0.0 copy-done.5
  10.0 1.0 %build.1 = (bf16[2,4,256,256]{3,2,1,0:T(8,128)(2,1)S(1)}, bf16[2,4,256,256]{3,2,1,0:T(8,128)(2,1)S(1)}, f32[2,8,128]{2,1,0:T(8,128)S(1)}) custom-call(f32[8,768]{1,0:T(8,128)S(1)} %copy-done.2, s32[8]{0:T(128)S(1)} %copy-done.4, f32[8,128]{1,0:T(8,128)S(1)} %bitcast.2, s32[1,128]{1,0:T(1,128)S(1)} %bitcast.3), custom_call_target="tpu_custom_call" | custom-call | tf_op jit(solution)/shard_map/build/pallas_call | solution.py:138
  11.0 0.0 collective-permute-done.6.refs_1_
  11.0 2.9 %collective-permute-start.2 = (bf16[256,128]{1,0:T(8,128)(2,1)S(1)}, bf16[256,128]{1,0:T(8,128)(2,1)S(1)}, u32[]{:S(2)}, u32[]{:S(2)}) collective-permute-start(bf16[256,128]{1,0:T(8,128)(2,1)S(1)} %get-tuple-element.27), channel_id=1, source_target_pairs={{0,12},{4,0},{8,4},{12,8},{1,13},{5,1},{9,5},{13,9},{2,14},{6,2},{... | collective-permute-start | bytes 196616 | tf_op jit(solution)/shard_map/ppermute | solution.py:21
  13.8 0.0 collective-permute-done.7.refs_2_
  13.8 0.0 collective-permute-done.8.refs_3_
  13.8 0.7 %mix0.1 = (bf16[256,128]{1,0:T(8,128)(2,1)S(1)}, bf16[256,128]{1,0:T(8,128)(2,1)S(1)}, bf16[256,128]{1,0:T(8,128)(2,1)S(1)}, bf16[256,128]{1,0:T(8,128)(2,1)S(1)}) custom-call(bf16[256,128]{1,0:T(8,128)(2,1)S(1)} %get-tuple-element.35.refs_0_, bf16[256,128]{1,0:T(8,128)(2,1)S(1)} %collective-permute-done.6.refs_1_, ...), custom_call_target="tpu_custom_call" | custom-call | tf_op jit(solution)/shard_map/mix0/pallas_call | solution.py:149
  14.5 1.9 %collective-permute-start.9 = (bf16[256,128]{1,0:T(8,128)(2,1)S(1)}, bf16[256,128]{1,0:T(8,128)(2,1)S(1)}, u32[]{:S(2)}, u32[]{:S(2)}) collective-permute-start(bf16[256,128]{1,0:T(8,128)(2,1)S(1)} %get-tuple-element.40), channel_id=1, source_target_pairs={{0,4},{4,8},{8,12},{12,0},{1,5},{5,9},{9,13},{13,1},{2,6},{6,10},{... | collective-permute-start | bytes 196616 | tf_op jit(solution)/shard_map/ppermute | solution.py:21
  16.4 1.0 %collective-permute-start.10 = (bf16[256,128]{1,0:T(8,128)(2,1)S(1)}, bf16[256,128]{1,0:T(8,128)(2,1)S(1)}, u32[]{:S(2)}, u32[]{:S(2)}) collective-permute-start(bf16[256,128]{1,0:T(8,128)(2,1)S(1)} %get-tuple-element.41), channel_id=1, source_target_pairs={{0,8},{4,12},{8,0},{12,4},{1,9},{5,13},{9,1},{13,5},{2,10},{6,14},... | collective-permute-start | bytes 196616 | tf_op jit(solution)/shard_map/ppermute | solution.py:21
  17.5 0.0 collective-permute-done.refs_1_
  17.5 2.1 %collective-permute-start.11 = (bf16[256,128]{1,0:T(8,128)(2,1)S(1)}, bf16[256,128]{1,0:T(8,128)(2,1)S(1)}, u32[]{:S(2)}, u32[]{:S(2)}) collective-permute-start(bf16[256,128]{1,0:T(8,128)(2,1)S(1)} %get-tuple-element.42), channel_id=1, source_target_pairs={{0,12},{4,0},{8,4},{12,8},{1,13},{5,1},{9,5},{13,9},{2,14},{6,2},{... | collective-permute-start | bytes 196616 | tf_op jit(solution)/shard_map/ppermute | solution.py:21
  19.5 0.0 collective-permute-done.1.refs_2_
  19.5 0.0 collective-permute-done.2.refs_3_
  19.5 0.7 %mix1.1 = (bf16[256,128]{1,0:T(8,128)(2,1)S(1)}, bf16[256,128]{1,0:T(8,128)(2,1)S(1)}, bf16[256,128]{1,0:T(8,128)(2,1)S(1)}, bf16[256,128]{1,0:T(8,128)(2,1)S(1)}) custom-call(bf16[256,128]{1,0:T(8,128)(2,1)S(1)} %get-tuple-element.24.refs_0_, bf16[256,128]{1,0:T(8,128)(2,1)S(1)} %collective-permute-done.refs_1_, ...), custom_call_target="tpu_custom_call" | custom-call | tf_op jit(solution)/shard_map/mix1/pallas_call | solution.py:149
  20.3 0.1 collective-permute-start.3
  20.3 1.8 %collective-permute-start.4 = (bf16[256,128]{1,0:T(8,128)(2,1)S(1)}, bf16[256,128]{1,0:T(8,128)(2,1)S(1)}, u32[]{:S(2)}, u32[]{:S(2)}) collective-permute-start(bf16[256,128]{1,0:T(8,128)(2,1)S(1)} %get-tuple-element.33), channel_id=1, source_target_pairs={{0,8},{4,12},{8,0},{12,4},{1,9},{5,13},{9,1},{13,5},{2,10},{6,14},... | collective-permute-start | bytes 196616 | tf_op jit(solution)/shard_map/ppermute | solution.py:21
  22.1 2.0 %collective-permute-start.5 = (bf16[256,128]{1,0:T(8,128)(2,1)S(1)}, bf16[256,128]{1,0:T(8,128)(2,1)S(1)}, u32[]{:S(2)}, u32[]{:S(2)}) collective-permute-start(bf16[256,128]{1,0:T(8,128)(2,1)S(1)} %get-tuple-element.34), channel_id=1, source_target_pairs={{0,12},{4,0},{8,4},{12,8},{1,13},{5,1},{9,5},{13,9},{2,14},{6,2},{... | collective-permute-start | bytes 196616 | tf_op jit(solution)/shard_map/ppermute | solution.py:21
  24.1 0.4 %collective-permute-done.10.refs_2_ = bf16[256,128]{1,0:T(8,128)(2,1)S(1)} collective-permute-done((bf16[256,128]{1,0:T(8,128)(2,1)S(1)}, bf16[256,128]{1,0:T(8,128)(2,1)S(1)}, u32[]{:S(2)}, u32[]{:S(2)}) %collective-permute-start.10) | collective-permute-done | bytes 65568 | tf_op jit(solution)/shard_map/ppermute | solution.py:21
  24.5 0.0 collective-permute-done.11.refs_3_
  24.6 0.8 %gate0.1.refs_4_ = bf16[256,1024]{1,0:T(8,128)(2,1)} custom-call(bf16[256,1024]{1,0:T(8,128)(2,1)S(1)} %copy-done, bf16[256,128]{1,0:T(8,128)(2,1)S(1)} %get-tuple-element.39.refs_0_, bf16[256,128]{1,0:T(8,128)(2,1)S(1)} %collective-permute-done.9.refs_1_, bf16[256,128]{1,0:T(8,128)(2,1)S(1)} %collective-permute-done.10.refs_2_, ...), custom_call_target="tpu_custom_call" | custom-call | tf_op jit(solution)/shard_map/gate0/pallas_call | solution.py:164
  25.3 1.2 %collective-permute-done.3.refs_1_ = bf16[256,128]{1,0:T(8,128)(2,1)S(1)} collective-permute-done((bf16[256,128]{1,0:T(8,128)(2,1)S(1)}, bf16[256,128]{1,0:T(8,128)(2,1)S(1)}, u32[]{:S(2)}, u32[]{:S(2)}) %collective-permute-start.3) | collective-permute-done | bytes 65568 | tf_op jit(solution)/shard_map/ppermute | solution.py:21
  26.5 2.3 %collective-permute-done.4.refs_2_ = bf16[256,128]{1,0:T(8,128)(2,1)S(1)} collective-permute-done((bf16[256,128]{1,0:T(8,128)(2,1)S(1)}, bf16[256,128]{1,0:T(8,128)(2,1)S(1)}, u32[]{:S(2)}, u32[]{:S(2)}) %collective-permute-start.4) | collective-permute-done | bytes 65568 | tf_op jit(solution)/shard_map/ppermute | solution.py:21
  28.8 0.0 collective-permute-done.5.refs_3_
  28.8 0.8 %gate1.1 = bf16[256,1024]{1,0:T(8,128)(2,1)} custom-call(bf16[256,1024]{1,0:T(8,128)(2,1)S(1)} %copy-done, bf16[256,128]{1,0:T(8,128)(2,1)S(1)} %get-tuple-element.31.refs_0_, bf16[256,128]{1,0:T(8,128)(2,1)S(1)} %collective-permute-done.3.refs_1_, bf16[256,128]{1,0:T(8,128)(2,1)S(1)} %collective-permute-done.4.refs_2_, ...), custom_call_target="tpu_custom_call", output_to_operand_aliasing={{}: (5, {})} | custom-call | tf_op jit(solution)/shard_map/gate1/pallas_call | solution.py:164
  (10 shorter events, 0.0 us)
Async XLA Ops:
  0.0 1.0 %copy-start.1 = (bf16[256,1024]{1,0:T(8,128)(2,1)S(1)}, bf16[256,1024]{1,0:T(8,128)(2,1)}, u32[]{:S(2)}) copy-start(bf16[256,1024]{1,0:T(8,128)(2,1)} %x_ref.1) | copy-start | bytes 1572868
  1.0 8.3 %copy-start.2 = (f32[8,768]{1,0:T(8,128)S(1)}, f32[8,768]{1,0:T(8,128)}, u32[]{:S(2)}) copy-start(f32[8,768]{1,0:T(8,128)} %filters_ref.1) | copy-start | bytes 73732
  1.3 9.7 %collective-permute-start.6 = (bf16[256,128]{1,0:T(8,128)(2,1)S(1)}, bf16[256,128]{1,0:T(8,128)(2,1)S(1)}, u32[]{:S(2)}, u32[]{:S(2)}) collective-permute-start(bf16[256,128]{1,0:T(8,128)(2,1)S(1)} %get-tuple-element.36), channel_id=1, source_target_pairs={{0,4},{4,8},{8,12},{12,0},{1,5},{5,9},{9,13},{13,1},{2,6},{6,10},{... | collective-permute-start | bytes 196616 | tf_op jit(solution)/shard_map/ppermute | solution.py:21
  4.4 9.5 %collective-permute-start.7 = (bf16[256,128]{1,0:T(8,128)(2,1)S(1)}, bf16[256,128]{1,0:T(8,128)(2,1)S(1)}, u32[]{:S(2)}, u32[]{:S(2)}) collective-permute-start(bf16[256,128]{1,0:T(8,128)(2,1)S(1)} %get-tuple-element.37), channel_id=1, source_target_pairs={{0,8},{4,12},{8,0},{12,4},{1,9},{5,13},{9,1},{13,5},{2,10},{6,14},... | collective-permute-start | bytes 196616 | tf_op jit(solution)/shard_map/ppermute | solution.py:21
  7.0 2.4 %copy-start.3 = (f32[1024]{0:T(1024)S(1)}, f32[1024]{0:T(1024)}, u32[]{:S(2)}) copy-start(f32[1024]{0:T(1024)} %param.10) | copy-start | bytes 12292
  7.0 6.9 %collective-permute-start.8 = (bf16[256,128]{1,0:T(8,128)(2,1)S(1)}, bf16[256,128]{1,0:T(8,128)(2,1)S(1)}, u32[]{:S(2)}, u32[]{:S(2)}) collective-permute-start(bf16[256,128]{1,0:T(8,128)(2,1)S(1)} %get-tuple-element.38), channel_id=1, source_target_pairs={{0,12},{4,0},{8,4},{12,8},{1,13},{5,1},{9,5},{13,9},{2,14},{6,2},{... | collective-permute-start | bytes 196616 | tf_op jit(solution)/shard_map/ppermute | solution.py:21
  8.3 9.1 %collective-permute-start = (bf16[256,128]{1,0:T(8,128)(2,1)S(1)}, bf16[256,128]{1,0:T(8,128)(2,1)S(1)}, u32[]{:S(2)}, u32[]{:S(2)}) collective-permute-start(bf16[256,128]{1,0:T(8,128)(2,1)S(1)} %get-tuple-element.25), channel_id=1, source_target_pairs={{0,4},{4,8},{8,12},{12,0},{1,5},{5,9},{9,13},{13,1},{2,6},{6,10},{... | collective-permute-start | bytes 196616 | tf_op jit(solution)/shard_map/ppermute | solution.py:21
  9.0 10.5 %collective-permute-start.1 = (bf16[256,128]{1,0:T(8,128)(2,1)S(1)}, bf16[256,128]{1,0:T(8,128)(2,1)S(1)}, u32[]{:S(2)}, u32[]{:S(2)}) collective-permute-start(bf16[256,128]{1,0:T(8,128)(2,1)S(1)} %get-tuple-element.26), channel_id=1, source_target_pairs={{0,8},{4,12},{8,0},{12,4},{1,9},{5,13},{9,1},{13,5},{2,10},{6,14},... | collective-permute-start | bytes 196616 | tf_op jit(solution)/shard_map/ppermute | solution.py:21
  9.3 0.7 %copy-start.4 = (s32[8]{0:T(128)S(1)}, s32[8]{0:T(128)}, u32[]{:S(2)}) copy-start(s32[8]{0:T(128)} %lengths_ref.1) | copy-start | bytes 100
  9.3 0.7 %copy-start.5 = (s32[128]{0:T(128)S(1)}, s32[128]{0:T(128)}, u32[]{:S(2)}) copy-start(s32[128]{0:T(128)} %param.11) | copy-start | bytes 1540
  11.0 8.6 %collective-permute-start.2 = (bf16[256,128]{1,0:T(8,128)(2,1)S(1)}, bf16[256,128]{1,0:T(8,128)(2,1)S(1)}, u32[]{:S(2)}, u32[]{:S(2)}) collective-permute-start(bf16[256,128]{1,0:T(8,128)(2,1)S(1)} %get-tuple-element.27), channel_id=1, source_target_pairs={{0,12},{4,0},{8,4},{12,8},{1,13},{5,1},{9,5},{13,9},{2,14},{6,2},{... | collective-permute-start | bytes 196616 | tf_op jit(solution)/shard_map/ppermute | solution.py:21
  14.5 7.6 %collective-permute-start.9 = (bf16[256,128]{1,0:T(8,128)(2,1)S(1)}, bf16[256,128]{1,0:T(8,128)(2,1)S(1)}, u32[]{:S(2)}, u32[]{:S(2)}) collective-permute-start(bf16[256,128]{1,0:T(8,128)(2,1)S(1)} %get-tuple-element.40), channel_id=1, source_target_pairs={{0,4},{4,8},{8,12},{12,0},{1,5},{5,9},{9,13},{13,1},{2,6},{6,10},{... | collective-permute-start | bytes 196616 | tf_op jit(solution)/shard_map/ppermute | solution.py:21
  16.4 8.1 %collective-permute-start.10 = (bf16[256,128]{1,0:T(8,128)(2,1)S(1)}, bf16[256,128]{1,0:T(8,128)(2,1)S(1)}, u32[]{:S(2)}, u32[]{:S(2)}) collective-permute-start(bf16[256,128]{1,0:T(8,128)(2,1)S(1)} %get-tuple-element.41), channel_id=1, source_target_pairs={{0,8},{4,12},{8,0},{12,4},{1,9},{5,13},{9,1},{13,5},{2,10},{6,14},... | collective-permute-start | bytes 196616 | tf_op jit(solution)/shard_map/ppermute | solution.py:21
  17.5 7.1 %collective-permute-start.11 = (bf16[256,128]{1,0:T(8,128)(2,1)S(1)}, bf16[256,128]{1,0:T(8,128)(2,1)S(1)}, u32[]{:S(2)}, u32[]{:S(2)}) collective-permute-start(bf16[256,128]{1,0:T(8,128)(2,1)S(1)} %get-tuple-element.42), channel_id=1, source_target_pairs={{0,12},{4,0},{8,4},{12,8},{1,13},{5,1},{9,5},{13,9},{2,14},{6,2},{... | collective-permute-start | bytes 196616 | tf_op jit(solution)/shard_map/ppermute | solution.py:21
  19.5 5.0 %copy-start = (bf16[256,1024]{1,0:T(8,128)(2,1)S(1)}, bf16[256,1024]{1,0:T(8,128)(2,1)}, u32[]{:S(2)}) copy-start(bf16[256,1024]{1,0:T(8,128)(2,1)} %gate_ref.3) | copy-start | bytes 1572868
  20.3 6.2 %collective-permute-start.3 = (bf16[256,128]{1,0:T(8,128)(2,1)S(1)}, bf16[256,128]{1,0:T(8,128)(2,1)S(1)}, u32[]{:S(2)}, u32[]{:S(2)}) collective-permute-start(bf16[256,128]{1,0:T(8,128)(2,1)S(1)} %get-tuple-element.32), channel_id=1, source_target_pairs={{0,4},{4,8},{8,12},{12,0},{1,5},{5,9},{9,13},{13,1},{2,6},{6,10},{... | collective-permute-start | bytes 196616 | tf_op jit(solution)/shard_map/ppermute | solution.py:21
  20.3 8.4 %collective-permute-start.4 = (bf16[256,128]{1,0:T(8,128)(2,1)S(1)}, bf16[256,128]{1,0:T(8,128)(2,1)S(1)}, u32[]{:S(2)}, u32[]{:S(2)}) collective-permute-start(bf16[256,128]{1,0:T(8,128)(2,1)S(1)} %get-tuple-element.33), channel_id=1, source_target_pairs={{0,8},{4,12},{8,0},{12,4},{1,9},{5,13},{9,1},{13,5},{2,10},{6,14},... | collective-permute-start | bytes 196616 | tf_op jit(solution)/shard_map/ppermute | solution.py:21
  22.1 6.6 %collective-permute-start.5 = (bf16[256,128]{1,0:T(8,128)(2,1)S(1)}, bf16[256,128]{1,0:T(8,128)(2,1)S(1)}, u32[]{:S(2)}, u32[]{:S(2)}) collective-permute-start(bf16[256,128]{1,0:T(8,128)(2,1)S(1)} %get-tuple-element.34), channel_id=1, source_target_pairs={{0,12},{4,0},{8,4},{12,8},{1,13},{5,1},{9,5},{13,9},{2,14},{6,2},{... | collective-permute-start | bytes 196616 | tf_op jit(solution)/shard_map/ppermute | solution.py:21

commit v4 on v2

--- a/solution.py
+++ b/solution.py
@@ -25,38 +25,60 @@
     return pltpu.with_memory_space_constraint(array, VMEM)
 
 
-def build_kernel(rows, lags, owned, filters_ref, lengths_ref, gain_ref, perm_ref, fwd_ref, bwd_ref, gains_ref):
+def build_kernel(rows, lags, owned, owns, filters_ref, lengths_ref, gain_ref, perm_ref, fwd_ref, bwd_ref, gains_ref):
     first = lax.axis_index("ctx") * owned
     group_w = perm_ref.shape[1]
     taps = filters_ref.shape[1]
     span = lags * rows
     target = lax.broadcasted_iota(jnp.int32, (group_w, group_w), 0)
     match = perm_ref[...] == target
-    for own in range(owned):
+    group_ids = lax.broadcasted_iota(jnp.int32, lengths_ref.shape, 1)
+    tap_ids = lax.broadcasted_iota(jnp.int32, (1, taps), 1)
+    for at, own in enumerate(owns):
         group = first + own
-        taps_row = filters_ref[pl.ds(group, 1), :]
-        tap_ids = lax.broadcasted_iota(jnp.int32, (1, taps), 1)
-        taps_row = jnp.where(tap_ids < lengths_ref[group] * rows, taps_row, 0.0)
+        length = jnp.sum(jnp.where(group_ids == group, lengths_ref[...], 0), axis=1, keepdims=True)
+        taps_row = jnp.where(tap_ids < length * rows, filters_ref[pl.ds(group, 1), :], 0.0)
         taps_row = jnp.concatenate([taps_row, jnp.zeros((1, span - taps), F32)], axis=1)
         strip = pltpu.roll(jnp.broadcast_to(taps_row, (rows, span)), 0, 1, stride=1, stride_axis=0)
         for lag in range(lags):
             block = strip[:, lag * rows : (lag + 1) * rows]
-            bwd_ref[own, lag] = block.astype(BF16)
-            fwd_ref[own, lag] = block.T.astype(BF16)
+            bwd_ref[at, lag] = block.astype(BF16)
+            fwd_ref[at, lag] = block.T.astype(BF16)
         gain_row = gain_ref[pl.ds(group, 1), :]
         spread = jnp.where(match, gain_row, 0.0)
-        gains_ref[own, 0:1, :] = gain_row
-        gains_ref[own, 1:2, :] = jnp.sum(spread.T, axis=0, keepdims=True)
-
-
-def mix_kernel(count, lags, own, *refs):
+        gains_ref[at, 0:1, :] = gain_row
+        gains_ref[at, 1:2, :] = jnp.sum(spread.T, axis=0, keepdims=True)
+
+
+def deal_kernel(count, owned, group_w, messages, x_ref, *refs):
+    sems = refs[-1]
+    small = (len(refs) - 1 - len(messages)) // 2
+    outs = refs[small:-1]
+    me = lax.axis_index("ctx")
+    copies = []
+    for i, (k, chunk) in enumerate(messages):
+        at = (lax.rem(me + k, count) * owned + chunk[0]) * group_w
+        place = pl.ds(pl.multiple_of(at, group_w), len(chunk) * group_w)
+        copies.append(pltpu.make_async_copy(x_ref.at[:, place], outs[i], sems.at[i]))
+        copies[i].start()
+    for i in range(small):
+        at = len(messages) + i
+        copies.append(pltpu.make_async_copy(refs[i], outs[at], sems.at[at]))
+        copies[at].start()
+    for copy in copies:
+        copy.wait()
+
+
+def mix_kernel(count, lags, own, messages, late, *refs):
     blocks, (fwd_ref, bwd_ref, gains_ref) = refs[:count], refs[count : count + 3]
-    outs, (inputs, sums) = refs[count + 3 : 2 * count + 3], refs[2 * count + 3 :]
+    earlier, refs = refs[count + 3 : count + 3 + len(late)], refs[count + 3 + len(late) :]
+    outs, (inputs, sums) = refs[:count], refs[count:]
     me = lax.axis_index("ctx")
     group_w = gains_ref.shape[2]
     places = [lax.rem(me - k + count, count) for k in range(count)]
-    for k in range(count):
-        inputs[places[k]] = blocks[k][...]
+    for block, (k, chunk) in zip(blocks, messages):
+        first = chunk.index(own) * group_w
+        inputs[places[k]] = block[:, first : first + group_w]
     values = jnp.concatenate([inputs[i] for i in range(count)], axis=1).astype(F32)
     gated = (values * jnp.tile(gains_ref[own, 0:1, :], (1, count))).astype(BF16)
     flipped = (values * jnp.tile(gains_ref[own, 1:2, :], (1, count))).astype(BF16)
@@ -77,20 +99,23 @@
     for i in range(count):
         sums[i] = (ahead[i] + behind[i].astype(BF16).astype(F32)).astype(BF16)
     for k in range(count):
-        outs[k][...] = sums[places[k]]
-
-
-def gate_kernel(count, owned, own, gate_ref, *refs):
-    blocks, out_ref, (pieces, sems) = refs[:count], refs[-3], refs[-2:]
+        outs[k][:, outs[k].shape[1] - group_w :] = sums[places[k]]
+    for k, ref in zip(late, earlier):
+        outs[k][:, :group_w] = ref[...]
+
+
+def gate_kernel(count, owned, messages, group_w, gate_ref, *refs):
+    blocks, out_ref, (pieces, sems) = refs[: len(messages)], refs[-3], refs[-2:]
     me = lax.axis_index("ctx")
-    group_w = blocks[0].shape[1]
     copies = []
-    for k in range(count):
-        at = (lax.rem(me + k, count) * owned + own) * group_w
-        place = pl.ds(pl.multiple_of(at, group_w), group_w)
-        pieces[k] = (gate_ref[:, place].astype(F32) * blocks[k][...].astype(F32)).astype(BF16)
-        copies.append(pltpu.make_async_copy(pieces.at[k], out_ref.at[:, place], sems.at[k]))
-        copies[k].start()
+    for i, (k, chunk) in enumerate(messages):
+        at = (lax.rem(me + k, count) * owned + chunk[0]) * group_w
+        place = pl.ds(pl.multiple_of(at, group_w), len(chunk) * group_w)
+        mixed = (gate_ref[:, place].astype(F32) * blocks[i][...].astype(F32)).astype(BF16)
+        piece = pieces.at[i, :, : len(chunk) * group_w]
+        piece[...] = mixed
+        copies.append(pltpu.make_async_copy(piece, out_ref.at[:, place], sems.at[i]))
+        copies[i].start()
     for copy in copies:
         copy.wait()
 
@@ -102,48 +127,82 @@
     group_w = permutation.shape[0]
     owned = groups_dev // count
     lags = taps // rows + 1
-    me = lax.axis_index("ctx")
     vmem, anywhere = pl.BlockSpec(memory_space=VMEM), pl.BlockSpec(memory_space=pl.ANY)
-
-    def part(k, own):
-        group = lax.rem(me + k, count) * owned + own
-        return lax.dynamic_slice(sequence, (0, group * group_w), (rows, group_w))
-
-    def deal(own):
-        return [part(0, own)] + [rotated(part(k, own), k) for k in range(1, count)]
-
-    blocks = [deal(own) for own in range(owned)]
-    toeplitz = pl.pallas_call(
-        functools.partial(build_kernel, rows, lags, owned),
-        in_specs=[vmem, pl.BlockSpec(memory_space=SMEM), vmem, vmem],
-        out_specs=[vmem] * 3,
-        out_shape=[VMEM((owned, lags, rows, rows), BF16)] * 2 + [VMEM((owned, 8, group_w), F32)],
-        name="build",
-    )(filters, lengths, gain.reshape(groups_dev, group_w), permutation.reshape(1, group_w))
-    back = []
+    params = pltpu.CompilerParams(vmem_limit_bytes=24 << 20)
+    deals = (((2, (0,)), (1, (0,)), (3, (0,)), (2, (1,)), (1, (1,)), (3, (1,)), (0, (0,)), (0, (1,))),)
+    used = (((0, (0,)), (2, (0,)), (1, (0,)), (3, (0,))), ((0, (1,)), (2, (1,)), (1, (1,)), (3, (1,))))
+    gates = (((0, (0,)), (3, (0,)), (2, (0,)), (1, (0,))), ((0, (1,)), (3, (1,)), (2, (1,)), (1, (1,))))
+
+    sequence = pltpu.with_memory_space_constraint(sequence, pltpu.HBM)
+    sent = {}
+    small = [
+        filters,
+        lengths.reshape(1, groups_dev),
+        gain.reshape(groups_dev, group_w),
+        permutation.reshape(1, group_w),
+    ]
+    small = [pltpu.with_memory_space_constraint(array, pltpu.HBM) for array in small]
+    for d, messages in enumerate(deals):
+        fetched = [] if d else small
+        parts = pl.pallas_call(
+            functools.partial(deal_kernel, count, owned, group_w, messages),
+            in_specs=[anywhere] * (1 + len(fetched)),
+            out_specs=[vmem] * (len(messages) + len(fetched)),
+            out_shape=[VMEM((rows, len(chunk) * group_w), BF16) for _, chunk in messages]
+            + [VMEM(array.shape, array.dtype) for array in fetched],
+            scratch_shapes=[pltpu.SemaphoreType.DMA((len(messages) + len(fetched),))],
+            compiler_params=params,
+            name=f"deal{d}",
+        )(sequence, *fetched)
+        if fetched:
+            small = parts[len(messages) :]
+        for (k, chunk), part in zip(messages, parts):
+            sent[k, chunk] = part if k == 0 else rotated(part, k)
+    built = [
+        pl.pallas_call(
+            functools.partial(build_kernel, rows, lags, owned, owns),
+            in_specs=[vmem] * 4,
+            out_specs=[vmem] * 3,
+            out_shape=[VMEM((len(owns), lags, rows, rows), BF16)] * 2 + [VMEM((len(owns), 8, group_w), F32)],
+            compiler_params=params,
+            name=f"build{owns[0]}",
+        )(*map(held, small))
+        for owns in [tuple(range(owned))]
+    ]
+    back = {}
+    merged = ()
     for own in range(owned):
+        late = merged if own else ()
+        earlier = [outs[k] for k in late] if own else []
         outs = pl.pallas_call(
-            functools.partial(mix_kernel, count, lags, own),
-            in_specs=[vmem] * (count + 3),
+            functools.partial(mix_kernel, count, lags, own, used[own], late),
+            in_specs=[vmem] * (count + 3 + len(late)),
             out_specs=[vmem] * count,
-            out_shape=[VMEM((rows, group_w), BF16)] * count,
+            out_shape=[VMEM((rows, 2 * group_w if k in late else group_w), BF16) for k in range(count)],
             scratch_shapes=[VMEM((count, rows, group_w), BF16)] * 2,
+            compiler_params=params,
             name=f"mix{own}",
-        )(*map(held, [*blocks[own], *toeplitz]))
-        back.append([outs[0]] + [rotated(outs[k], -k) for k in range(1, count)])
+        )(*map(held, [*[sent[message] for message in used[own]], *built[0], *earlier]))
+        for k in range(count):
+            if k in merged and not own:
+                continue
+            chunk = (0, 1) if k in merged else (own,)
+            back[k, chunk] = outs[k] if k == 0 else rotated(outs[k], -k)
     gate = held(gate)
     out = []
-    for own in range(owned):
+    for g, messages in enumerate(gates):
+        widest = max(len(chunk) for _, chunk in messages) * group_w
         out = [
             pl.pallas_call(
-                functools.partial(gate_kernel, count, owned, own),
-                in_specs=[vmem] * (count + 1) + [anywhere] * len(out),
+                functools.partial(gate_kernel, count, owned, messages, group_w),
+                in_specs=[vmem] * (len(messages) + 1) + [anywhere] * len(out),
                 out_specs=anywhere,
                 out_shape=jax.ShapeDtypeStruct((rows, width), BF16),
-                scratch_shapes=[VMEM((count, rows, group_w), BF16), pltpu.SemaphoreType.DMA((count,))],
-                input_output_aliases={count + 1: 0} if out else {},
-                name=f"gate{own}",
-            )(gate, *map(held, back[own]), *out)
+                scratch_shapes=[VMEM((len(messages), rows, widest), BF16), pltpu.SemaphoreType.DMA((len(messages),))],
+                input_output_aliases={len(messages) + 1: 0} if out else {},
+                compiler_params=params,
+                name=f"gate{g}",
+            )(gate, *[held(back[message]) for message in messages], *out)
         ]
     return out[0]
 
@@ -189,7 +248,7 @@
 def body(*args):
     count = lax.axis_size("ctx")
     groups_dev = args[2].shape[0]
-    if count <= 8 and groups_dev % count == 0:
+    if count == 4 and groups_dev == 2 * count:
         return dealt(*args)
     return halos(*args)
 

time: 33.6 us -> 28.9 us (0.86)
  waiting for transfers between devices: 6.88 us -> 2.17 us
  starting transfers between devices: 19.9 us -> 21.9 us
  local copies, waits for them, and re-layouts: 1.11 us -> 0.01 us
  Pallas kernels: 5.39 us -> 4.63 us
    ppermute x12, waiting for transfers between devices: 6.88 us -> 2.17 us  [rotated(): lax.ppermute(array, 'ctx', [(i, (i + by) % count) for i in range(count)])]
    ppermute x12, starting transfers between devices: 19.9 us -> 21.9 us  [rotated(): lax.ppermute(array, 'ctx', [(i, (i + by) % count) for i in range(count)])]
    dynamic_slice x1 -> x0, local copies, waits for them, and re-layouts: 1.11 us -> none  [part(): return lax.dynamic_slice(sequence, (0, group * group_w), (rows, group_w))]
    pallas_call x5 -> x6, Pallas kernels: 5.39 us -> 4.63 us  [the longest x2 1.53 us: dealt(): pl.pallas_call(functools.partial(gate_kernel, count, owned, messages, gro...]
  transfers between devices with their start and end apart: 12 -> 12, of which waited for: 4 -> 2; matrix products, arithmetic and copies ran while one was open for 0% -> 0% of each run, Pallas kernels for 14% -> 9%
where the time goes in v4:
time: 28.9 us; the launch traced here: 28.7 us
  starting transfers between devices  21.9 us (76%)
  Pallas kernels  4.63 us (16%)
  waiting for transfers between devices  2.17 us (8%)
    ppermute x12, starting transfers between devices, rotated(): lax.ppermute(array, 'ctx', [(i, (i + by) % count) for i in range(count)])  21.9 us
    ppermute x12, waiting for transfers between devices, rotated(): lax.ppermute(array, 'ctx', [(i, (i + by) % count) for i in range(count)])  2.17 us
    pallas_call x2, Pallas kernels, dealt(): pl.pallas_call(functools.partial(gate_kernel, count, owned, messages, gro...  1.53 us
    pallas_call x2, Pallas kernels, dealt(): pl.pallas_call(functools.partial(mix_kernel, count, lags, own, used[own],...  1.4 us
    pallas_call x1, Pallas kernels, dealt(): pl.pallas_call(functools.partial(deal_kernel, count, owned, group_w, mess...  1.18 us
  transfers between devices with their start and end apart: 12, of which 2 were waited for; matrix products, arithmetic and copies ran while one was open for 0% of the time, Pallas kernels for 9%

profile of v4, /device:TPU:0, one launch (start us, length us, event | category | flops | bytes accessed | tf_op | source)
XLA Modules:
  0.0 28.7 jit_solution(1907730279502583068)
XLA Ops:
  0.0 1.2 %deal0.1 = (bf16[256,128]{1,0:T(8,128)(2,1)S(1)}, bf16[256,128]{1,0:T(8,128)(2,1)S(1)}, bf16[256,128]{1,0:T(8,128)(2,1)S(1)}, bf16[256,128]{1,0:T(8,128)(2,1)S(1...) custom-call(bf16[256,1024]{1,0:T(8,128)(2,1)} %x_ref.1, ...), custom_call_target="tpu_custom_call" | custom-call | tf_op jit(solution)/shard_map/deal0/pallas_call | solution.py:147
  1.2 4.1 %collective-permute-start.6 = (bf16[256,128]{1,0:T(8,128)(2,1)S(1)}, bf16[256,128]{1,0:T(8,128)(2,1)S(1)}, u32[]{:S(2)}, u32[]{:S(2)}) collective-permute-start(bf16[256,128]{1,0:T(8,128)(2,1)S(1)} %get-tuple-element.44), channel_id=1, source_target_pairs={{0,8},{4,12},{8,0},{12,4},{1,9},{5,13},{9,1},{13,5},{2,10},{6,14},... | collective-permute-start | bytes 196616 | tf_op jit(solution)/shard_map/ppermute | solution.py:21
  5.3 1.6 %collective-permute-start.7 = (bf16[256,128]{1,0:T(8,128)(2,1)S(1)}, bf16[256,128]{1,0:T(8,128)(2,1)S(1)}, u32[]{:S(2)}, u32[]{:S(2)}) collective-permute-start(bf16[256,128]{1,0:T(8,128)(2,1)S(1)} %get-tuple-element.45), channel_id=1, source_target_pairs={{0,4},{4,8},{8,12},{12,0},{1,5},{5,9},{9,13},{13,1},{2,6},{6,10},{... | collective-permute-start | bytes 196616 | tf_op jit(solution)/shard_map/ppermute | solution.py:21
  6.9 2.2 %collective-permute-start.8 = (bf16[256,128]{1,0:T(8,128)(2,1)S(1)}, bf16[256,128]{1,0:T(8,128)(2,1)S(1)}, u32[]{:S(2)}, u32[]{:S(2)}) collective-permute-start(bf16[256,128]{1,0:T(8,128)(2,1)S(1)} %get-tuple-element.46), channel_id=1, source_target_pairs={{0,12},{4,0},{8,4},{12,8},{1,13},{5,1},{9,5},{13,9},{2,14},{6,2},{... | collective-permute-start | bytes 196616 | tf_op jit(solution)/shard_map/ppermute | solution.py:21
  9.1 0.0 collective-permute-start
  9.1 0.6 %collective-permute-start.1 = (bf16[256,128]{1,0:T(8,128)(2,1)S(1)}, bf16[256,128]{1,0:T(8,128)(2,1)S(1)}, u32[]{:S(2)}, u32[]{:S(2)}) collective-permute-start(bf16[256,128]{1,0:T(8,128)(2,1)S(1)} %get-tuple-element.30), channel_id=1, source_target_pairs={{0,4},{4,8},{8,12},{12,0},{1,5},{5,9},{9,13},{13,1},{2,6},{6,10},{... | collective-permute-start | bytes 196616 | tf_op jit(solution)/shard_map/ppermute | solution.py:21
  9.7 0.5 %build0.1 = (bf16[2,4,256,256]{3,2,1,0:T(8,128)(2,1)S(1)}, bf16[2,4,256,256]{3,2,1,0:T(8,128)(2,1)S(1)}, f32[2,8,128]{2,1,0:T(8,128)S(1)}) custom-call(f32[8,768]{1,0:T(8,128)S(1)} %get-tuple-element.32.filters_ref, s32[1,8]{1,0:T(1,128)S(1)} %get-tuple-element.33.lengths_ref, f32[8,128]{1,0:T(8,128)S(1)} %get-tuple-element.34.gain_ref, ...), custom_call_target="tpu_custom_call" | custom-call | tf_op jit(solution)/shard_map/build0/pallas_call | solution.py:162
  10.2 0.0 collective-permute-done.6.refs_1_
  10.2 3.3 %collective-permute-start.2 = (bf16[256,128]{1,0:T(8,128)(2,1)S(1)}, bf16[256,128]{1,0:T(8,128)(2,1)S(1)}, u32[]{:S(2)}, u32[]{:S(2)}) collective-permute-start(bf16[256,128]{1,0:T(8,128)(2,1)S(1)} %get-tuple-element.31), channel_id=1, source_target_pairs={{0,12},{4,0},{8,4},{12,8},{1,13},{5,1},{9,5},{13,9},{2,14},{6,2},{... | collective-permute-start | bytes 196616 | tf_op jit(solution)/shard_map/ppermute | solution.py:21
  13.5 0.0 collective-permute-done.7.refs_2_
  13.5 0.0 collective-permute-done.8.refs_3_
  13.5 0.7 %mix0.1 = (bf16[256,128]{1,0:T(8,128)(2,1)S(1)}, bf16[256,128]{1,0:T(8,128)(2,1)S(1)}, bf16[256,128]{1,0:T(8,128)(2,1)S(1)}, bf16[256,128]{1,0:T(8,128)(2,1)S(1)}) custom-call(bf16[256,128]{1,0:T(8,128)(2,1)S(1)} %get-tuple-element.43.refs_0_, bf16[256,128]{1,0:T(8,128)(2,1)S(1)} %collective-permute-done.6.refs_1_, ...), custom_call_target="tpu_custom_call" | custom-call | tf_op jit(solution)/shard_map/mix0/pallas_call | solution.py:177
  14.2 0.5 %collective-permute-start.9 = (bf16[256,128]{1,0:T(8,128)(2,1)S(1)}, bf16[256,128]{1,0:T(8,128)(2,1)S(1)}, u32[]{:S(2)}, u32[]{:S(2)}) collective-permute-start(bf16[256,128]{1,0:T(8,128)(2,1)S(1)} %get-tuple-element.48), channel_id=1, source_target_pairs={{0,4},{4,8},{8,12},{12,0},{1,5},{5,9},{9,13},{13,1},{2,6},{6,10},{... | collective-permute-start | bytes 196616 | tf_op jit(solution)/shard_map/ppermute | solution.py:21
  14.8 2.4 %collective-permute-start.10 = (bf16[256,128]{1,0:T(8,128)(2,1)S(1)}, bf16[256,128]{1,0:T(8,128)(2,1)S(1)}, u32[]{:S(2)}, u32[]{:S(2)}) collective-permute-start(bf16[256,128]{1,0:T(8,128)(2,1)S(1)} %get-tuple-element.49), channel_id=1, source_target_pairs={{0,8},{4,12},{8,0},{12,4},{1,9},{5,13},{9,1},{13,5},{2,10},{6,14},... | collective-permute-start | bytes 196616 | tf_op jit(solution)/shard_map/ppermute | solution.py:21
  17.2 0.0 collective-permute-done.refs_1_
  17.2 3.3 %collective-permute-start.11 = (bf16[256,128]{1,0:T(8,128)(2,1)S(1)}, bf16[256,128]{1,0:T(8,128)(2,1)S(1)}, u32[]{:S(2)}, u32[]{:S(2)}) collective-permute-start(bf16[256,128]{1,0:T(8,128)(2,1)S(1)} %get-tuple-element.50), channel_id=1, source_target_pairs={{0,12},{4,0},{8,4},{12,8},{1,13},{5,1},{9,5},{13,9},{2,14},{6,2},{... | collective-permute-start | bytes 196616 | tf_op jit(solution)/shard_map/ppermute | solution.py:21
  20.4 0.0 collective-permute-done.1.refs_2_
  20.4 0.0 collective-permute-done.2.refs_3_
  20.4 0.0 copy-start
  20.5 0.7 %mix1.1 = (bf16[256,128]{1,0:T(8,128)(2,1)S(1)}, bf16[256,128]{1,0:T(8,128)(2,1)S(1)}, bf16[256,128]{1,0:T(8,128)(2,1)S(1)}, bf16[256,128]{1,0:T(8,128)(2,1)S(1)}) custom-call(bf16[256,128]{1,0:T(8,128)(2,1)S(1)} %get-tuple-element.28.refs_0_, bf16[256,128]{1,0:T(8,128)(2,1)S(1)} %collective-permute-done.refs_1_, ...), custom_call_target="tpu_custom_call" | custom-call | tf_op jit(solution)/shard_map/mix1/pallas_call | solution.py:177
  21.2 0.1 collective-permute-start.3
  21.2 0.6 %collective-permute-start.4 = (bf16[256,128]{1,0:T(8,128)(2,1)S(1)}, bf16[256,128]{1,0:T(8,128)(2,1)S(1)}, u32[]{:S(2)}, u32[]{:S(2)}) collective-permute-start(bf16[256,128]{1,0:T(8,128)(2,1)S(1)} %get-tuple-element.41), channel_id=1, source_target_pairs={{0,8},{4,12},{8,0},{12,4},{1,9},{5,13},{9,1},{13,5},{2,10},{6,14},... | collective-permute-start | bytes 196616 | tf_op jit(solution)/shard_map/ppermute | solution.py:21
  21.8 0.0 collective-permute-done.9.refs_1_
  21.8 3.2 %collective-permute-start.5 = (bf16[256,128]{1,0:T(8,128)(2,1)S(1)}, bf16[256,128]{1,0:T(8,128)(2,1)S(1)}, u32[]{:S(2)}, u32[]{:S(2)}) collective-permute-start(bf16[256,128]{1,0:T(8,128)(2,1)S(1)} %get-tuple-element.42), channel_id=1, source_target_pairs={{0,12},{4,0},{8,4},{12,8},{1,13},{5,1},{9,5},{13,9},{2,14},{6,2},{... | collective-permute-start | bytes 196616 | tf_op jit(solution)/shard_map/ppermute | solution.py:21
  25.0 0.0 collective-permute-done.10.refs_2_
  25.0 0.0 collective-permute-done.11.refs_3_
  25.0 0.0 copy-done
  25.1 0.8 %gate0.1.refs_4_ = bf16[256,1024]{1,0:T(8,128)(2,1)} custom-call(bf16[256,1024]{1,0:T(8,128)(2,1)S(1)} %copy-done, bf16[256,128]{1,0:T(8,128)(2,1)S(1)} %get-tuple-element.47.refs_0_, bf16[256,128]{1,0:T(8,128)(2,1)S(1)} %collective-permute-done.9.refs_1_, bf16[256,128]{1,0:T(8,128)(2,1)S(1)} %collective-permute-done.10.refs_2_, ...), custom_call_target="tpu_custom_call" | custom-call | tf_op jit(solution)/shard_map/gate0/pallas_call | solution.py:196
  25.8 1.5 %collective-permute-done.3.refs_1_ = bf16[256,128]{1,0:T(8,128)(2,1)S(1)} collective-permute-done((bf16[256,128]{1,0:T(8,128)(2,1)S(1)}, bf16[256,128]{1,0:T(8,128)(2,1)S(1)}, u32[]{:S(2)}, u32[]{:S(2)}) %collective-permute-start.3) | collective-permute-done | bytes 65568 | tf_op jit(solution)/shard_map/ppermute | solution.py:21
  27.3 0.0 collective-permute-done.4.refs_2_
  27.3 0.7 %collective-permute-done.5.refs_3_ = bf16[256,128]{1,0:T(8,128)(2,1)S(1)} collective-permute-done((bf16[256,128]{1,0:T(8,128)(2,1)S(1)}, bf16[256,128]{1,0:T(8,128)(2,1)S(1)}, u32[]{:S(2)}, u32[]{:S(2)}) %collective-permute-start.5) | collective-permute-done | bytes 65568 | tf_op jit(solution)/shard_map/ppermute | solution.py:21
  28.0 0.8 %gate1.1 = bf16[256,1024]{1,0:T(8,128)(2,1)} custom-call(bf16[256,1024]{1,0:T(8,128)(2,1)S(1)} %copy-done, bf16[256,128]{1,0:T(8,128)(2,1)S(1)} %get-tuple-element.39.refs_0_, bf16[256,128]{1,0:T(8,128)(2,1)S(1)} %collective-permute-done.3.refs_1_, bf16[256,128]{1,0:T(8,128)(2,1)S(1)} %collective-permute-done.4.refs_2_, ...), custom_call_target="tpu_custom_call", output_to_operand_aliasing={{}: (5, {})} | custom-call | tf_op jit(solution)/shard_map/gate1/pallas_call | solution.py:196
Async XLA Ops:
  1.2 9.0 %collective-permute-start.6 = (bf16[256,128]{1,0:T(8,128)(2,1)S(1)}, bf16[256,128]{1,0:T(8,128)(2,1)S(1)}, u32[]{:S(2)}, u32[]{:S(2)}) collective-permute-start(bf16[256,128]{1,0:T(8,128)(2,1)S(1)} %get-tuple-element.44), channel_id=1, source_target_pairs={{0,8},{4,12},{8,0},{12,4},{1,9},{5,13},{9,1},{13,5},{2,10},{6,14},... | collective-permute-start | bytes 196616 | tf_op jit(solution)/shard_map/ppermute | solution.py:21
  5.3 8.2 %collective-permute-start.7 = (bf16[256,128]{1,0:T(8,128)(2,1)S(1)}, bf16[256,128]{1,0:T(8,128)(2,1)S(1)}, u32[]{:S(2)}, u32[]{:S(2)}) collective-permute-start(bf16[256,128]{1,0:T(8,128)(2,1)S(1)} %get-tuple-element.45), channel_id=1, source_target_pairs={{0,4},{4,8},{8,12},{12,0},{1,5},{5,9},{9,13},{13,1},{2,6},{6,10},{... | collective-permute-start | bytes 196616 | tf_op jit(solution)/shard_map/ppermute | solution.py:21
  6.9 6.7 %collective-permute-start.8 = (bf16[256,128]{1,0:T(8,128)(2,1)S(1)}, bf16[256,128]{1,0:T(8,128)(2,1)S(1)}, u32[]{:S(2)}, u32[]{:S(2)}) collective-permute-start(bf16[256,128]{1,0:T(8,128)(2,1)S(1)} %get-tuple-element.46), channel_id=1, source_target_pairs={{0,12},{4,0},{8,4},{12,8},{1,13},{5,1},{9,5},{13,9},{2,14},{6,2},{... | collective-permute-start | bytes 196616 | tf_op jit(solution)/shard_map/ppermute | solution.py:21
  9.1 8.1 %collective-permute-start = (bf16[256,128]{1,0:T(8,128)(2,1)S(1)}, bf16[256,128]{1,0:T(8,128)(2,1)S(1)}, u32[]{:S(2)}, u32[]{:S(2)}) collective-permute-start(bf16[256,128]{1,0:T(8,128)(2,1)S(1)} %get-tuple-element.29), channel_id=1, source_target_pairs={{0,8},{4,12},{8,0},{12,4},{1,9},{5,13},{9,1},{13,5},{2,10},{6,14},... | collective-permute-start | bytes 196616 | tf_op jit(solution)/shard_map/ppermute | solution.py:21
  9.1 11.3 %collective-permute-start.1 = (bf16[256,128]{1,0:T(8,128)(2,1)S(1)}, bf16[256,128]{1,0:T(8,128)(2,1)S(1)}, u32[]{:S(2)}, u32[]{:S(2)}) collective-permute-start(bf16[256,128]{1,0:T(8,128)(2,1)S(1)} %get-tuple-element.30), channel_id=1, source_target_pairs={{0,4},{4,8},{8,12},{12,0},{1,5},{5,9},{9,13},{13,1},{2,6},{6,10},{... | collective-permute-start | bytes 196616 | tf_op jit(solution)/shard_map/ppermute | solution.py:21
  10.2 10.2 %collective-permute-start.2 = (bf16[256,128]{1,0:T(8,128)(2,1)S(1)}, bf16[256,128]{1,0:T(8,128)(2,1)S(1)}, u32[]{:S(2)}, u32[]{:S(2)}) collective-permute-start(bf16[256,128]{1,0:T(8,128)(2,1)S(1)} %get-tuple-element.31), channel_id=1, source_target_pairs={{0,12},{4,0},{8,4},{12,8},{1,13},{5,1},{9,5},{13,9},{2,14},{6,2},{... | collective-permute-start | bytes 196616 | tf_op jit(solution)/shard_map/ppermute | solution.py:21
  14.2 7.6 %collective-permute-start.9 = (bf16[256,128]{1,0:T(8,128)(2,1)S(1)}, bf16[256,128]{1,0:T(8,128)(2,1)S(1)}, u32[]{:S(2)}, u32[]{:S(2)}) collective-permute-start(bf16[256,128]{1,0:T(8,128)(2,1)S(1)} %get-tuple-element.48), channel_id=1, source_target_pairs={{0,4},{4,8},{8,12},{12,0},{1,5},{5,9},{9,13},{13,1},{2,6},{6,10},{... | collective-permute-start | bytes 196616 | tf_op jit(solution)/shard_map/ppermute | solution.py:21
  14.8 10.3 %collective-permute-start.10 = (bf16[256,128]{1,0:T(8,128)(2,1)S(1)}, bf16[256,128]{1,0:T(8,128)(2,1)S(1)}, u32[]{:S(2)}, u32[]{:S(2)}) collective-permute-start(bf16[256,128]{1,0:T(8,128)(2,1)S(1)} %get-tuple-element.49), channel_id=1, source_target_pairs={{0,8},{4,12},{8,0},{12,4},{1,9},{5,13},{9,1},{13,5},{2,10},{6,14},... | collective-permute-start | bytes 196616 | tf_op jit(solution)/shard_map/ppermute | solution.py:21
  17.2 7.9 %collective-permute-start.11 = (bf16[256,128]{1,0:T(8,128)(2,1)S(1)}, bf16[256,128]{1,0:T(8,128)(2,1)S(1)}, u32[]{:S(2)}, u32[]{:S(2)}) collective-permute-start(bf16[256,128]{1,0:T(8,128)(2,1)S(1)} %get-tuple-element.50), channel_id=1, source_target_pairs={{0,12},{4,0},{8,4},{12,8},{1,13},{5,1},{9,5},{13,9},{2,14},{6,2},{... | collective-permute-start | bytes 196616 | tf_op jit(solution)/shard_map/ppermute | solution.py:21
  20.4 4.6 %copy-start = (bf16[256,1024]{1,0:T(8,128)(2,1)S(1)}, bf16[256,1024]{1,0:T(8,128)(2,1)}, u32[]{:S(2)}) copy-start(bf16[256,1024]{1,0:T(8,128)(2,1)} %gate_ref.3) | copy-start | bytes 1572868
  21.2 6.1 %collective-permute-start.3 = (bf16[256,128]{1,0:T(8,128)(2,1)S(1)}, bf16[256,128]{1,0:T(8,128)(2,1)S(1)}, u32[]{:S(2)}, u32[]{:S(2)}) collective-permute-start(bf16[256,128]{1,0:T(8,128)(2,1)S(1)} %get-tuple-element.40), channel_id=1, source_target_pairs={{0,4},{4,8},{8,12},{12,0},{1,5},{5,9},{9,13},{13,1},{2,6},{6,10},{... | collective-permute-start | bytes 196616 | tf_op jit(solution)/shard_map/ppermute | solution.py:21
  21.2 6.1 %collective-permute-start.4 = (bf16[256,128]{1,0:T(8,128)(2,1)S(1)}, bf16[256,128]{1,0:T(8,128)(2,1)S(1)}, u32[]{:S(2)}, u32[]{:S(2)}) collective-permute-start(bf16[256,128]{1,0:T(8,128)(2,1)S(1)} %get-tuple-element.41), channel_id=1, source_target_pairs={{0,8},{4,12},{8,0},{12,4},{1,9},{5,13},{9,1},{13,5},{2,10},{6,14},... | collective-permute-start | bytes 196616 | tf_op jit(solution)/shard_map/ppermute | solution.py:21
  21.8 6.2 %collective-permute-start.5 = (bf16[256,128]{1,0:T(8,128)(2,1)S(1)}, bf16[256,128]{1,0:T(8,128)(2,1)S(1)}, u32[]{:S(2)}, u32[]{:S(2)}) collective-permute-start(bf16[256,128]{1,0:T(8,128)(2,1)S(1)} %get-tuple-element.42), channel_id=1, source_target_pairs={{0,12},{4,0},{8,4},{12,8},{1,13},{5,1},{9,5},{13,9},{2,14},{6,2},{... | collective-permute-start | bytes 196616 | tf_op jit(solution)/shard_map/ppermute | solution.py:21

commit v5 on v2

--- a/solution.py
+++ b/solution.py
@@ -8,7 +8,7 @@
 from jax.sharding import PartitionSpec as P
 
 F32, BF16 = jnp.float32, jnp.bfloat16
-VMEM, SMEM = pltpu.VMEM, pltpu.SMEM
+VMEM = pltpu.VMEM
 
 
 def shifted(array, by):
@@ -25,38 +25,61 @@
     return pltpu.with_memory_space_constraint(array, VMEM)
 
 
-def build_kernel(rows, lags, owned, filters_ref, lengths_ref, gain_ref, perm_ref, fwd_ref, bwd_ref, gains_ref):
+def rounds(count):
+    if count == 4:
+        return (2, 1, 3), (1, 2, 3)
+    return (tuple(range(1, count)),) * 2
+
+
+def lanes(by, own, count, owned, group_w):
+    block = lax.rem(lax.axis_index("ctx") + by, count)
+    return pl.ds(pl.multiple_of((block * owned + own) * group_w, group_w), group_w)
+
+
+def build_kernel(rows, lags, owned, owns, filters_ref, lengths_ref, gain_ref, perm_ref, fwd_ref, bwd_ref, gains_ref):
     first = lax.axis_index("ctx") * owned
     group_w = perm_ref.shape[1]
     taps = filters_ref.shape[1]
     span = lags * rows
     target = lax.broadcasted_iota(jnp.int32, (group_w, group_w), 0)
     match = perm_ref[...] == target
-    for own in range(owned):
+    group_ids = lax.broadcasted_iota(jnp.int32, lengths_ref.shape, 1)
+    tap_ids = lax.broadcasted_iota(jnp.int32, (1, taps), 1)
+    for at, own in enumerate(owns):
         group = first + own
-        taps_row = filters_ref[pl.ds(group, 1), :]
-        tap_ids = lax.broadcasted_iota(jnp.int32, (1, taps), 1)
-        taps_row = jnp.where(tap_ids < lengths_ref[group] * rows, taps_row, 0.0)
+        length = jnp.sum(jnp.where(group_ids == group, lengths_ref[...], 0), axis=1, keepdims=True)
+        taps_row = jnp.where(tap_ids < length * rows, filters_ref[pl.ds(group, 1), :], 0.0)
         taps_row = jnp.concatenate([taps_row, jnp.zeros((1, span - taps), F32)], axis=1)
         strip = pltpu.roll(jnp.broadcast_to(taps_row, (rows, span)), 0, 1, stride=1, stride_axis=0)
         for lag in range(lags):
             block = strip[:, lag * rows : (lag + 1) * rows]
-            bwd_ref[own, lag] = block.astype(BF16)
-            fwd_ref[own, lag] = block.T.astype(BF16)
+            bwd_ref[at, lag] = block.astype(BF16)
+            fwd_ref[at, lag] = block.T.astype(BF16)
         gain_row = gain_ref[pl.ds(group, 1), :]
         spread = jnp.where(match, gain_row, 0.0)
-        gains_ref[own, 0:1, :] = gain_row
-        gains_ref[own, 1:2, :] = jnp.sum(spread.T, axis=0, keepdims=True)
-
-
-def mix_kernel(count, lags, own, *refs):
+        gains_ref[at, 0:1, :] = gain_row
+        gains_ref[at, 1:2, :] = jnp.sum(spread.T, axis=0, keepdims=True)
+
+
+def deal_kernel(count, owned, group_w, messages, x_ref, *refs):
+    sems = refs[-1]
+    small = (len(refs) - 1 - len(messages)) // 2
+    outs = refs[small:-1]
+    sources = [x_ref.at[:, lanes(by, own, count, owned, group_w)] for own, by in messages] + list(refs[:small])
+    copies = [pltpu.make_async_copy(source, outs[i], sems.at[i]) for i, source in enumerate(sources)]
+    for copy in copies:
+        copy.start()
+    for copy in copies:
+        copy.wait()
+
+
+def mix_kernel(count, lags, own, out_order, back_order, *refs):
     blocks, (fwd_ref, bwd_ref, gains_ref) = refs[:count], refs[count : count + 3]
     outs, (inputs, sums) = refs[count + 3 : 2 * count + 3], refs[2 * count + 3 :]
     me = lax.axis_index("ctx")
     group_w = gains_ref.shape[2]
-    places = [lax.rem(me - k + count, count) for k in range(count)]
-    for k in range(count):
-        inputs[places[k]] = blocks[k][...]
+    for block, by in zip(blocks, (0, *out_order)):
+        inputs[lax.rem(me - by + count, count)] = block[...]
     values = jnp.concatenate([inputs[i] for i in range(count)], axis=1).astype(F32)
     gated = (values * jnp.tile(gains_ref[own, 0:1, :], (1, count))).astype(BF16)
     flipped = (values * jnp.tile(gains_ref[own, 1:2, :], (1, count))).astype(BF16)
@@ -76,21 +99,19 @@
             add(behind, i, down[:, piece])
     for i in range(count):
         sums[i] = (ahead[i] + behind[i].astype(BF16).astype(F32)).astype(BF16)
-    for k in range(count):
-        outs[k][...] = sums[places[k]]
-
-
-def gate_kernel(count, owned, own, gate_ref, *refs):
+    for out, by in zip(outs, (0, *back_order)):
+        out[...] = sums[lax.rem(me + by, count)]
+
+
+def gate_kernel(count, owned, own, back_order, gate_ref, *refs):
     blocks, out_ref, (pieces, sems) = refs[:count], refs[-3], refs[-2:]
-    me = lax.axis_index("ctx")
     group_w = blocks[0].shape[1]
     copies = []
-    for k in range(count):
-        at = (lax.rem(me + k, count) * owned + own) * group_w
-        place = pl.ds(pl.multiple_of(at, group_w), group_w)
-        pieces[k] = (gate_ref[:, place].astype(F32) * blocks[k][...].astype(F32)).astype(BF16)
-        copies.append(pltpu.make_async_copy(pieces.at[k], out_ref.at[:, place], sems.at[k]))
-        copies[k].start()
+    for i, by in enumerate((0, *back_order)):
+        place = lanes(count - by, own, count, owned, group_w)
+        pieces[i] = (gate_ref[:, place].astype(F32) * blocks[i][...].astype(F32)).astype(BF16)
+        copies.append(pltpu.make_async_copy(pieces.at[i], out_ref.at[:, place], sems.at[i]))
+        copies[i].start()
     for copy in copies:
         copy.wait()
 
@@ -102,47 +123,68 @@
     group_w = permutation.shape[0]
     owned = groups_dev // count
     lags = taps // rows + 1
-    me = lax.axis_index("ctx")
+    out_order, back_order = rounds(count)
     vmem, anywhere = pl.BlockSpec(memory_space=VMEM), pl.BlockSpec(memory_space=pl.ANY)
-
-    def part(k, own):
-        group = lax.rem(me + k, count) * owned + own
-        return lax.dynamic_slice(sequence, (0, group * group_w), (rows, group_w))
-
-    def deal(own):
-        return [part(0, own)] + [rotated(part(k, own), k) for k in range(1, count)]
-
-    blocks = [deal(own) for own in range(owned)]
-    toeplitz = pl.pallas_call(
-        functools.partial(build_kernel, rows, lags, owned),
-        in_specs=[vmem, pl.BlockSpec(memory_space=SMEM), vmem, vmem],
+    params = pltpu.CompilerParams(vmem_limit_bytes=24 << 20)
+    dma = pltpu.SemaphoreType.DMA
+
+    small = [
+        filters,
+        lengths.reshape(1, groups_dev),
+        gain.reshape(groups_dev, group_w),
+        permutation.reshape(1, group_w),
+    ]
+    small = [pltpu.with_memory_space_constraint(array, pltpu.HBM) for array in small]
+    messages = [(own, by) for own in range(owned) for by in out_order] + [(own, 0) for own in range(owned)]
+    sent = {}
+    for part, source, extra in (
+        (messages[:1], pltpu.with_memory_space_constraint(sequence, pltpu.HBM), small),
+        (messages[1:], sequence, []),
+    ):
+        copied = pl.pallas_call(
+            functools.partial(deal_kernel, count, owned, group_w, part),
+            in_specs=[anywhere] * (1 + len(extra)),
+            out_specs=[vmem] * (len(part) + len(extra)),
+            out_shape=[VMEM((rows, group_w), BF16) for _ in part] + [VMEM(array.shape, array.dtype) for array in extra],
+            scratch_shapes=[dma((len(part) + len(extra),))],
+            compiler_params=params,
+            name="deal",
+        )(source, *extra)
+        sent.update({(own, by): rotated(array, by) if by else array for (own, by), array in zip(part, copied)})
+        small = copied[len(part) :] if extra else small
+    built = pl.pallas_call(
+        functools.partial(build_kernel, rows, lags, owned, tuple(range(owned))),
+        in_specs=[vmem] * 4,
         out_specs=[vmem] * 3,
         out_shape=[VMEM((owned, lags, rows, rows), BF16)] * 2 + [VMEM((owned, 8, group_w), F32)],
+        compiler_params=params,
         name="build",
-    )(filters, lengths, gain.reshape(groups_dev, group_w), permutation.reshape(1, group_w))
+    )(*map(held, small))
     back = []
     for own in range(owned):
         outs = pl.pallas_call(
-            functools.partial(mix_kernel, count, lags, own),
+            functools.partial(mix_kernel, count, lags, own, out_order, back_order),
             in_specs=[vmem] * (count + 3),
             out_specs=[vmem] * count,
             out_shape=[VMEM((rows, group_w), BF16)] * count,
             scratch_shapes=[VMEM((count, rows, group_w), BF16)] * 2,
-            name=f"mix{own}",
-        )(*map(held, [*blocks[own], *toeplitz]))
-        back.append([outs[0]] + [rotated(outs[k], -k) for k in range(1, count)])
+            compiler_params=params,
+            name="mix",
+        )(*map(held, [*[sent[own, by] for by in (0, *out_order)], *built]))
+        back.append([rotated(array, by) if by else array for by, array in zip((0, *back_order), outs)])
     gate = held(gate)
     out = []
     for own in range(owned):
         out = [
             pl.pallas_call(
-                functools.partial(gate_kernel, count, owned, own),
+                functools.partial(gate_kernel, count, owned, own, back_order),
                 in_specs=[vmem] * (count + 1) + [anywhere] * len(out),
                 out_specs=anywhere,
                 out_shape=jax.ShapeDtypeStruct((rows, width), BF16),
-                scratch_shapes=[VMEM((count, rows, group_w), BF16), pltpu.SemaphoreType.DMA((count,))],
+                scratch_shapes=[VMEM((count, rows, group_w), BF16), dma((count,))],
                 input_output_aliases={count + 1: 0} if out else {},
-                name=f"gate{own}",
+                compiler_params=params,
+                name="gate",
             )(gate, *map(held, back[own]), *out)
         ]
     return out[0]

time: 33.6 us -> 28.6 us (0.85)
  waiting for transfers between devices: 6.88 us -> 2.47 us
  starting transfers between devices: 19.9 us -> 21.3 us
  local copies, waits for them, and re-layouts: 1.11 us -> 0.01 us
  Pallas kernels: 5.39 us -> 4.6 us
    ppermute x12, waiting for transfers between devices: 6.88 us -> 2.47 us  [rotated(): lax.ppermute(array, 'ctx', [(i, (i + by) % count) for i in range(count)])]
    ppermute x12, starting transfers between devices: 19.9 us -> 21.3 us  [rotated(): lax.ppermute(array, 'ctx', [(i, (i + by) % count) for i in range(count)])]
    dynamic_slice x1 -> x0, local copies, waits for them, and re-layouts: 1.11 us -> none  [part(): return lax.dynamic_slice(sequence, (0, group * group_w), (rows, group_w))]
    pallas_call x5 -> x7, Pallas kernels: 5.39 us -> 4.6 us  [the longest x2 1.53 us: dealt(): pl.pallas_call(functools.partial(gate_kernel, count, owned, own, back_ord...]
  transfers between devices with their start and end apart: 12 -> 12, of which waited for: 4 -> 2; matrix products, arithmetic and copies ran while one was open for 0% -> 0% of each run, Pallas kernels for 14% -> 10%
where the time goes in v5:
time: 28.6 us; the launch traced here: 28.5 us
  starting transfers between devices  21.3 us (74%)
  Pallas kernels  4.6 us (16%)
  waiting for transfers between devices  2.47 us (9%)
    ppermute x12, starting transfers between devices, rotated(): lax.ppermute(array, 'ctx', [(i, (i + by) % count) for i in range(count)])  21.3 us
    ppermute x12, waiting for transfers between devices, rotated(): lax.ppermute(array, 'ctx', [(i, (i + by) % count) for i in range(count)])  2.47 us
    pallas_call x2, Pallas kernels, dealt(): pl.pallas_call(functools.partial(gate_kernel, count, owned, own, back_ord...  1.53 us
    pallas_call x2, Pallas kernels, dealt(): pl.pallas_call(functools.partial(mix_kernel, count, lags, own, out_order,...  1.4 us
    pallas_call x2, Pallas kernels, dealt(): pl.pallas_call(functools.partial(deal_kernel, count, owned, group_w, part...  1.16 us
  transfers between devices with their start and end apart: 12, of which 2 were waited for; matrix products, arithmetic and copies ran while one was open for 0% of the time, Pallas kernels for 10%

profile of v5, /device:TPU:0, one launch (start us, length us, event | category | flops | bytes accessed | tf_op | source)
XLA Modules:
  0.0 28.5 jit_solution(6402377271733113631)
XLA Ops:
  0.0 1.0 %deal.3 = (bf16[256,128]{1,0:T(8,128)(2,1)S(1)}, f32[8,768]{1,0:T(8,128)S(1)}, s32[1,8]{1,0:T(1,128)S(1)}, f32[8,128]{1,0:T(8,128)S(1)}, s32[1,128]{1,0:T(1,128)S(1)}) custom-call(bf16[256,1024]{1,0:T(8,128)(2,1)} %x_ref.3, f32[8,768]{1,0:T(8,128)} %refs_0_.1, s32[1,8]{1,0:T(1,128)} %bitcast.4, f32[8,128]{1,0:T(8,128)} %bitcast.3, s32[1,128]{1,0:T(1,128)} %bitcast.5), custom_call_target="tpu_custom_call" | custom-call | tf_op jit(solution)/shard_map/deal/pallas_call | solution.py:144
  1.0 4.1 %collective-permute-start.6 = (bf16[256,128]{1,0:T(8,128)(2,1)S(1)}, bf16[256,128]{1,0:T(8,128)(2,1)S(1)}, u32[]{:S(2)}, u32[]{:S(2)}) collective-permute-start(bf16[256,128]{1,0:T(8,128)(2,1)S(1)} %get-tuple-element.44), channel_id=1, source_target_pairs={{0,8},{4,12},{8,0},{12,4},{1,9},{5,13},{9,1},{13,5},{2,10},{6,14},... | collective-permute-start | bytes 196616 | tf_op jit(solution)/shard_map/ppermute | solution.py:21
  5.1 0.2 deal.2
  5.3 1.6 %collective-permute-start.7 = (bf16[256,128]{1,0:T(8,128)(2,1)S(1)}, bf16[256,128]{1,0:T(8,128)(2,1)S(1)}, u32[]{:S(2)}, u32[]{:S(2)}) collective-permute-start(bf16[256,128]{1,0:T(8,128)(2,1)S(1)} %get-tuple-element.45), channel_id=1, source_target_pairs={{0,4},{4,8},{8,12},{12,0},{1,5},{5,9},{9,13},{13,1},{2,6},{6,10},{... | collective-permute-start | bytes 196616 | tf_op jit(solution)/shard_map/ppermute | solution.py:21
  6.9 2.2 %collective-permute-start.8 = (bf16[256,128]{1,0:T(8,128)(2,1)S(1)}, bf16[256,128]{1,0:T(8,128)(2,1)S(1)}, u32[]{:S(2)}, u32[]{:S(2)}) collective-permute-start(bf16[256,128]{1,0:T(8,128)(2,1)S(1)} %get-tuple-element.46), channel_id=1, source_target_pairs={{0,12},{4,0},{8,4},{12,8},{1,13},{5,1},{9,5},{13,9},{2,14},{6,2},{... | collective-permute-start | bytes 196616 | tf_op jit(solution)/shard_map/ppermute | solution.py:21
  9.2 0.0 collective-permute-start
  9.2 0.6 %collective-permute-start.1 = (bf16[256,128]{1,0:T(8,128)(2,1)S(1)}, bf16[256,128]{1,0:T(8,128)(2,1)S(1)}, u32[]{:S(2)}, u32[]{:S(2)}) collective-permute-start(bf16[256,128]{1,0:T(8,128)(2,1)S(1)} %get-tuple-element.30), channel_id=1, source_target_pairs={{0,4},{4,8},{8,12},{12,0},{1,5},{5,9},{9,13},{13,1},{2,6},{6,10},{... | collective-permute-start | bytes 196616 | tf_op jit(solution)/shard_map/ppermute | solution.py:21
  9.7 0.5 %build.1 = (bf16[2,4,256,256]{3,2,1,0:T(8,128)(2,1)S(1)}, bf16[2,4,256,256]{3,2,1,0:T(8,128)(2,1)S(1)}, f32[2,8,128]{2,1,0:T(8,128)S(1)}) custom-call(f32[8,768]{1,0:T(8,128)S(1)} %get-tuple-element.32.filters_ref, s32[1,8]{1,0:T(1,128)S(1)} %get-tuple-element.33.lengths_ref, f32[8,128]{1,0:T(8,128)S(1)} %get-tuple-element.34.gain_ref, ...), custom_call_target="tpu_custom_call" | custom-call | tf_op jit(solution)/shard_map/build/pallas_call | solution.py:155
  10.2 0.0 collective-permute-done.6.refs_1_
  10.3 3.3 %collective-permute-start.2 = (bf16[256,128]{1,0:T(8,128)(2,1)S(1)}, bf16[256,128]{1,0:T(8,128)(2,1)S(1)}, u32[]{:S(2)}, u32[]{:S(2)}) collective-permute-start(bf16[256,128]{1,0:T(8,128)(2,1)S(1)} %get-tuple-element.31), channel_id=1, source_target_pairs={{0,12},{4,0},{8,4},{12,8},{1,13},{5,1},{9,5},{13,9},{2,14},{6,2},{... | collective-permute-start | bytes 196616 | tf_op jit(solution)/shard_map/ppermute | solution.py:21
  13.6 0.0 collective-permute-done.7.refs_2_
  13.6 0.0 collective-permute-done.8.refs_3_
  13.6 0.7 %mix.3 = (bf16[256,128]{1,0:T(8,128)(2,1)S(1)}, bf16[256,128]{1,0:T(8,128)(2,1)S(1)}, bf16[256,128]{1,0:T(8,128)(2,1)S(1)}, bf16[256,128]{1,0:T(8,128)(2,1)S(1)}) custom-call(bf16[256,128]{1,0:T(8,128)(2,1)S(1)} %get-tuple-element.43.refs_0_, bf16[256,128]{1,0:T(8,128)(2,1)S(1)} %collective-permute-done.6.refs_1_, ...), custom_call_target="tpu_custom_call" | custom-call | tf_op jit(solution)/shard_map/mix/pallas_call | solution.py:165
  14.3 0.1 collective-permute-start.9
  14.3 2.8 %collective-permute-start.10 = (bf16[256,128]{1,0:T(8,128)(2,1)S(1)}, bf16[256,128]{1,0:T(8,128)(2,1)S(1)}, u32[]{:S(2)}, u32[]{:S(2)}) collective-permute-start(bf16[256,128]{1,0:T(8,128)(2,1)S(1)} %get-tuple-element.49), channel_id=1, source_target_pairs={{0,8},{4,12},{8,0},{12,4},{1,9},{5,13},{9,1},{13,5},{2,10},{6,14},... | collective-permute-start | bytes 196616 | tf_op jit(solution)/shard_map/ppermute | solution.py:21
  17.1 0.0 collective-permute-done.refs_1_
  17.1 2.4 %collective-permute-start.11 = (bf16[256,128]{1,0:T(8,128)(2,1)S(1)}, bf16[256,128]{1,0:T(8,128)(2,1)S(1)}, u32[]{:S(2)}, u32[]{:S(2)}) collective-permute-start(bf16[256,128]{1,0:T(8,128)(2,1)S(1)} %get-tuple-element.50), channel_id=1, source_target_pairs={{0,12},{4,0},{8,4},{12,8},{1,13},{5,1},{9,5},{13,9},{2,14},{6,2},{... | collective-permute-start | bytes 196616 | tf_op jit(solution)/shard_map/ppermute | solution.py:21
  19.6 0.0 collective-permute-done.1.refs_2_
  19.6 0.0 collective-permute-done.2.refs_3_
  19.6 0.7 %mix.2 = (bf16[256,128]{1,0:T(8,128)(2,1)S(1)}, bf16[256,128]{1,0:T(8,128)(2,1)S(1)}, bf16[256,128]{1,0:T(8,128)(2,1)S(1)}, bf16[256,128]{1,0:T(8,128)(2,1)S(1)}) custom-call(bf16[256,128]{1,0:T(8,128)(2,1)S(1)} %get-tuple-element.28.refs_0_, bf16[256,128]{1,0:T(8,128)(2,1)S(1)} %collective-permute-done.refs_1_, ...), custom_call_target="tpu_custom_call" | custom-call | tf_op jit(solution)/shard_map/mix/pallas_call | solution.py:165
  20.3 0.3 collective-permute-start.3
  20.5 1.2 %collective-permute-start.4 = (bf16[256,128]{1,0:T(8,128)(2,1)S(1)}, bf16[256,128]{1,0:T(8,128)(2,1)S(1)}, u32[]{:S(2)}, u32[]{:S(2)}) collective-permute-start(bf16[256,128]{1,0:T(8,128)(2,1)S(1)} %get-tuple-element.41), channel_id=1, source_target_pairs={{0,8},{4,12},{8,0},{12,4},{1,9},{5,13},{9,1},{13,5},{2,10},{6,14},... | collective-permute-start | bytes 196616 | tf_op jit(solution)/shard_map/ppermute | solution.py:21
  21.7 0.0 collective-permute-done.9.refs_1_
  21.7 2.8 %collective-permute-start.5 = (bf16[256,128]{1,0:T(8,128)(2,1)S(1)}, bf16[256,128]{1,0:T(8,128)(2,1)S(1)}, u32[]{:S(2)}, u32[]{:S(2)}) collective-permute-start(bf16[256,128]{1,0:T(8,128)(2,1)S(1)} %get-tuple-element.42), channel_id=1, source_target_pairs={{0,12},{4,0},{8,4},{12,8},{1,13},{5,1},{9,5},{13,9},{2,14},{6,2},{... | collective-permute-start | bytes 196616 | tf_op jit(solution)/shard_map/ppermute | solution.py:21
  24.5 0.0 collective-permute-done.10.refs_2_
  24.5 0.0 collective-permute-done.11.refs_3_
  24.5 0.0 copy-done
  24.5 0.8 %gate.2.refs_4_ = bf16[256,1024]{1,0:T(8,128)(2,1)} custom-call(bf16[256,1024]{1,0:T(8,128)(2,1)S(1)} %copy-done, bf16[256,128]{1,0:T(8,128)(2,1)S(1)} %get-tuple-element.47.refs_0_, bf16[256,128]{1,0:T(8,128)(2,1)S(1)} %collective-permute-done.9.refs_1_, bf16[256,128]{1,0:T(8,128)(2,1)S(1)} %collective-permute-done.10.refs_2_, ...), custom_call_target="tpu_custom_call" | custom-call | tf_op jit(solution)/shard_map/gate/pallas_call | solution.py:179
  25.2 1.3 %collective-permute-done.3.refs_1_ = bf16[256,128]{1,0:T(8,128)(2,1)S(1)} collective-permute-done((bf16[256,128]{1,0:T(8,128)(2,1)S(1)}, bf16[256,128]{1,0:T(8,128)(2,1)S(1)}, u32[]{:S(2)}, u32[]{:S(2)}) %collective-permute-start.3) | collective-permute-done | bytes 65568 | tf_op jit(solution)/shard_map/ppermute | solution.py:21
  26.5 1.2 %collective-permute-done.4.refs_2_ = bf16[256,128]{1,0:T(8,128)(2,1)S(1)} collective-permute-done((bf16[256,128]{1,0:T(8,128)(2,1)S(1)}, bf16[256,128]{1,0:T(8,128)(2,1)S(1)}, u32[]{:S(2)}, u32[]{:S(2)}) %collective-permute-start.4) | collective-permute-done | bytes 65568 | tf_op jit(solution)/shard_map/ppermute | solution.py:21
  27.7 0.0 collective-permute-done.5.refs_3_
  27.7 0.8 %gate.3 = bf16[256,1024]{1,0:T(8,128)(2,1)} custom-call(bf16[256,1024]{1,0:T(8,128)(2,1)S(1)} %copy-done, bf16[256,128]{1,0:T(8,128)(2,1)S(1)} %get-tuple-element.39.refs_0_, bf16[256,128]{1,0:T(8,128)(2,1)S(1)} %collective-permute-done.3.refs_1_, bf16[256,128]{1,0:T(8,128)(2,1)S(1)} %collective-permute-done.4.refs_2_, ...), custom_call_target="tpu_custom_call", output_to_operand_aliasing={{}: (5, {})} | custom-call | tf_op jit(solution)/shard_map/gate/pallas_call | solution.py:179
  (3 shorter events, 0.0 us)
Async XLA Ops:
  0.0 5.1 %copy-start.1 = (bf16[256,1024]{1,0:T(8,128)(2,1)S(1)}, bf16[256,1024]{1,0:T(8,128)(2,1)}, u32[]{:S(2)}) copy-start(bf16[256,1024]{1,0:T(8,128)(2,1)} %x_ref.3) | copy-start | bytes 1572868
  1.0 9.3 %collective-permute-start.6 = (bf16[256,128]{1,0:T(8,128)(2,1)S(1)}, bf16[256,128]{1,0:T(8,128)(2,1)S(1)}, u32[]{:S(2)}, u32[]{:S(2)}) collective-permute-start(bf16[256,128]{1,0:T(8,128)(2,1)S(1)} %get-tuple-element.44), channel_id=1, source_target_pairs={{0,8},{4,12},{8,0},{12,4},{1,9},{5,13},{9,1},{13,5},{2,10},{6,14},... | collective-permute-start | bytes 196616 | tf_op jit(solution)/shard_map/ppermute | solution.py:21
  5.3 8.3 %collective-permute-start.7 = (bf16[256,128]{1,0:T(8,128)(2,1)S(1)}, bf16[256,128]{1,0:T(8,128)(2,1)S(1)}, u32[]{:S(2)}, u32[]{:S(2)}) collective-permute-start(bf16[256,128]{1,0:T(8,128)(2,1)S(1)} %get-tuple-element.45), channel_id=1, source_target_pairs={{0,4},{4,8},{8,12},{12,0},{1,5},{5,9},{9,13},{13,1},{2,6},{6,10},{... | collective-permute-start | bytes 196616 | tf_op jit(solution)/shard_map/ppermute | solution.py:21
  6.9 6.7 %collective-permute-start.8 = (bf16[256,128]{1,0:T(8,128)(2,1)S(1)}, bf16[256,128]{1,0:T(8,128)(2,1)S(1)}, u32[]{:S(2)}, u32[]{:S(2)}) collective-permute-start(bf16[256,128]{1,0:T(8,128)(2,1)S(1)} %get-tuple-element.46), channel_id=1, source_target_pairs={{0,12},{4,0},{8,4},{12,8},{1,13},{5,1},{9,5},{13,9},{2,14},{6,2},{... | collective-permute-start | bytes 196616 | tf_op jit(solution)/shard_map/ppermute | solution.py:21
  9.2 8.0 %collective-permute-start = (bf16[256,128]{1,0:T(8,128)(2,1)S(1)}, bf16[256,128]{1,0:T(8,128)(2,1)S(1)}, u32[]{:S(2)}, u32[]{:S(2)}) collective-permute-start(bf16[256,128]{1,0:T(8,128)(2,1)S(1)} %get-tuple-element.29), channel_id=1, source_target_pairs={{0,8},{4,12},{8,0},{12,4},{1,9},{5,13},{9,1},{13,5},{2,10},{6,14},... | collective-permute-start | bytes 196616 | tf_op jit(solution)/shard_map/ppermute | solution.py:21
  9.2 10.4 %collective-permute-start.1 = (bf16[256,128]{1,0:T(8,128)(2,1)S(1)}, bf16[256,128]{1,0:T(8,128)(2,1)S(1)}, u32[]{:S(2)}, u32[]{:S(2)}) collective-permute-start(bf16[256,128]{1,0:T(8,128)(2,1)S(1)} %get-tuple-element.30), channel_id=1, source_target_pairs={{0,4},{4,8},{8,12},{12,0},{1,5},{5,9},{9,13},{13,1},{2,6},{6,10},{... | collective-permute-start | bytes 196616 | tf_op jit(solution)/shard_map/ppermute | solution.py:21
  10.3 9.3 %collective-permute-start.2 = (bf16[256,128]{1,0:T(8,128)(2,1)S(1)}, bf16[256,128]{1,0:T(8,128)(2,1)S(1)}, u32[]{:S(2)}, u32[]{:S(2)}) collective-permute-start(bf16[256,128]{1,0:T(8,128)(2,1)S(1)} %get-tuple-element.31), channel_id=1, source_target_pairs={{0,12},{4,0},{8,4},{12,8},{1,13},{5,1},{9,5},{13,9},{2,14},{6,2},{... | collective-permute-start | bytes 196616 | tf_op jit(solution)/shard_map/ppermute | solution.py:21
  14.3 7.4 %collective-permute-start.9 = (bf16[256,128]{1,0:T(8,128)(2,1)S(1)}, bf16[256,128]{1,0:T(8,128)(2,1)S(1)}, u32[]{:S(2)}, u32[]{:S(2)}) collective-permute-start(bf16[256,128]{1,0:T(8,128)(2,1)S(1)} %get-tuple-element.48), channel_id=1, source_target_pairs={{0,4},{4,8},{8,12},{12,0},{1,5},{5,9},{9,13},{13,1},{2,6},{6,10},{... | collective-permute-start | bytes 196616 | tf_op jit(solution)/shard_map/ppermute | solution.py:21
  14.3 10.1 %collective-permute-start.10 = (bf16[256,128]{1,0:T(8,128)(2,1)S(1)}, bf16[256,128]{1,0:T(8,128)(2,1)S(1)}, u32[]{:S(2)}, u32[]{:S(2)}) collective-permute-start(bf16[256,128]{1,0:T(8,128)(2,1)S(1)} %get-tuple-element.49), channel_id=1, source_target_pairs={{0,8},{4,12},{8,0},{12,4},{1,9},{5,13},{9,1},{13,5},{2,10},{6,14},... | collective-permute-start | bytes 196616 | tf_op jit(solution)/shard_map/ppermute | solution.py:21
  17.1 7.3 %collective-permute-start.11 = (bf16[256,128]{1,0:T(8,128)(2,1)S(1)}, bf16[256,128]{1,0:T(8,128)(2,1)S(1)}, u32[]{:S(2)}, u32[]{:S(2)}) collective-permute-start(bf16[256,128]{1,0:T(8,128)(2,1)S(1)} %get-tuple-element.50), channel_id=1, source_target_pairs={{0,12},{4,0},{8,4},{12,8},{1,13},{5,1},{9,5},{13,9},{2,14},{6,2},{... | collective-permute-start | bytes 196616 | tf_op jit(solution)/shard_map/ppermute | solution.py:21
  19.6 4.9 %copy-start = (bf16[256,1024]{1,0:T(8,128)(2,1)S(1)}, bf16[256,1024]{1,0:T(8,128)(2,1)}, u32[]{:S(2)}) copy-start(bf16[256,1024]{1,0:T(8,128)(2,1)} %gate_ref.3) | copy-start | bytes 1572868
  20.3 6.2 %collective-permute-start.3 = (bf16[256,128]{1,0:T(8,128)(2,1)S(1)}, bf16[256,128]{1,0:T(8,128)(2,1)S(1)}, u32[]{:S(2)}, u32[]{:S(2)}) collective-permute-start(bf16[256,128]{1,0:T(8,128)(2,1)S(1)} %get-tuple-element.40), channel_id=1, source_target_pairs={{0,4},{4,8},{8,12},{12,0},{1,5},{5,9},{9,13},{13,1},{2,6},{6,10},{... | collective-permute-start | bytes 196616 | tf_op jit(solution)/shard_map/ppermute | solution.py:21
  20.5 7.2 %collective-permute-start.4 = (bf16[256,128]{1,0:T(8,128)(2,1)S(1)}, bf16[256,128]{1,0:T(8,128)(2,1)S(1)}, u32[]{:S(2)}, u32[]{:S(2)}) collective-permute-start(bf16[256,128]{1,0:T(8,128)(2,1)S(1)} %get-tuple-element.41), channel_id=1, source_target_pairs={{0,8},{4,12},{8,0},{12,4},{1,9},{5,13},{9,1},{13,5},{2,10},{6,14},... | collective-permute-start | bytes 196616 | tf_op jit(solution)/shard_map/ppermute | solution.py:21
  21.7 6.0 %collective-permute-start.5 = (bf16[256,128]{1,0:T(8,128)(2,1)S(1)}, bf16[256,128]{1,0:T(8,128)(2,1)S(1)}, u32[]{:S(2)}, u32[]{:S(2)}) collective-permute-start(bf16[256,128]{1,0:T(8,128)(2,1)S(1)} %get-tuple-element.42), channel_id=1, source_target_pairs={{0,12},{4,0},{8,4},{12,8},{1,13},{5,1},{9,5},{13,9},{2,14},{6,2},{... | collective-permute-start | bytes 196616 | tf_op jit(solution)/shard_map/ppermute | solution.py:21

commit v6 on v5

--- a/solution.py
+++ b/solution.py
@@ -73,16 +73,33 @@
         copy.wait()
 
 
+def deal_build_kernel(count, rows, lags, owned, group_w, messages, x_ref, *refs):
+    small, outs, built, sems = refs[:4], refs[4 : 4 + len(messages)], refs[4 + len(messages) : -1], refs[-1]
+    copies = [
+        pltpu.make_async_copy(x_ref.at[:, lanes(by, own, count, owned, group_w)], outs[i], sems.at[i])
+        for i, (own, by) in enumerate(messages)
+    ]
+    for copy in copies:
+        copy.start()
+    build_kernel(rows, lags, owned, tuple(range(owned)), *small, *built)
+    for copy in copies:
+        copy.wait()
+
+
 def mix_kernel(count, lags, own, out_order, back_order, *refs):
-    blocks, (fwd_ref, bwd_ref, gains_ref) = refs[:count], refs[count : count + 3]
-    outs, (inputs, sums) = refs[count + 3 : 2 * count + 3], refs[2 * count + 3 :]
-    me = lax.axis_index("ctx")
+    for me in range(count):
+        body = functools.partial(mix_at, me, count, lags, own, out_order, back_order, *refs)
+        pl.when(lax.axis_index("ctx") == me)(body)
+
+
+def mix_at(me, count, lags, own, out_order, back_order, *refs):
+    blocks, (fwd_ref, bwd_ref, gains_ref), outs = refs[:count], refs[count : count + 3], refs[count + 3 :]
     group_w = gains_ref.shape[2]
-    for block, by in zip(blocks, (0, *out_order)):
-        inputs[lax.rem(me - by + count, count)] = block[...]
-    values = jnp.concatenate([inputs[i] for i in range(count)], axis=1).astype(F32)
-    gated = (values * jnp.tile(gains_ref[own, 0:1, :], (1, count))).astype(BF16)
-    flipped = (values * jnp.tile(gains_ref[own, 1:2, :], (1, count))).astype(BF16)
+    inputs = {(me - by) % count: block for block, by in zip(blocks, (0, *out_order))}
+    sums = {(me + by) % count: out for out, by in zip(outs, (0, *back_order))}
+    values = [inputs[i][...].astype(F32) for i in range(count)]
+    gated = jnp.concatenate([(value * gains_ref[own, 0:1, :]).astype(BF16) for value in values], axis=1)
+    flipped = jnp.concatenate([(value * gains_ref[own, 1:2, :]).astype(BF16) for value in values], axis=1)
     ahead = [None] * count
     behind = [None] * count
 
@@ -98,9 +115,7 @@
             add(ahead, i + lag, up[:, piece])
             add(behind, i, down[:, piece])
     for i in range(count):
-        sums[i] = (ahead[i] + behind[i].astype(BF16).astype(F32)).astype(BF16)
-    for out, by in zip(outs, (0, *back_order)):
-        out[...] = sums[lax.rem(me + by, count)]
+        sums[i][...] = (ahead[i] + behind[i].astype(BF16).astype(F32)).astype(BF16)
 
 
 def gate_kernel(count, owned, own, back_order, gate_ref, *refs):
@@ -137,29 +152,27 @@
     small = [pltpu.with_memory_space_constraint(array, pltpu.HBM) for array in small]
     messages = [(own, by) for own in range(owned) for by in out_order] + [(own, 0) for own in range(owned)]
     sent = {}
-    for part, source, extra in (
-        (messages[:1], pltpu.with_memory_space_constraint(sequence, pltpu.HBM), small),
-        (messages[1:], sequence, []),
-    ):
+    shares = (messages[:1], messages[1:5], messages[5:])
+    for step, part in enumerate(shares):
+        extra = small if step == 0 else []
+        source = pltpu.with_memory_space_constraint(sequence, pltpu.HBM) if step == 0 else sequence
+        if step == 2:
+            kernel, extra = functools.partial(deal_build_kernel, count, rows, lags, owned, group_w, part), list(map(held, small))
+            added = [VMEM((owned, lags, rows, rows), BF16)] * 2 + [VMEM((owned, 8, group_w), F32)]
+        else:
+            kernel, added = functools.partial(deal_kernel, count, owned, group_w, part), [VMEM(a.shape, a.dtype) for a in extra]
         copied = pl.pallas_call(
-            functools.partial(deal_kernel, count, owned, group_w, part),
-            in_specs=[anywhere] * (1 + len(extra)),
-            out_specs=[vmem] * (len(part) + len(extra)),
-            out_shape=[VMEM((rows, group_w), BF16) for _ in part] + [VMEM(array.shape, array.dtype) for array in extra],
+            kernel,
+            in_specs=[anywhere] + [vmem if step == 2 else anywhere] * len(extra),
+            out_specs=[vmem] * (len(part) + len(added)),
+            out_shape=[VMEM((rows, group_w), BF16) for _ in part] + added,
             scratch_shapes=[dma((len(part) + len(extra),))],
             compiler_params=params,
             name="deal",
         )(source, *extra)
         sent.update({(own, by): rotated(array, by) if by else array for (own, by), array in zip(part, copied)})
-        small = copied[len(part) :] if extra else small
-    built = pl.pallas_call(
-        functools.partial(build_kernel, rows, lags, owned, tuple(range(owned))),
-        in_specs=[vmem] * 4,
-        out_specs=[vmem] * 3,
-        out_shape=[VMEM((owned, lags, rows, rows), BF16)] * 2 + [VMEM((owned, 8, group_w), F32)],
-        compiler_params=params,
-        name="build",
-    )(*map(held, small))
+        small = copied[len(part) :] if step == 0 else small
+    built = copied[len(part) :]
     back = []
     for own in range(owned):
         outs = pl.pallas_call(
@@ -167,7 +180,6 @@
             in_specs=[vmem] * (count + 3),
             out_specs=[vmem] * count,
             out_shape=[VMEM((rows, group_w), BF16)] * count,
-            scratch_shapes=[VMEM((count, rows, group_w), BF16)] * 2,
             compiler_params=params,
             name="mix",
         )(*map(held, [*[sent[own, by] for by in (0, *out_order)], *built]))

time: 28.6 us -> 28.6 us (level)
  no operation moved by 1% of the time
where the time goes in v6:
time: 28.6 us; the launch traced here: 28.5 us
  starting transfers between devices  21.3 us (74%)
  Pallas kernels  4.61 us (16%)
  waiting for transfers between devices  2.49 us (9%)
    ppermute x12, starting transfers between devices, rotated(): lax.ppermute(array, 'ctx', [(i, (i + by) % count) for i in range(count)])  21.3 us
    ppermute x12, waiting for transfers between devices, rotated(): lax.ppermute(array, 'ctx', [(i, (i + by) % count) for i in range(count)])  2.49 us
    pallas_call x3, Pallas kernels, dealt(): pl.pallas_call(kernel, in_specs=[anywhere] + [vmem if step == 2 else anyw...  1.81 us
    pallas_call x2, Pallas kernels, dealt(): pl.pallas_call(functools.partial(gate_kernel, count, owned, own, back_ord...  1.54 us
    pallas_call x2, Pallas kernels, dealt(): pl.pallas_call(functools.partial(mix_kernel, count, lags, own, out_order,...  1.26 us
  transfers between devices with their start and end apart: 12, of which 2 were waited for; matrix products, arithmetic and copies ran while one was open for 0% of the time, Pallas kernels for 10%

profile of v6, /device:TPU:0, one launch (start us, length us, event | category | flops | bytes accessed | tf_op | source)
XLA Modules:
  0.0 28.5 jit_solution(4281885004639491684)
XLA Ops:
  0.0 1.0 %deal.3 = (bf16[256,128]{1,0:T(8,128)(2,1)S(1)}, f32[8,768]{1,0:T(8,128)S(1)}, s32[1,8]{1,0:T(1,128)S(1)}, f32[8,128]{1,0:T(8,128)S(1)}, s32[1,128]{1,0:T(1,128)S(1)}) custom-call(bf16[256,1024]{1,0:T(8,128)(2,1)} %x_ref.5, f32[8,768]{1,0:T(8,128)} %refs_0_.1, s32[1,8]{1,0:T(1,128)} %bitcast.4, f32[8,128]{1,0:T(8,128)} %bitcast.3, s32[1,128]{1,0:T(1,128)} %bitcast.5), custom_call_target="tpu_custom_call" | custom-call | tf_op jit(solution)/shard_map/deal/pallas_call | solution.py:164
  1.0 4.1 %collective-permute-start.6 = (bf16[256,128]{1,0:T(8,128)(2,1)S(1)}, bf16[256,128]{1,0:T(8,128)(2,1)S(1)}, u32[]{:S(2)}, u32[]{:S(2)}) collective-permute-start(bf16[256,128]{1,0:T(8,128)(2,1)S(1)} %get-tuple-element.44), channel_id=1, source_target_pairs={{0,8},{4,12},{8,0},{12,4},{1,9},{5,13},{9,1},{13,5},{2,10},{6,14},... | collective-permute-start | bytes 196616 | tf_op jit(solution)/shard_map/ppermute | solution.py:21
  5.1 0.0 copy-done
  5.1 0.1 deal.5
  5.2 1.6 %collective-permute-start.7 = (bf16[256,128]{1,0:T(8,128)(2,1)S(1)}, bf16[256,128]{1,0:T(8,128)(2,1)S(1)}, u32[]{:S(2)}, u32[]{:S(2)}) collective-permute-start(bf16[256,128]{1,0:T(8,128)(2,1)S(1)} %get-tuple-element.45), channel_id=1, source_target_pairs={{0,4},{4,8},{8,12},{12,0},{1,5},{5,9},{9,13},{13,1},{2,6},{6,10},{... | collective-permute-start | bytes 196616 | tf_op jit(solution)/shard_map/ppermute | solution.py:21
  6.8 2.2 %collective-permute-start.8 = (bf16[256,128]{1,0:T(8,128)(2,1)S(1)}, bf16[256,128]{1,0:T(8,128)(2,1)S(1)}, u32[]{:S(2)}, u32[]{:S(2)}) collective-permute-start(bf16[256,128]{1,0:T(8,128)(2,1)S(1)} %get-tuple-element.46), channel_id=1, source_target_pairs={{0,12},{4,0},{8,4},{12,8},{1,13},{5,1},{9,5},{13,9},{2,14},{6,2},{... | collective-permute-start | bytes 196616 | tf_op jit(solution)/shard_map/ppermute | solution.py:21
  9.1 0.0 collective-permute-start
  9.1 0.6 %collective-permute-start.1 = (bf16[256,128]{1,0:T(8,128)(2,1)S(1)}, bf16[256,128]{1,0:T(8,128)(2,1)S(1)}, u32[]{:S(2)}, u32[]{:S(2)}) collective-permute-start(bf16[256,128]{1,0:T(8,128)(2,1)S(1)} %get-tuple-element.34), channel_id=1, source_target_pairs={{0,4},{4,8},{8,12},{12,0},{1,5},{5,9},{9,13},{13,1},{2,6},{6,10},{... | collective-permute-start | bytes 196616 | tf_op jit(solution)/shard_map/ppermute | solution.py:21
  9.6 0.7 %deal.4 = (bf16[256,128]{1,0:T(8,128)(2,1)S(1)}, bf16[256,128]{1,0:T(8,128)(2,1)S(1)}, bf16[256,128]{1,0:T(8,128)(2,1)S(1)}, bf16[2,4,256,256]{3,2,1,0:T(8,128)(...) custom-call(bf16[256,1024]{1,0:T(8,128)(2,1)S(1)} %copy-done, ...), custom_call_target="tpu_custom_call" | custom-call | tf_op jit(solution)/shard_map/deal/pallas_call | solution.py:164
  10.4 0.0 collective-permute-done.6.refs_1_
  10.4 3.3 %collective-permute-start.2 = (bf16[256,128]{1,0:T(8,128)(2,1)S(1)}, bf16[256,128]{1,0:T(8,128)(2,1)S(1)}, u32[]{:S(2)}, u32[]{:S(2)}) collective-permute-start(bf16[256,128]{1,0:T(8,128)(2,1)S(1)} %get-tuple-element.35), channel_id=1, source_target_pairs={{0,12},{4,0},{8,4},{12,8},{1,13},{5,1},{9,5},{13,9},{2,14},{6,2},{... | collective-permute-start | bytes 196616 | tf_op jit(solution)/shard_map/ppermute | solution.py:21
  13.7 0.0 collective-permute-done.7.refs_2_
  13.7 0.0 collective-permute-done.8.refs_3_
  13.7 0.6 %mix.3 = (bf16[256,128]{1,0:T(8,128)(2,1)S(1)}, bf16[256,128]{1,0:T(8,128)(2,1)S(1)}, bf16[256,128]{1,0:T(8,128)(2,1)S(1)}, bf16[256,128]{1,0:T(8,128)(2,1)S(1)}) custom-call(bf16[256,128]{1,0:T(8,128)(2,1)S(1)} %get-tuple-element.43.refs_0_, bf16[256,128]{1,0:T(8,128)(2,1)S(1)} %collective-permute-done.6.refs_1_, ...), custom_call_target="tpu_custom_call" | custom-call | tf_op jit(solution)/shard_map/mix/pallas_call | solution.py:178
  14.3 0.1 collective-permute-start.9
  14.5 2.5 %collective-permute-start.10 = (bf16[256,128]{1,0:T(8,128)(2,1)S(1)}, bf16[256,128]{1,0:T(8,128)(2,1)S(1)}, u32[]{:S(2)}, u32[]{:S(2)}) collective-permute-start(bf16[256,128]{1,0:T(8,128)(2,1)S(1)} %get-tuple-element.49), channel_id=1, source_target_pairs={{0,8},{4,12},{8,0},{12,4},{1,9},{5,13},{9,1},{13,5},{2,10},{6,14},... | collective-permute-start | bytes 196616 | tf_op jit(solution)/shard_map/ppermute | solution.py:21
  17.0 0.0 collective-permute-done.refs_1_
  17.0 2.5 %collective-permute-start.11 = (bf16[256,128]{1,0:T(8,128)(2,1)S(1)}, bf16[256,128]{1,0:T(8,128)(2,1)S(1)}, u32[]{:S(2)}, u32[]{:S(2)}) collective-permute-start(bf16[256,128]{1,0:T(8,128)(2,1)S(1)} %get-tuple-element.50), channel_id=1, source_target_pairs={{0,12},{4,0},{8,4},{12,8},{1,13},{5,1},{9,5},{13,9},{2,14},{6,2},{... | collective-permute-start | bytes 196616 | tf_op jit(solution)/shard_map/ppermute | solution.py:21
  19.5 0.0 collective-permute-done.1.refs_2_
  19.5 0.0 collective-permute-done.2.refs_3_
  19.5 0.6 %mix.2 = (bf16[256,128]{1,0:T(8,128)(2,1)S(1)}, bf16[256,128]{1,0:T(8,128)(2,1)S(1)}, bf16[256,128]{1,0:T(8,128)(2,1)S(1)}, bf16[256,128]{1,0:T(8,128)(2,1)S(1)}) custom-call(bf16[256,128]{1,0:T(8,128)(2,1)S(1)} %get-tuple-element.32.refs_0_, bf16[256,128]{1,0:T(8,128)(2,1)S(1)} %collective-permute-done.refs_1_, ...), custom_call_target="tpu_custom_call" | custom-call | tf_op jit(solution)/shard_map/mix/pallas_call | solution.py:178
  20.1 0.4 %collective-permute-start.3 = (bf16[256,128]{1,0:T(8,128)(2,1)S(1)}, bf16[256,128]{1,0:T(8,128)(2,1)S(1)}, u32[]{:S(2)}, u32[]{:S(2)}) collective-permute-start(bf16[256,128]{1,0:T(8,128)(2,1)S(1)} %get-tuple-element.40), channel_id=1, source_target_pairs={{0,4},{4,8},{8,12},{12,0},{1,5},{5,9},{9,13},{13,1},{2,6},{6,10},{... | collective-permute-start | bytes 196616 | tf_op jit(solution)/shard_map/ppermute | solution.py:21
  20.5 1.1 %collective-permute-start.4 = (bf16[256,128]{1,0:T(8,128)(2,1)S(1)}, bf16[256,128]{1,0:T(8,128)(2,1)S(1)}, u32[]{:S(2)}, u32[]{:S(2)}) collective-permute-start(bf16[256,128]{1,0:T(8,128)(2,1)S(1)} %get-tuple-element.41), channel_id=1, source_target_pairs={{0,8},{4,12},{8,0},{12,4},{1,9},{5,13},{9,1},{13,5},{2,10},{6,14},... | collective-permute-start | bytes 196616 | tf_op jit(solution)/shard_map/ppermute | solution.py:21
  21.6 0.0 collective-permute-done.9.refs_1_
  21.6 2.8 %collective-permute-start.5 = (bf16[256,128]{1,0:T(8,128)(2,1)S(1)}, bf16[256,128]{1,0:T(8,128)(2,1)S(1)}, u32[]{:S(2)}, u32[]{:S(2)}) collective-permute-start(bf16[256,128]{1,0:T(8,128)(2,1)S(1)} %get-tuple-element.42), channel_id=1, source_target_pairs={{0,12},{4,0},{8,4},{12,8},{1,13},{5,1},{9,5},{13,9},{2,14},{6,2},{... | collective-permute-start | bytes 196616 | tf_op jit(solution)/shard_map/ppermute | solution.py:21
  24.4 0.0 collective-permute-done.10.refs_2_
  24.4 0.0 collective-permute-done.11.refs_3_
  24.4 0.8 %gate.2.refs_4_ = bf16[256,1024]{1,0:T(8,128)(2,1)} custom-call(bf16[256,1024]{1,0:T(8,128)(2,1)S(1)} %copy-done.1, bf16[256,128]{1,0:T(8,128)(2,1)S(1)} %get-tuple-element.47.refs_0_, bf16[256,128]{1,0:T(8,128)(2,1)S(1)} %collective-permute-done.9.refs_1_, bf16[256,128]{1,0:T(8,128)(2,1)S(1)} %collective-permute-done.10.refs_2_, ...), custom_call_target="tpu_custom_call" | custom-call | tf_op jit(solution)/shard_map/gate/pallas_call | solution.py:191
  25.2 1.1 %collective-permute-done.3.refs_1_ = bf16[256,128]{1,0:T(8,128)(2,1)S(1)} collective-permute-done((bf16[256,128]{1,0:T(8,128)(2,1)S(1)}, bf16[256,128]{1,0:T(8,128)(2,1)S(1)}, u32[]{:S(2)}, u32[]{:S(2)}) %collective-permute-start.3) | collective-permute-done | bytes 65568 | tf_op jit(solution)/shard_map/ppermute | solution.py:21
  26.4 1.3 %collective-permute-done.4.refs_2_ = bf16[256,128]{1,0:T(8,128)(2,1)S(1)} collective-permute-done((bf16[256,128]{1,0:T(8,128)(2,1)S(1)}, bf16[256,128]{1,0:T(8,128)(2,1)S(1)}, u32[]{:S(2)}, u32[]{:S(2)}) %collective-permute-start.4) | collective-permute-done | bytes 65568 | tf_op jit(solution)/shard_map/ppermute | solution.py:21
  27.7 0.0 collective-permute-done.5.refs_3_
  27.7 0.8 %gate.3 = bf16[256,1024]{1,0:T(8,128)(2,1)} custom-call(bf16[256,1024]{1,0:T(8,128)(2,1)S(1)} %copy-done.1, bf16[256,128]{1,0:T(8,128)(2,1)S(1)} %get-tuple-element.39.refs_0_, bf16[256,128]{1,0:T(8,128)(2,1)S(1)} %collective-permute-done.3.refs_1_, bf16[256,128]{1,0:T(8,128)(2,1)S(1)} %collective-permute-done.4.refs_2_, ...), custom_call_target="tpu_custom_call", output_to_operand_aliasing={{}: (5, {})} | custom-call | tf_op jit(solution)/shard_map/gate/pallas_call | solution.py:191
  (3 shorter events, 0.0 us)
Async XLA Ops:
  0.0 5.1 %copy-start = (bf16[256,1024]{1,0:T(8,128)(2,1)S(1)}, bf16[256,1024]{1,0:T(8,128)(2,1)}, u32[]{:S(2)}) copy-start(bf16[256,1024]{1,0:T(8,128)(2,1)} %x_ref.5) | copy-start | bytes 1572868
  1.0 9.4 %collective-permute-start.6 = (bf16[256,128]{1,0:T(8,128)(2,1)S(1)}, bf16[256,128]{1,0:T(8,128)(2,1)S(1)}, u32[]{:S(2)}, u32[]{:S(2)}) collective-permute-start(bf16[256,128]{1,0:T(8,128)(2,1)S(1)} %get-tuple-element.44), channel_id=1, source_target_pairs={{0,8},{4,12},{8,0},{12,4},{1,9},{5,13},{9,1},{13,5},{2,10},{6,14},... | collective-permute-start | bytes 196616 | tf_op jit(solution)/shard_map/ppermute | solution.py:21
  5.2 8.5 %collective-permute-start.7 = (bf16[256,128]{1,0:T(8,128)(2,1)S(1)}, bf16[256,128]{1,0:T(8,128)(2,1)S(1)}, u32[]{:S(2)}, u32[]{:S(2)}) collective-permute-start(bf16[256,128]{1,0:T(8,128)(2,1)S(1)} %get-tuple-element.45), channel_id=1, source_target_pairs={{0,4},{4,8},{8,12},{12,0},{1,5},{5,9},{9,13},{13,1},{2,6},{6,10},{... | collective-permute-start | bytes 196616 | tf_op jit(solution)/shard_map/ppermute | solution.py:21
  6.8 6.9 %collective-permute-start.8 = (bf16[256,128]{1,0:T(8,128)(2,1)S(1)}, bf16[256,128]{1,0:T(8,128)(2,1)S(1)}, u32[]{:S(2)}, u32[]{:S(2)}) collective-permute-start(bf16[256,128]{1,0:T(8,128)(2,1)S(1)} %get-tuple-element.46), channel_id=1, source_target_pairs={{0,12},{4,0},{8,4},{12,8},{1,13},{5,1},{9,5},{13,9},{2,14},{6,2},{... | collective-permute-start | bytes 196616 | tf_op jit(solution)/shard_map/ppermute | solution.py:21
  9.1 7.9 %collective-permute-start = (bf16[256,128]{1,0:T(8,128)(2,1)S(1)}, bf16[256,128]{1,0:T(8,128)(2,1)S(1)}, u32[]{:S(2)}, u32[]{:S(2)}) collective-permute-start(bf16[256,128]{1,0:T(8,128)(2,1)S(1)} %get-tuple-element.33), channel_id=1, source_target_pairs={{0,8},{4,12},{8,0},{12,4},{1,9},{5,13},{9,1},{13,5},{2,10},{6,14},... | collective-permute-start | bytes 196616 | tf_op jit(solution)/shard_map/ppermute | solution.py:21
  9.1 10.4 %collective-permute-start.1 = (bf16[256,128]{1,0:T(8,128)(2,1)S(1)}, bf16[256,128]{1,0:T(8,128)(2,1)S(1)}, u32[]{:S(2)}, u32[]{:S(2)}) collective-permute-start(bf16[256,128]{1,0:T(8,128)(2,1)S(1)} %get-tuple-element.34), channel_id=1, source_target_pairs={{0,4},{4,8},{8,12},{12,0},{1,5},{5,9},{9,13},{13,1},{2,6},{6,10},{... | collective-permute-start | bytes 196616 | tf_op jit(solution)/shard_map/ppermute | solution.py:21
  10.4 9.1 %collective-permute-start.2 = (bf16[256,128]{1,0:T(8,128)(2,1)S(1)}, bf16[256,128]{1,0:T(8,128)(2,1)S(1)}, u32[]{:S(2)}, u32[]{:S(2)}) collective-permute-start(bf16[256,128]{1,0:T(8,128)(2,1)S(1)} %get-tuple-element.35), channel_id=1, source_target_pairs={{0,12},{4,0},{8,4},{12,8},{1,13},{5,1},{9,5},{13,9},{2,14},{6,2},{... | collective-permute-start | bytes 196616 | tf_op jit(solution)/shard_map/ppermute | solution.py:21
  14.3 7.3 %collective-permute-start.9 = (bf16[256,128]{1,0:T(8,128)(2,1)S(1)}, bf16[256,128]{1,0:T(8,128)(2,1)S(1)}, u32[]{:S(2)}, u32[]{:S(2)}) collective-permute-start(bf16[256,128]{1,0:T(8,128)(2,1)S(1)} %get-tuple-element.48), channel_id=1, source_target_pairs={{0,4},{4,8},{8,12},{12,0},{1,5},{5,9},{9,13},{13,1},{2,6},{6,10},{... | collective-permute-start | bytes 196616 | tf_op jit(solution)/shard_map/ppermute | solution.py:21
  14.5 10.0 %collective-permute-start.10 = (bf16[256,128]{1,0:T(8,128)(2,1)S(1)}, bf16[256,128]{1,0:T(8,128)(2,1)S(1)}, u32[]{:S(2)}, u32[]{:S(2)}) collective-permute-start(bf16[256,128]{1,0:T(8,128)(2,1)S(1)} %get-tuple-element.49), channel_id=1, source_target_pairs={{0,8},{4,12},{8,0},{12,4},{1,9},{5,13},{9,1},{13,5},{2,10},{6,14},... | collective-permute-start | bytes 196616 | tf_op jit(solution)/shard_map/ppermute | solution.py:21
  17.0 7.5 %collective-permute-start.11 = (bf16[256,128]{1,0:T(8,128)(2,1)S(1)}, bf16[256,128]{1,0:T(8,128)(2,1)S(1)}, u32[]{:S(2)}, u32[]{:S(2)}) collective-permute-start(bf16[256,128]{1,0:T(8,128)(2,1)S(1)} %get-tuple-element.50), channel_id=1, source_target_pairs={{0,12},{4,0},{8,4},{12,8},{1,13},{5,1},{9,5},{13,9},{2,14},{6,2},{... | collective-permute-start | bytes 196616 | tf_op jit(solution)/shard_map/ppermute | solution.py:21
  19.5 5.0 %copy-start.1 = (bf16[256,1024]{1,0:T(8,128)(2,1)S(1)}, bf16[256,1024]{1,0:T(8,128)(2,1)}, u32[]{:S(2)}) copy-start(bf16[256,1024]{1,0:T(8,128)(2,1)} %gate_ref.3) | copy-start | bytes 1572868
  20.1 6.2 %collective-permute-start.3 = (bf16[256,128]{1,0:T(8,128)(2,1)S(1)}, bf16[256,128]{1,0:T(8,128)(2,1)S(1)}, u32[]{:S(2)}, u32[]{:S(2)}) collective-permute-start(bf16[256,128]{1,0:T(8,128)(2,1)S(1)} %get-tuple-element.40), channel_id=1, source_target_pairs={{0,4},{4,8},{8,12},{12,0},{1,5},{5,9},{9,13},{13,1},{2,6},{6,10},{... | collective-permute-start | bytes 196616 | tf_op jit(solution)/shard_map/ppermute | solution.py:21
  20.5 7.2 %collective-permute-start.4 = (bf16[256,128]{1,0:T(8,128)(2,1)S(1)}, bf16[256,128]{1,0:T(8,128)(2,1)S(1)}, u32[]{:S(2)}, u32[]{:S(2)}) collective-permute-start(bf16[256,128]{1,0:T(8,128)(2,1)S(1)} %get-tuple-element.41), channel_id=1, source_target_pairs={{0,8},{4,12},{8,0},{12,4},{1,9},{5,13},{9,1},{13,5},{2,10},{6,14},... | collective-permute-start | bytes 196616 | tf_op jit(solution)/shard_map/ppermute | solution.py:21
  21.6 6.1 %collective-permute-start.5 = (bf16[256,128]{1,0:T(8,128)(2,1)S(1)}, bf16[256,128]{1,0:T(8,128)(2,1)S(1)}, u32[]{:S(2)}, u32[]{:S(2)}) collective-permute-start(bf16[256,128]{1,0:T(8,128)(2,1)S(1)} %get-tuple-element.42), channel_id=1, source_target_pairs={{0,12},{4,0},{8,4},{12,8},{1,13},{5,1},{9,5},{13,9},{2,14},{6,2},{... | collective-permute-start | bytes 196616 | tf_op jit(solution)/shard_map/ppermute | solution.py:21

commit v7 on v6

--- a/solution.py
+++ b/solution.py
@@ -21,14 +21,21 @@
     return lax.ppermute(array, "ctx", [(i, (i + by) % count) for i in range(count)])
 
 
+def returned(array, bys):
+    count, cores = lax.axis_size("ctx"), lax.axis_size("sub")
+    pairs = [(i * cores + c, (i + bys[c % 2]) % count * cores + c) for c in range(cores) for i in range(count)]
+    return lax.ppermute(array, ("ctx", "sub"), pairs)
+
+
 def held(array):
     return pltpu.with_memory_space_constraint(array, VMEM)
 
 
 def rounds(count):
     if count == 4:
-        return (2, 1, 3), (1, 2, 3)
-    return (tuple(range(1, count)),) * 2
+        return (2, 1, 3), (((1, 2, 3), (1, 2, 3)), ((1, 2, 3), (2, 1, 3)))
+    plain = tuple(range(1, count))
+    return plain, ((plain, plain),) * 8
 
 
 def lanes(by, own, count, owned, group_w):
@@ -87,9 +94,13 @@
 
 
 def mix_kernel(count, lags, own, out_order, back_order, *refs):
+    core = lax.rem(lax.axis_index("sub"), 2)
+    same = back_order[0] == back_order[1]
     for me in range(count):
-        body = functools.partial(mix_at, me, count, lags, own, out_order, back_order, *refs)
-        pl.when(lax.axis_index("ctx") == me)(body)
+        here = lax.axis_index("ctx") == me
+        for at in range(1 if same else 2):
+            body = functools.partial(mix_at, me, count, lags, own, out_order, back_order[at], *refs)
+            pl.when(here if same else here & (core == at))(body)
 
 
 def mix_at(me, count, lags, own, out_order, back_order, *refs):
@@ -122,7 +133,9 @@
     blocks, out_ref, (pieces, sems) = refs[:count], refs[-3], refs[-2:]
     group_w = blocks[0].shape[1]
     copies = []
-    for i, by in enumerate((0, *back_order)):
+    core = lax.rem(lax.axis_index("sub"), 2)
+    for i, (first, second) in enumerate(zip((0, *back_order[0]), (0, *back_order[1]))):
+        by = first if first == second else jnp.where(core == 0, first, second)
         place = lanes(count - by, own, count, owned, group_w)
         pieces[i] = (gate_ref[:, place].astype(F32) * blocks[i][...].astype(F32)).astype(BF16)
         copies.append(pltpu.make_async_copy(pieces.at[i], out_ref.at[:, place], sems.at[i]))
@@ -176,20 +189,20 @@
     back = []
     for own in range(owned):
         outs = pl.pallas_call(
-            functools.partial(mix_kernel, count, lags, own, out_order, back_order),
+            functools.partial(mix_kernel, count, lags, own, out_order, back_order[own]),
             in_specs=[vmem] * (count + 3),
             out_specs=[vmem] * count,
             out_shape=[VMEM((rows, group_w), BF16)] * count,
             compiler_params=params,
             name="mix",
         )(*map(held, [*[sent[own, by] for by in (0, *out_order)], *built]))
-        back.append([rotated(array, by) if by else array for by, array in zip((0, *back_order), outs)])
+        back.append([outs[0]] + [returned(array, bys) for bys, array in zip(zip(*back_order[own]), outs[1:])])
     gate = held(gate)
     out = []
     for own in range(owned):
         out = [
             pl.pallas_call(
-                functools.partial(gate_kernel, count, owned, own, back_order),
+                functools.partial(gate_kernel, count, owned, own, back_order[own]),
                 in_specs=[vmem] * (count + 1) + [anywhere] * len(out),
                 out_specs=anywhere,
                 out_shape=jax.ShapeDtypeStruct((rows, width), BF16),

time: 28.6 us -> 28.6 us (level)
    ppermute x12 -> x6, starting transfers between devices: 21.3 us -> 11.9 us  [rotated(): lax.ppermute(array, 'ctx', [(i, (i + by) % count) for i in range(count)])]
    ppermute x0 -> x6, starting transfers between devices: none -> 9.41 us  [returned(): return lax.ppermute(array, ('ctx', 'sub'), pairs)]
    ppermute x12 -> x6, waiting for transfers between devices: 2.49 us -> 0.02 us  [rotated(): lax.ppermute(array, 'ctx', [(i, (i + by) % count) for i in range(count)])]
    ppermute x0 -> x6, waiting for transfers between devices: none -> 2.46 us  [returned(): return lax.ppermute(array, ('ctx', 'sub'), pairs)]
where the time goes in v7:
time: 28.6 us; the launch traced here: 28.4 us
  starting transfers between devices  21.3 us (74%)
  Pallas kernels  4.62 us (16%)
  waiting for transfers between devices  2.48 us (9%)
    ppermute x6, starting transfers between devices, rotated(): lax.ppermute(array, 'ctx', [(i, (i + by) % count) for i in range(count)])  11.9 us
    ppermute x6, starting transfers between devices, returned(): return lax.ppermute(array, ('ctx', 'sub'), pairs)  9.41 us
    ppermute x6, waiting for transfers between devices, returned(): return lax.ppermute(array, ('ctx', 'sub'), pairs)  2.46 us
    pallas_call x3, Pallas kernels, dealt(): pl.pallas_call(kernel, in_specs=[anywhere] + [vmem if step == 2 else anyw...  1.81 us
    pallas_call x2, Pallas kernels, dealt(): pl.pallas_call(functools.partial(gate_kernel, count, owned, own, back_ord...  1.53 us
    pallas_call x2, Pallas kernels, dealt(): pl.pallas_call(functools.partial(mix_kernel, count, lags, own, out_order,...  1.28 us
  transfers between devices with their start and end apart: 12, of which 2 were waited for; matrix products, arithmetic and copies ran while one was open for 0% of the time, Pallas kernels for 10%

profile of v7, /device:TPU:0, one launch (start us, length us, event | category | flops | bytes accessed | tf_op | source)
XLA Modules:
  0.0 28.4 jit_solution(6363743531628484225)
XLA Ops:
  0.0 1.0 %deal.3 = (bf16[256,128]{1,0:T(8,128)(2,1)S(1)}, f32[8,768]{1,0:T(8,128)S(1)}, s32[1,8]{1,0:T(1,128)S(1)}, f32[8,128]{1,0:T(8,128)S(1)}, s32[1,128]{1,0:T(1,128)S(1)}) custom-call(bf16[256,1024]{1,0:T(8,128)(2,1)} %x_ref.5, f32[8,768]{1,0:T(8,128)} %refs_0_.1, s32[1,8]{1,0:T(1,128)} %bitcast.4, f32[8,128]{1,0:T(8,128)} %bitcast.3, s32[1,128]{1,0:T(1,128)} %bitcast.5), custom_call_target="tpu_custom_call" | custom-call | tf_op jit(solution)/shard_map/deal/pallas_call | solution.py:177
  1.0 4.1 %collective-permute-start.6 = (bf16[256,128]{1,0:T(8,128)(2,1)S(1)}, bf16[256,128]{1,0:T(8,128)(2,1)S(1)}, u32[]{:S(2)}, u32[]{:S(2)}) collective-permute-start(bf16[256,128]{1,0:T(8,128)(2,1)S(1)} %get-tuple-element.44), channel_id=1, source_target_pairs={{0,8},{4,12},{8,0},{12,4},{1,9},{5,13},{9,1},{13,5},{2,10},{6,14},... | collective-permute-start | bytes 196616 | tf_op jit(solution)/shard_map/ppermute | solution.py:21
  5.1 0.1 deal.5
  5.2 1.6 %collective-permute-start.7 = (bf16[256,128]{1,0:T(8,128)(2,1)S(1)}, bf16[256,128]{1,0:T(8,128)(2,1)S(1)}, u32[]{:S(2)}, u32[]{:S(2)}) collective-permute-start(bf16[256,128]{1,0:T(8,128)(2,1)S(1)} %get-tuple-element.45), channel_id=1, source_target_pairs={{0,4},{4,8},{8,12},{12,0},{1,5},{5,9},{9,13},{13,1},{2,6},{6,10},{... | collective-permute-start | bytes 196616 | tf_op jit(solution)/shard_map/ppermute | solution.py:21
  6.8 2.2 %collective-permute-start.8 = (bf16[256,128]{1,0:T(8,128)(2,1)S(1)}, bf16[256,128]{1,0:T(8,128)(2,1)S(1)}, u32[]{:S(2)}, u32[]{:S(2)}) collective-permute-start(bf16[256,128]{1,0:T(8,128)(2,1)S(1)} %get-tuple-element.46), channel_id=1, source_target_pairs={{0,12},{4,0},{8,4},{12,8},{1,13},{5,1},{9,5},{13,9},{2,14},{6,2},{... | collective-permute-start | bytes 196616 | tf_op jit(solution)/shard_map/ppermute | solution.py:21
  9.1 0.0 collective-permute-start
  9.1 0.6 %collective-permute-start.1 = (bf16[256,128]{1,0:T(8,128)(2,1)S(1)}, bf16[256,128]{1,0:T(8,128)(2,1)S(1)}, u32[]{:S(2)}, u32[]{:S(2)}) collective-permute-start(bf16[256,128]{1,0:T(8,128)(2,1)S(1)} %get-tuple-element.34), channel_id=1, source_target_pairs={{0,4},{4,8},{8,12},{12,0},{1,5},{5,9},{9,13},{13,1},{2,6},{6,10},{... | collective-permute-start | bytes 196616 | tf_op jit(solution)/shard_map/ppermute | solution.py:21
  9.6 0.7 %deal.4 = (bf16[256,128]{1,0:T(8,128)(2,1)S(1)}, bf16[256,128]{1,0:T(8,128)(2,1)S(1)}, bf16[256,128]{1,0:T(8,128)(2,1)S(1)}, bf16[2,4,256,256]{3,2,1,0:T(8,128)(...) custom-call(bf16[256,1024]{1,0:T(8,128)(2,1)S(1)} %copy-done, ...), custom_call_target="tpu_custom_call" | custom-call | tf_op jit(solution)/shard_map/deal/pallas_call | solution.py:177
  10.4 0.0 collective-permute-done.6.refs_1_
  10.4 3.3 %collective-permute-start.2 = (bf16[256,128]{1,0:T(8,128)(2,1)S(1)}, bf16[256,128]{1,0:T(8,128)(2,1)S(1)}, u32[]{:S(2)}, u32[]{:S(2)}) collective-permute-start(bf16[256,128]{1,0:T(8,128)(2,1)S(1)} %get-tuple-element.35), channel_id=1, source_target_pairs={{0,12},{4,0},{8,4},{12,8},{1,13},{5,1},{9,5},{13,9},{2,14},{6,2},{... | collective-permute-start | bytes 196616 | tf_op jit(solution)/shard_map/ppermute | solution.py:21
  13.7 0.0 collective-permute-done.7.refs_2_
  13.7 0.0 collective-permute-done.8.refs_3_
  13.7 0.6 %mix.3 = (bf16[256,128]{1,0:T(8,128)(2,1)S(1)}, bf16[256,128]{1,0:T(8,128)(2,1)S(1)}, bf16[256,128]{1,0:T(8,128)(2,1)S(1)}, bf16[256,128]{1,0:T(8,128)(2,1)S(1)}) custom-call(bf16[256,128]{1,0:T(8,128)(2,1)S(1)} %get-tuple-element.43.refs_0_, bf16[256,128]{1,0:T(8,128)(2,1)S(1)} %collective-permute-done.6.refs_1_, ...), custom_call_target="tpu_custom_call" | custom-call | tf_op jit(solution)/shard_map/mix/pallas_call | solution.py:191
  14.3 0.1 collective-permute-start.9
  14.5 2.5 %collective-permute-start.10 = (bf16[256,128]{1,0:T(8,128)(2,1)S(1)}, bf16[256,128]{1,0:T(8,128)(2,1)S(1)}, u32[]{:S(2)}, u32[]{:S(2)}) collective-permute-start(bf16[256,128]{1,0:T(8,128)(2,1)S(1)} %get-tuple-element.49), channel_id=1, source_target_pairs={{0,8},{4,12},{8,0},{12,4},{1,9},{5,13},{9,1},{13,5},{2,10},{6,14},... | collective-permute-start | bytes 196616 | tf_op jit(solution)/shard_map/ppermute | solution.py:27
  17.0 0.0 collective-permute-done.refs_1_
  17.0 2.5 %collective-permute-start.11 = (bf16[256,128]{1,0:T(8,128)(2,1)S(1)}, bf16[256,128]{1,0:T(8,128)(2,1)S(1)}, u32[]{:S(2)}, u32[]{:S(2)}) collective-permute-start(bf16[256,128]{1,0:T(8,128)(2,1)S(1)} %get-tuple-element.50), channel_id=1, source_target_pairs={{0,12},{4,0},{8,4},{12,8},{1,13},{5,1},{9,5},{13,9},{2,14},{6,2},{... | collective-permute-start | bytes 196616 | tf_op jit(solution)/shard_map/ppermute | solution.py:27
  19.5 0.0 collective-permute-done.1.refs_2_
  19.5 0.0 collective-permute-done.2.refs_3_
  19.5 0.7 %mix.2 = (bf16[256,128]{1,0:T(8,128)(2,1)S(1)}, bf16[256,128]{1,0:T(8,128)(2,1)S(1)}, bf16[256,128]{1,0:T(8,128)(2,1)S(1)}, bf16[256,128]{1,0:T(8,128)(2,1)S(1)}) custom-call(bf16[256,128]{1,0:T(8,128)(2,1)S(1)} %get-tuple-element.32.refs_0_, bf16[256,128]{1,0:T(8,128)(2,1)S(1)} %collective-permute-done.refs_1_, ...), custom_call_target="tpu_custom_call" | custom-call | tf_op jit(solution)/shard_map/mix/pallas_call | solution.py:191
  20.2 0.4 %collective-permute-start.3 = (bf16[256,128]{1,0:T(8,128)(2,1)S(1)}, bf16[256,128]{1,0:T(8,128)(2,1)S(1)}, u32[]{:S(2)}, u32[]{:S(2)}) collective-permute-start(bf16[256,128]{1,0:T(8,128)(2,1)S(1)} %get-tuple-element.40), channel_id=1, source_target_pairs={{0,4},{4,8},{8,12},{12,0},{1,9},{5,13},{9,1},{13,5},{2,6},{6,10},{... | collective-permute-start | bytes 196616 | tf_op jit(solution)/shard_map/ppermute | solution.py:27
  20.5 1.1 %collective-permute-start.4 = (bf16[256,128]{1,0:T(8,128)(2,1)S(1)}, bf16[256,128]{1,0:T(8,128)(2,1)S(1)}, u32[]{:S(2)}, u32[]{:S(2)}) collective-permute-start(bf16[256,128]{1,0:T(8,128)(2,1)S(1)} %get-tuple-element.41), channel_id=1, source_target_pairs={{0,8},{4,12},{8,0},{12,4},{1,5},{5,9},{9,13},{13,1},{2,10},{6,14},... | collective-permute-start | bytes 196616 | tf_op jit(solution)/shard_map/ppermute | solution.py:27
  21.6 0.0 collective-permute-done.9.refs_1_
  21.6 2.8 %collective-permute-start.5 = (bf16[256,128]{1,0:T(8,128)(2,1)S(1)}, bf16[256,128]{1,0:T(8,128)(2,1)S(1)}, u32[]{:S(2)}, u32[]{:S(2)}) collective-permute-start(bf16[256,128]{1,0:T(8,128)(2,1)S(1)} %get-tuple-element.42), channel_id=1, source_target_pairs={{0,12},{4,0},{8,4},{12,8},{1,13},{5,1},{9,5},{13,9},{2,14},{6,2},{... | collective-permute-start | bytes 196616 | tf_op jit(solution)/shard_map/ppermute | solution.py:27
  24.4 0.0 collective-permute-done.10.refs_2_
  24.4 0.0 collective-permute-done.11.refs_3_
  24.5 0.0 copy-done.1
  24.5 0.8 %gate.2.refs_4_ = bf16[256,1024]{1,0:T(8,128)(2,1)} custom-call(bf16[256,1024]{1,0:T(8,128)(2,1)S(1)} %copy-done.1, bf16[256,128]{1,0:T(8,128)(2,1)S(1)} %get-tuple-element.47.refs_0_, bf16[256,128]{1,0:T(8,128)(2,1)S(1)} %collective-permute-done.9.refs_1_, bf16[256,128]{1,0:T(8,128)(2,1)S(1)} %collective-permute-done.10.refs_2_, ...), custom_call_target="tpu_custom_call" | custom-call | tf_op jit(solution)/shard_map/gate/pallas_call | solution.py:204
  25.2 1.8 %collective-permute-done.3.refs_1_ = bf16[256,128]{1,0:T(8,128)(2,1)S(1)} collective-permute-done((bf16[256,128]{1,0:T(8,128)(2,1)S(1)}, bf16[256,128]{1,0:T(8,128)(2,1)S(1)}, u32[]{:S(2)}, u32[]{:S(2)}) %collective-permute-start.3) | collective-permute-done | bytes 65568 | tf_op jit(solution)/shard_map/ppermute | solution.py:27
  27.0 0.7 %collective-permute-done.4.refs_2_ = bf16[256,128]{1,0:T(8,128)(2,1)S(1)} collective-permute-done((bf16[256,128]{1,0:T(8,128)(2,1)S(1)}, bf16[256,128]{1,0:T(8,128)(2,1)S(1)}, u32[]{:S(2)}, u32[]{:S(2)}) %collective-permute-start.4) | collective-permute-done | bytes 65568 | tf_op jit(solution)/shard_map/ppermute | solution.py:27
  27.7 0.0 collective-permute-done.5.refs_3_
  27.7 0.8 %gate.3 = bf16[256,1024]{1,0:T(8,128)(2,1)} custom-call(bf16[256,1024]{1,0:T(8,128)(2,1)S(1)} %copy-done.1, bf16[256,128]{1,0:T(8,128)(2,1)S(1)} %get-tuple-element.39.refs_0_, bf16[256,128]{1,0:T(8,128)(2,1)S(1)} %collective-permute-done.3.refs_1_, bf16[256,128]{1,0:T(8,128)(2,1)S(1)} %collective-permute-done.4.refs_2_, ...), custom_call_target="tpu_custom_call", output_to_operand_aliasing={{}: (5, {})} | custom-call | tf_op jit(solution)/shard_map/gate/pallas_call | solution.py:204
  (3 shorter events, 0.0 us)
Async XLA Ops:
  0.0 5.1 %copy-start = (bf16[256,1024]{1,0:T(8,128)(2,1)S(1)}, bf16[256,1024]{1,0:T(8,128)(2,1)}, u32[]{:S(2)}) copy-start(bf16[256,1024]{1,0:T(8,128)(2,1)} %x_ref.5) | copy-start | bytes 1572868
  1.0 9.4 %collective-permute-start.6 = (bf16[256,128]{1,0:T(8,128)(2,1)S(1)}, bf16[256,128]{1,0:T(8,128)(2,1)S(1)}, u32[]{:S(2)}, u32[]{:S(2)}) collective-permute-start(bf16[256,128]{1,0:T(8,128)(2,1)S(1)} %get-tuple-element.44), channel_id=1, source_target_pairs={{0,8},{4,12},{8,0},{12,4},{1,9},{5,13},{9,1},{13,5},{2,10},{6,14},... | collective-permute-start | bytes 196616 | tf_op jit(solution)/shard_map/ppermute | solution.py:21
  5.2 8.5 %collective-permute-start.7 = (bf16[256,128]{1,0:T(8,128)(2,1)S(1)}, bf16[256,128]{1,0:T(8,128)(2,1)S(1)}, u32[]{:S(2)}, u32[]{:S(2)}) collective-permute-start(bf16[256,128]{1,0:T(8,128)(2,1)S(1)} %get-tuple-element.45), channel_id=1, source_target_pairs={{0,4},{4,8},{8,12},{12,0},{1,5},{5,9},{9,13},{13,1},{2,6},{6,10},{... | collective-permute-start | bytes 196616 | tf_op jit(solution)/shard_map/ppermute | solution.py:21
  6.8 6.9 %collective-permute-start.8 = (bf16[256,128]{1,0:T(8,128)(2,1)S(1)}, bf16[256,128]{1,0:T(8,128)(2,1)S(1)}, u32[]{:S(2)}, u32[]{:S(2)}) collective-permute-start(bf16[256,128]{1,0:T(8,128)(2,1)S(1)} %get-tuple-element.46), channel_id=1, source_target_pairs={{0,12},{4,0},{8,4},{12,8},{1,13},{5,1},{9,5},{13,9},{2,14},{6,2},{... | collective-permute-start | bytes 196616 | tf_op jit(solution)/shard_map/ppermute | solution.py:21
  9.1 7.9 %collective-permute-start = (bf16[256,128]{1,0:T(8,128)(2,1)S(1)}, bf16[256,128]{1,0:T(8,128)(2,1)S(1)}, u32[]{:S(2)}, u32[]{:S(2)}) collective-permute-start(bf16[256,128]{1,0:T(8,128)(2,1)S(1)} %get-tuple-element.33), channel_id=1, source_target_pairs={{0,8},{4,12},{8,0},{12,4},{1,9},{5,13},{9,1},{13,5},{2,10},{6,14},... | collective-permute-start | bytes 196616 | tf_op jit(solution)/shard_map/ppermute | solution.py:21
  9.1 10.4 %collective-permute-start.1 = (bf16[256,128]{1,0:T(8,128)(2,1)S(1)}, bf16[256,128]{1,0:T(8,128)(2,1)S(1)}, u32[]{:S(2)}, u32[]{:S(2)}) collective-permute-start(bf16[256,128]{1,0:T(8,128)(2,1)S(1)} %get-tuple-element.34), channel_id=1, source_target_pairs={{0,4},{4,8},{8,12},{12,0},{1,5},{5,9},{9,13},{13,1},{2,6},{6,10},{... | collective-permute-start | bytes 196616 | tf_op jit(solution)/shard_map/ppermute | solution.py:21
  10.4 9.1 %collective-permute-start.2 = (bf16[256,128]{1,0:T(8,128)(2,1)S(1)}, bf16[256,128]{1,0:T(8,128)(2,1)S(1)}, u32[]{:S(2)}, u32[]{:S(2)}) collective-permute-start(bf16[256,128]{1,0:T(8,128)(2,1)S(1)} %get-tuple-element.35), channel_id=1, source_target_pairs={{0,12},{4,0},{8,4},{12,8},{1,13},{5,1},{9,5},{13,9},{2,14},{6,2},{... | collective-permute-start | bytes 196616 | tf_op jit(solution)/shard_map/ppermute | solution.py:21
  14.3 7.3 %collective-permute-start.9 = (bf16[256,128]{1,0:T(8,128)(2,1)S(1)}, bf16[256,128]{1,0:T(8,128)(2,1)S(1)}, u32[]{:S(2)}, u32[]{:S(2)}) collective-permute-start(bf16[256,128]{1,0:T(8,128)(2,1)S(1)} %get-tuple-element.48), channel_id=1, source_target_pairs={{0,4},{4,8},{8,12},{12,0},{1,5},{5,9},{9,13},{13,1},{2,6},{6,10},{... | collective-permute-start | bytes 196616 | tf_op jit(solution)/shard_map/ppermute | solution.py:27
  14.5 10.0 %collective-permute-start.10 = (bf16[256,128]{1,0:T(8,128)(2,1)S(1)}, bf16[256,128]{1,0:T(8,128)(2,1)S(1)}, u32[]{:S(2)}, u32[]{:S(2)}) collective-permute-start(bf16[256,128]{1,0:T(8,128)(2,1)S(1)} %get-tuple-element.49), channel_id=1, source_target_pairs={{0,8},{4,12},{8,0},{12,4},{1,9},{5,13},{9,1},{13,5},{2,10},{6,14},... | collective-permute-start | bytes 196616 | tf_op jit(solution)/shard_map/ppermute | solution.py:27
  17.0 7.5 %collective-permute-start.11 = (bf16[256,128]{1,0:T(8,128)(2,1)S(1)}, bf16[256,128]{1,0:T(8,128)(2,1)S(1)}, u32[]{:S(2)}, u32[]{:S(2)}) collective-permute-start(bf16[256,128]{1,0:T(8,128)(2,1)S(1)} %get-tuple-element.50), channel_id=1, source_target_pairs={{0,12},{4,0},{8,4},{12,8},{1,13},{5,1},{9,5},{13,9},{2,14},{6,2},{... | collective-permute-start | bytes 196616 | tf_op jit(solution)/shard_map/ppermute | solution.py:27
  19.5 5.0 %copy-start.1 = (bf16[256,1024]{1,0:T(8,128)(2,1)S(1)}, bf16[256,1024]{1,0:T(8,128)(2,1)}, u32[]{:S(2)}) copy-start(bf16[256,1024]{1,0:T(8,128)(2,1)} %gate_ref.3) | copy-start | bytes 1572868
  20.2 6.9 %collective-permute-start.3 = (bf16[256,128]{1,0:T(8,128)(2,1)S(1)}, bf16[256,128]{1,0:T(8,128)(2,1)S(1)}, u32[]{:S(2)}, u32[]{:S(2)}) collective-permute-start(bf16[256,128]{1,0:T(8,128)(2,1)S(1)} %get-tuple-element.40), channel_id=1, source_target_pairs={{0,4},{4,8},{8,12},{12,0},{1,9},{5,13},{9,1},{13,5},{2,6},{6,10},{... | collective-permute-start | bytes 196616 | tf_op jit(solution)/shard_map/ppermute | solution.py:27
  20.5 7.2 %collective-permute-start.4 = (bf16[256,128]{1,0:T(8,128)(2,1)S(1)}, bf16[256,128]{1,0:T(8,128)(2,1)S(1)}, u32[]{:S(2)}, u32[]{:S(2)}) collective-permute-start(bf16[256,128]{1,0:T(8,128)(2,1)S(1)} %get-tuple-element.41), channel_id=1, source_target_pairs={{0,8},{4,12},{8,0},{12,4},{1,5},{5,9},{9,13},{13,1},{2,10},{6,14},... | collective-permute-start | bytes 196616 | tf_op jit(solution)/shard_map/ppermute | solution.py:27
  21.6 6.1 %collective-permute-start.5 = (bf16[256,128]{1,0:T(8,128)(2,1)S(1)}, bf16[256,128]{1,0:T(8,128)(2,1)S(1)}, u32[]{:S(2)}, u32[]{:S(2)}) collective-permute-start(bf16[256,128]{1,0:T(8,128)(2,1)S(1)} %get-tuple-element.42), channel_id=1, source_target_pairs={{0,12},{4,0},{8,4},{12,8},{1,13},{5,1},{9,5},{13,9},{2,14},{6,2},{... | collective-permute-start | bytes 196616 | tf_op jit(solution)/shard_map/ppermute | solution.py:27

commit v8 on v6

--- a/solution.py
+++ b/solution.py
@@ -124,7 +124,7 @@
     copies = []
     for i, by in enumerate((0, *back_order)):
         place = lanes(count - by, own, count, owned, group_w)
-        pieces[i] = (gate_ref[:, place].astype(F32) * blocks[i][...].astype(F32)).astype(BF16)
+        pieces[i] = gate_ref[:, place] * blocks[i][...]
         copies.append(pltpu.make_async_copy(pieces.at[i], out_ref.at[:, place], sems.at[i]))
         copies[i].start()
     for copy in copies:

time: 28.6 us -> 28.6 us (level)
  no operation moved by 1% of the time
where the time goes in v8:
time: 28.6 us; the launch traced here: 28.5 us
  starting transfers between devices  21.3 us (74%)
  Pallas kernels  4.6 us (16%)
  waiting for transfers between devices  2.49 us (9%)
    ppermute x12, starting transfers between devices, rotated(): lax.ppermute(array, 'ctx', [(i, (i + by) % count) for i in range(count)])  21.3 us
    ppermute x12, waiting for transfers between devices, rotated(): lax.ppermute(array, 'ctx', [(i, (i + by) % count) for i in range(count)])  2.49 us
    pallas_call x3, Pallas kernels, dealt(): pl.pallas_call(kernel, in_specs=[anywhere] + [vmem if step == 2 else anyw...  1.81 us
    pallas_call x2, Pallas kernels, dealt(): pl.pallas_call(functools.partial(gate_kernel, count, owned, own, back_ord...  1.53 us
    pallas_call x2, Pallas kernels, dealt(): pl.pallas_call(functools.partial(mix_kernel, count, lags, own, out_order,...  1.26 us
  transfers between devices with their start and end apart: 12, of which 2 were waited for; matrix products, arithmetic and copies ran while one was open for 0% of the time, Pallas kernels for 10%

profile of v8, /device:TPU:0, one launch (start us, length us, event | category | flops | bytes accessed | tf_op | source)
XLA Modules:
  0.0 28.5 jit_solution(84282045308356361)
XLA Ops:
  0.0 1.0 %deal.3 = (bf16[256,128]{1,0:T(8,128)(2,1)S(1)}, f32[8,768]{1,0:T(8,128)S(1)}, s32[1,8]{1,0:T(1,128)S(1)}, f32[8,128]{1,0:T(8,128)S(1)}, s32[1,128]{1,0:T(1,128)S(1)}) custom-call(bf16[256,1024]{1,0:T(8,128)(2,1)} %x_ref.5, f32[8,768]{1,0:T(8,128)} %refs_0_.1, s32[1,8]{1,0:T(1,128)} %bitcast.4, f32[8,128]{1,0:T(8,128)} %bitcast.3, s32[1,128]{1,0:T(1,128)} %bitcast.5), custom_call_target="tpu_custom_call" | custom-call | tf_op jit(solution)/shard_map/deal/pallas_call | solution.py:164
  1.0 4.1 %collective-permute-start.6 = (bf16[256,128]{1,0:T(8,128)(2,1)S(1)}, bf16[256,128]{1,0:T(8,128)(2,1)S(1)}, u32[]{:S(2)}, u32[]{:S(2)}) collective-permute-start(bf16[256,128]{1,0:T(8,128)(2,1)S(1)} %get-tuple-element.44), channel_id=1, source_target_pairs={{0,8},{4,12},{8,0},{12,4},{1,9},{5,13},{9,1},{13,5},{2,10},{6,14},... | collective-permute-start | bytes 196616 | tf_op jit(solution)/shard_map/ppermute | solution.py:21
  5.1 0.0 copy-done
  5.1 0.1 deal.5
  5.2 1.6 %collective-permute-start.7 = (bf16[256,128]{1,0:T(8,128)(2,1)S(1)}, bf16[256,128]{1,0:T(8,128)(2,1)S(1)}, u32[]{:S(2)}, u32[]{:S(2)}) collective-permute-start(bf16[256,128]{1,0:T(8,128)(2,1)S(1)} %get-tuple-element.45), channel_id=1, source_target_pairs={{0,4},{4,8},{8,12},{12,0},{1,5},{5,9},{9,13},{13,1},{2,6},{6,10},{... | collective-permute-start | bytes 196616 | tf_op jit(solution)/shard_map/ppermute | solution.py:21
  6.8 2.2 %collective-permute-start.8 = (bf16[256,128]{1,0:T(8,128)(2,1)S(1)}, bf16[256,128]{1,0:T(8,128)(2,1)S(1)}, u32[]{:S(2)}, u32[]{:S(2)}) collective-permute-start(bf16[256,128]{1,0:T(8,128)(2,1)S(1)} %get-tuple-element.46), channel_id=1, source_target_pairs={{0,12},{4,0},{8,4},{12,8},{1,13},{5,1},{9,5},{13,9},{2,14},{6,2},{... | collective-permute-start | bytes 196616 | tf_op jit(solution)/shard_map/ppermute | solution.py:21
  9.1 0.0 collective-permute-start
  9.1 0.6 %collective-permute-start.1 = (bf16[256,128]{1,0:T(8,128)(2,1)S(1)}, bf16[256,128]{1,0:T(8,128)(2,1)S(1)}, u32[]{:S(2)}, u32[]{:S(2)}) collective-permute-start(bf16[256,128]{1,0:T(8,128)(2,1)S(1)} %get-tuple-element.34), channel_id=1, source_target_pairs={{0,4},{4,8},{8,12},{12,0},{1,5},{5,9},{9,13},{13,1},{2,6},{6,10},{... | collective-permute-start | bytes 196616 | tf_op jit(solution)/shard_map/ppermute | solution.py:21
  9.6 0.7 %deal.4 = (bf16[256,128]{1,0:T(8,128)(2,1)S(1)}, bf16[256,128]{1,0:T(8,128)(2,1)S(1)}, bf16[256,128]{1,0:T(8,128)(2,1)S(1)}, bf16[2,4,256,256]{3,2,1,0:T(8,128)(...) custom-call(bf16[256,1024]{1,0:T(8,128)(2,1)S(1)} %copy-done, ...), custom_call_target="tpu_custom_call" | custom-call | tf_op jit(solution)/shard_map/deal/pallas_call | solution.py:164
  10.4 0.0 collective-permute-done.6.refs_1_
  10.4 3.3 %collective-permute-start.2 = (bf16[256,128]{1,0:T(8,128)(2,1)S(1)}, bf16[256,128]{1,0:T(8,128)(2,1)S(1)}, u32[]{:S(2)}, u32[]{:S(2)}) collective-permute-start(bf16[256,128]{1,0:T(8,128)(2,1)S(1)} %get-tuple-element.35), channel_id=1, source_target_pairs={{0,12},{4,0},{8,4},{12,8},{1,13},{5,1},{9,5},{13,9},{2,14},{6,2},{... | collective-permute-start | bytes 196616 | tf_op jit(solution)/shard_map/ppermute | solution.py:21
  13.7 0.0 collective-permute-done.7.refs_2_
  13.7 0.0 collective-permute-done.8.refs_3_
  13.7 0.6 %mix.3 = (bf16[256,128]{1,0:T(8,128)(2,1)S(1)}, bf16[256,128]{1,0:T(8,128)(2,1)S(1)}, bf16[256,128]{1,0:T(8,128)(2,1)S(1)}, bf16[256,128]{1,0:T(8,128)(2,1)S(1)}) custom-call(bf16[256,128]{1,0:T(8,128)(2,1)S(1)} %get-tuple-element.43.refs_0_, bf16[256,128]{1,0:T(8,128)(2,1)S(1)} %collective-permute-done.6.refs_1_, ...), custom_call_target="tpu_custom_call" | custom-call | tf_op jit(solution)/shard_map/mix/pallas_call | solution.py:178
  14.3 0.1 collective-permute-start.9
  14.5 2.5 %collective-permute-start.10 = (bf16[256,128]{1,0:T(8,128)(2,1)S(1)}, bf16[256,128]{1,0:T(8,128)(2,1)S(1)}, u32[]{:S(2)}, u32[]{:S(2)}) collective-permute-start(bf16[256,128]{1,0:T(8,128)(2,1)S(1)} %get-tuple-element.49), channel_id=1, source_target_pairs={{0,8},{4,12},{8,0},{12,4},{1,9},{5,13},{9,1},{13,5},{2,10},{6,14},... | collective-permute-start | bytes 196616 | tf_op jit(solution)/shard_map/ppermute | solution.py:21
  17.0 0.0 collective-permute-done.refs_1_
  17.0 2.5 %collective-permute-start.11 = (bf16[256,128]{1,0:T(8,128)(2,1)S(1)}, bf16[256,128]{1,0:T(8,128)(2,1)S(1)}, u32[]{:S(2)}, u32[]{:S(2)}) collective-permute-start(bf16[256,128]{1,0:T(8,128)(2,1)S(1)} %get-tuple-element.50), channel_id=1, source_target_pairs={{0,12},{4,0},{8,4},{12,8},{1,13},{5,1},{9,5},{13,9},{2,14},{6,2},{... | collective-permute-start | bytes 196616 | tf_op jit(solution)/shard_map/ppermute | solution.py:21
  19.5 0.0 collective-permute-done.1.refs_2_
  19.5 0.0 collective-permute-done.2.refs_3_
  19.5 0.6 %mix.2 = (bf16[256,128]{1,0:T(8,128)(2,1)S(1)}, bf16[256,128]{1,0:T(8,128)(2,1)S(1)}, bf16[256,128]{1,0:T(8,128)(2,1)S(1)}, bf16[256,128]{1,0:T(8,128)(2,1)S(1)}) custom-call(bf16[256,128]{1,0:T(8,128)(2,1)S(1)} %get-tuple-element.32.refs_0_, bf16[256,128]{1,0:T(8,128)(2,1)S(1)} %collective-permute-done.refs_1_, ...), custom_call_target="tpu_custom_call" | custom-call | tf_op jit(solution)/shard_map/mix/pallas_call | solution.py:178
  20.1 0.4 %collective-permute-start.3 = (bf16[256,128]{1,0:T(8,128)(2,1)S(1)}, bf16[256,128]{1,0:T(8,128)(2,1)S(1)}, u32[]{:S(2)}, u32[]{:S(2)}) collective-permute-start(bf16[256,128]{1,0:T(8,128)(2,1)S(1)} %get-tuple-element.40), channel_id=1, source_target_pairs={{0,4},{4,8},{8,12},{12,0},{1,5},{5,9},{9,13},{13,1},{2,6},{6,10},{... | collective-permute-start | bytes 196616 | tf_op jit(solution)/shard_map/ppermute | solution.py:21
  20.5 1.1 %collective-permute-start.4 = (bf16[256,128]{1,0:T(8,128)(2,1)S(1)}, bf16[256,128]{1,0:T(8,128)(2,1)S(1)}, u32[]{:S(2)}, u32[]{:S(2)}) collective-permute-start(bf16[256,128]{1,0:T(8,128)(2,1)S(1)} %get-tuple-element.41), channel_id=1, source_target_pairs={{0,8},{4,12},{8,0},{12,4},{1,9},{5,13},{9,1},{13,5},{2,10},{6,14},... | collective-permute-start | bytes 196616 | tf_op jit(solution)/shard_map/ppermute | solution.py:21
  21.6 0.0 collective-permute-done.9.refs_1_
  21.6 2.8 %collective-permute-start.5 = (bf16[256,128]{1,0:T(8,128)(2,1)S(1)}, bf16[256,128]{1,0:T(8,128)(2,1)S(1)}, u32[]{:S(2)}, u32[]{:S(2)}) collective-permute-start(bf16[256,128]{1,0:T(8,128)(2,1)S(1)} %get-tuple-element.42), channel_id=1, source_target_pairs={{0,12},{4,0},{8,4},{12,8},{1,13},{5,1},{9,5},{13,9},{2,14},{6,2},{... | collective-permute-start | bytes 196616 | tf_op jit(solution)/shard_map/ppermute | solution.py:21
  24.4 0.0 collective-permute-done.10.refs_2_
  24.4 0.0 collective-permute-done.11.refs_3_
  24.4 0.8 %gate.2.refs_4_ = bf16[256,1024]{1,0:T(8,128)(2,1)} custom-call(bf16[256,1024]{1,0:T(8,128)(2,1)S(1)} %copy-done.1, bf16[256,128]{1,0:T(8,128)(2,1)S(1)} %get-tuple-element.47.refs_0_, bf16[256,128]{1,0:T(8,128)(2,1)S(1)} %collective-permute-done.9.refs_1_, bf16[256,128]{1,0:T(8,128)(2,1)S(1)} %collective-permute-done.10.refs_2_, ...), custom_call_target="tpu_custom_call" | custom-call | tf_op jit(solution)/shard_map/gate/pallas_call | solution.py:191
  25.2 1.1 %collective-permute-done.3.refs_1_ = bf16[256,128]{1,0:T(8,128)(2,1)S(1)} collective-permute-done((bf16[256,128]{1,0:T(8,128)(2,1)S(1)}, bf16[256,128]{1,0:T(8,128)(2,1)S(1)}, u32[]{:S(2)}, u32[]{:S(2)}) %collective-permute-start.3) | collective-permute-done | bytes 65568 | tf_op jit(solution)/shard_map/ppermute | solution.py:21
  26.4 1.3 %collective-permute-done.4.refs_2_ = bf16[256,128]{1,0:T(8,128)(2,1)S(1)} collective-permute-done((bf16[256,128]{1,0:T(8,128)(2,1)S(1)}, bf16[256,128]{1,0:T(8,128)(2,1)S(1)}, u32[]{:S(2)}, u32[]{:S(2)}) %collective-permute-start.4) | collective-permute-done | bytes 65568 | tf_op jit(solution)/shard_map/ppermute | solution.py:21
  27.7 0.0 collective-permute-done.5.refs_3_
  27.7 0.8 %gate.3 = bf16[256,1024]{1,0:T(8,128)(2,1)} custom-call(bf16[256,1024]{1,0:T(8,128)(2,1)S(1)} %copy-done.1, bf16[256,128]{1,0:T(8,128)(2,1)S(1)} %get-tuple-element.39.refs_0_, bf16[256,128]{1,0:T(8,128)(2,1)S(1)} %collective-permute-done.3.refs_1_, bf16[256,128]{1,0:T(8,128)(2,1)S(1)} %collective-permute-done.4.refs_2_, ...), custom_call_target="tpu_custom_call", output_to_operand_aliasing={{}: (5, {})} | custom-call | tf_op jit(solution)/shard_map/gate/pallas_call | solution.py:191
  (3 shorter events, 0.0 us)
Async XLA Ops:
  0.0 5.1 %copy-start = (bf16[256,1024]{1,0:T(8,128)(2,1)S(1)}, bf16[256,1024]{1,0:T(8,128)(2,1)}, u32[]{:S(2)}) copy-start(bf16[256,1024]{1,0:T(8,128)(2,1)} %x_ref.5) | copy-start | bytes 1572868
  1.0 9.4 %collective-permute-start.6 = (bf16[256,128]{1,0:T(8,128)(2,1)S(1)}, bf16[256,128]{1,0:T(8,128)(2,1)S(1)}, u32[]{:S(2)}, u32[]{:S(2)}) collective-permute-start(bf16[256,128]{1,0:T(8,128)(2,1)S(1)} %get-tuple-element.44), channel_id=1, source_target_pairs={{0,8},{4,12},{8,0},{12,4},{1,9},{5,13},{9,1},{13,5},{2,10},{6,14},... | collective-permute-start | bytes 196616 | tf_op jit(solution)/shard_map/ppermute | solution.py:21
  5.2 8.5 %collective-permute-start.7 = (bf16[256,128]{1,0:T(8,128)(2,1)S(1)}, bf16[256,128]{1,0:T(8,128)(2,1)S(1)}, u32[]{:S(2)}, u32[]{:S(2)}) collective-permute-start(bf16[256,128]{1,0:T(8,128)(2,1)S(1)} %get-tuple-element.45), channel_id=1, source_target_pairs={{0,4},{4,8},{8,12},{12,0},{1,5},{5,9},{9,13},{13,1},{2,6},{6,10},{... | collective-permute-start | bytes 196616 | tf_op jit(solution)/shard_map/ppermute | solution.py:21
  6.8 6.9 %collective-permute-start.8 = (bf16[256,128]{1,0:T(8,128)(2,1)S(1)}, bf16[256,128]{1,0:T(8,128)(2,1)S(1)}, u32[]{:S(2)}, u32[]{:S(2)}) collective-permute-start(bf16[256,128]{1,0:T(8,128)(2,1)S(1)} %get-tuple-element.46), channel_id=1, source_target_pairs={{0,12},{4,0},{8,4},{12,8},{1,13},{5,1},{9,5},{13,9},{2,14},{6,2},{... | collective-permute-start | bytes 196616 | tf_op jit(solution)/shard_map/ppermute | solution.py:21
  9.1 7.9 %collective-permute-start = (bf16[256,128]{1,0:T(8,128)(2,1)S(1)}, bf16[256,128]{1,0:T(8,128)(2,1)S(1)}, u32[]{:S(2)}, u32[]{:S(2)}) collective-permute-start(bf16[256,128]{1,0:T(8,128)(2,1)S(1)} %get-tuple-element.33), channel_id=1, source_target_pairs={{0,8},{4,12},{8,0},{12,4},{1,9},{5,13},{9,1},{13,5},{2,10},{6,14},... | collective-permute-start | bytes 196616 | tf_op jit(solution)/shard_map/ppermute | solution.py:21
  9.1 10.4 %collective-permute-start.1 = (bf16[256,128]{1,0:T(8,128)(2,1)S(1)}, bf16[256,128]{1,0:T(8,128)(2,1)S(1)}, u32[]{:S(2)}, u32[]{:S(2)}) collective-permute-start(bf16[256,128]{1,0:T(8,128)(2,1)S(1)} %get-tuple-element.34), channel_id=1, source_target_pairs={{0,4},{4,8},{8,12},{12,0},{1,5},{5,9},{9,13},{13,1},{2,6},{6,10},{... | collective-permute-start | bytes 196616 | tf_op jit(solution)/shard_map/ppermute | solution.py:21
  10.4 9.1 %collective-permute-start.2 = (bf16[256,128]{1,0:T(8,128)(2,1)S(1)}, bf16[256,128]{1,0:T(8,128)(2,1)S(1)}, u32[]{:S(2)}, u32[]{:S(2)}) collective-permute-start(bf16[256,128]{1,0:T(8,128)(2,1)S(1)} %get-tuple-element.35), channel_id=1, source_target_pairs={{0,12},{4,0},{8,4},{12,8},{1,13},{5,1},{9,5},{13,9},{2,14},{6,2},{... | collective-permute-start | bytes 196616 | tf_op jit(solution)/shard_map/ppermute | solution.py:21
  14.3 7.3 %collective-permute-start.9 = (bf16[256,128]{1,0:T(8,128)(2,1)S(1)}, bf16[256,128]{1,0:T(8,128)(2,1)S(1)}, u32[]{:S(2)}, u32[]{:S(2)}) collective-permute-start(bf16[256,128]{1,0:T(8,128)(2,1)S(1)} %get-tuple-element.48), channel_id=1, source_target_pairs={{0,4},{4,8},{8,12},{12,0},{1,5},{5,9},{9,13},{13,1},{2,6},{6,10},{... | collective-permute-start | bytes 196616 | tf_op jit(solution)/shard_map/ppermute | solution.py:21
  14.5 10.0 %collective-permute-start.10 = (bf16[256,128]{1,0:T(8,128)(2,1)S(1)}, bf16[256,128]{1,0:T(8,128)(2,1)S(1)}, u32[]{:S(2)}, u32[]{:S(2)}) collective-permute-start(bf16[256,128]{1,0:T(8,128)(2,1)S(1)} %get-tuple-element.49), channel_id=1, source_target_pairs={{0,8},{4,12},{8,0},{12,4},{1,9},{5,13},{9,1},{13,5},{2,10},{6,14},... | collective-permute-start | bytes 196616 | tf_op jit(solution)/shard_map/ppermute | solution.py:21
  17.0 7.5 %collective-permute-start.11 = (bf16[256,128]{1,0:T(8,128)(2,1)S(1)}, bf16[256,128]{1,0:T(8,128)(2,1)S(1)}, u32[]{:S(2)}, u32[]{:S(2)}) collective-permute-start(bf16[256,128]{1,0:T(8,128)(2,1)S(1)} %get-tuple-element.50), channel_id=1, source_target_pairs={{0,12},{4,0},{8,4},{12,8},{1,13},{5,1},{9,5},{13,9},{2,14},{6,2},{... | collective-permute-start | bytes 196616 | tf_op jit(solution)/shard_map/ppermute | solution.py:21
  19.5 5.0 %copy-start.1 = (bf16[256,1024]{1,0:T(8,128)(2,1)S(1)}, bf16[256,1024]{1,0:T(8,128)(2,1)}, u32[]{:S(2)}) copy-start(bf16[256,1024]{1,0:T(8,128)(2,1)} %gate_ref.3) | copy-start | bytes 1572868
  20.1 6.2 %collective-permute-start.3 = (bf16[256,128]{1,0:T(8,128)(2,1)S(1)}, bf16[256,128]{1,0:T(8,128)(2,1)S(1)}, u32[]{:S(2)}, u32[]{:S(2)}) collective-permute-start(bf16[256,128]{1,0:T(8,128)(2,1)S(1)} %get-tuple-element.40), channel_id=1, source_target_pairs={{0,4},{4,8},{8,12},{12,0},{1,5},{5,9},{9,13},{13,1},{2,6},{6,10},{... | collective-permute-start | bytes 196616 | tf_op jit(solution)/shard_map/ppermute | solution.py:21
  20.5 7.2 %collective-permute-start.4 = (bf16[256,128]{1,0:T(8,128)(2,1)S(1)}, bf16[256,128]{1,0:T(8,128)(2,1)S(1)}, u32[]{:S(2)}, u32[]{:S(2)}) collective-permute-start(bf16[256,128]{1,0:T(8,128)(2,1)S(1)} %get-tuple-element.41), channel_id=1, source_target_pairs={{0,8},{4,12},{8,0},{12,4},{1,9},{5,13},{9,1},{13,5},{2,10},{6,14},... | collective-permute-start | bytes 196616 | tf_op jit(solution)/shard_map/ppermute | solution.py:21
  21.6 6.1 %collective-permute-start.5 = (bf16[256,128]{1,0:T(8,128)(2,1)S(1)}, bf16[256,128]{1,0:T(8,128)(2,1)S(1)}, u32[]{:S(2)}, u32[]{:S(2)}) collective-permute-start(bf16[256,128]{1,0:T(8,128)(2,1)S(1)} %get-tuple-element.42), channel_id=1, source_target_pairs={{0,12},{4,0},{8,4},{12,8},{1,13},{5,1},{9,5},{13,9},{2,14},{6,2},{... | collective-permute-start | bytes 196616 | tf_op jit(solution)/shard_map/ppermute | solution.py:21

commit v9 on v7

--- a/solution.py
+++ b/solution.py
@@ -33,7 +33,7 @@
 
 def rounds(count):
     if count == 4:
-        return (2, 1, 3), (((1, 2, 3), (1, 2, 3)), ((1, 2, 3), (2, 1, 3)))
+        return (2, 1, 3), (((1, 2, 3), (1, 2, 3)), ((2, 1, 3), (2, 1, 3)))
     plain = tuple(range(1, count))
     return plain, ((plain, plain),) * 8
 

time: 28.6 us -> 28.8 us (level)
  starting transfers between devices: 21.3 us -> 22.2 us
  waiting for transfers between devices: 2.48 us -> 1.75 us
    ppermute x6, starting transfers between devices: 9.41 us -> 10.3 us  [returned(): return lax.ppermute(array, ('ctx', 'sub'), pairs)]
    ppermute x6, waiting for transfers between devices: 2.46 us -> 1.73 us  [returned(): return lax.ppermute(array, ('ctx', 'sub'), pairs)]
  transfers between devices with their start and end apart: 12 -> 12, of which waited for: 2 -> 3; matrix products, arithmetic and copies ran while one was open for 0% -> 0% of each run, Pallas kernels for 10% -> 10%
where the time goes in v9:
time: 28.8 us; the launch traced here: 28.6 us
  starting transfers between devices  22.2 us (77%)
  Pallas kernels  4.6 us (16%)
  waiting for transfers between devices  1.75 us (6%)
    ppermute x6, starting transfers between devices, rotated(): lax.ppermute(array, 'ctx', [(i, (i + by) % count) for i in range(count)])  11.9 us
    ppermute x6, starting transfers between devices, returned(): return lax.ppermute(array, ('ctx', 'sub'), pairs)  10.3 us
    pallas_call x3, Pallas kernels, dealt(): pl.pallas_call(kernel, in_specs=[anywhere] + [vmem if step == 2 else anyw...  1.81 us
    ppermute x6, waiting for transfers between devices, returned(): return lax.ppermute(array, ('ctx', 'sub'), pairs)  1.73 us
    pallas_call x2, Pallas kernels, dealt(): pl.pallas_call(functools.partial(gate_kernel, count, owned, own, back_ord...  1.53 us
    pallas_call x2, Pallas kernels, dealt(): pl.pallas_call(functools.partial(mix_kernel, count, lags, own, out_order,...  1.26 us
  transfers between devices with their start and end apart: 12, of which 3 were waited for; matrix products, arithmetic and copies ran while one was open for 0% of the time, Pallas kernels for 10%

profile of v9, /device:TPU:0, one launch (start us, length us, event | category | flops | bytes accessed | tf_op | source)
XLA Modules:
  0.0 28.6 jit_solution(12260637750300020514)
XLA Ops:
  0.0 1.0 %deal.3 = (bf16[256,128]{1,0:T(8,128)(2,1)S(1)}, f32[8,768]{1,0:T(8,128)S(1)}, s32[1,8]{1,0:T(1,128)S(1)}, f32[8,128]{1,0:T(8,128)S(1)}, s32[1,128]{1,0:T(1,128)S(1)}) custom-call(bf16[256,1024]{1,0:T(8,128)(2,1)} %x_ref.5, f32[8,768]{1,0:T(8,128)} %refs_0_.1, s32[1,8]{1,0:T(1,128)} %bitcast.4, f32[8,128]{1,0:T(8,128)} %bitcast.3, s32[1,128]{1,0:T(1,128)} %bitcast.5), custom_call_target="tpu_custom_call" | custom-call | tf_op jit(solution)/shard_map/deal/pallas_call | solution.py:177
  1.0 4.1 %collective-permute-start.6 = (bf16[256,128]{1,0:T(8,128)(2,1)S(1)}, bf16[256,128]{1,0:T(8,128)(2,1)S(1)}, u32[]{:S(2)}, u32[]{:S(2)}) collective-permute-start(bf16[256,128]{1,0:T(8,128)(2,1)S(1)} %get-tuple-element.44), channel_id=1, source_target_pairs={{0,8},{4,12},{8,0},{12,4},{1,9},{5,13},{9,1},{13,5},{2,10},{6,14},... | collective-permute-start | bytes 196616 | tf_op jit(solution)/shard_map/ppermute | solution.py:21
  5.1 0.1 deal.5
  5.2 1.6 %collective-permute-start.7 = (bf16[256,128]{1,0:T(8,128)(2,1)S(1)}, bf16[256,128]{1,0:T(8,128)(2,1)S(1)}, u32[]{:S(2)}, u32[]{:S(2)}) collective-permute-start(bf16[256,128]{1,0:T(8,128)(2,1)S(1)} %get-tuple-element.45), channel_id=1, source_target_pairs={{0,4},{4,8},{8,12},{12,0},{1,5},{5,9},{9,13},{13,1},{2,6},{6,10},{... | collective-permute-start | bytes 196616 | tf_op jit(solution)/shard_map/ppermute | solution.py:21
  6.8 2.2 %collective-permute-start.8 = (bf16[256,128]{1,0:T(8,128)(2,1)S(1)}, bf16[256,128]{1,0:T(8,128)(2,1)S(1)}, u32[]{:S(2)}, u32[]{:S(2)}) collective-permute-start(bf16[256,128]{1,0:T(8,128)(2,1)S(1)} %get-tuple-element.46), channel_id=1, source_target_pairs={{0,12},{4,0},{8,4},{12,8},{1,13},{5,1},{9,5},{13,9},{2,14},{6,2},{... | collective-permute-start | bytes 196616 | tf_op jit(solution)/shard_map/ppermute | solution.py:21
  9.1 0.0 collective-permute-start
  9.1 0.6 %collective-permute-start.1 = (bf16[256,128]{1,0:T(8,128)(2,1)S(1)}, bf16[256,128]{1,0:T(8,128)(2,1)S(1)}, u32[]{:S(2)}, u32[]{:S(2)}) collective-permute-start(bf16[256,128]{1,0:T(8,128)(2,1)S(1)} %get-tuple-element.34), channel_id=1, source_target_pairs={{0,4},{4,8},{8,12},{12,0},{1,5},{5,9},{9,13},{13,1},{2,6},{6,10},{... | collective-permute-start | bytes 196616 | tf_op jit(solution)/shard_map/ppermute | solution.py:21
  9.6 0.7 %deal.4 = (bf16[256,128]{1,0:T(8,128)(2,1)S(1)}, bf16[256,128]{1,0:T(8,128)(2,1)S(1)}, bf16[256,128]{1,0:T(8,128)(2,1)S(1)}, bf16[2,4,256,256]{3,2,1,0:T(8,128)(...) custom-call(bf16[256,1024]{1,0:T(8,128)(2,1)S(1)} %copy-done, ...), custom_call_target="tpu_custom_call" | custom-call | tf_op jit(solution)/shard_map/deal/pallas_call | solution.py:177
  10.4 0.0 collective-permute-done.6.refs_1_
  10.4 3.3 %collective-permute-start.2 = (bf16[256,128]{1,0:T(8,128)(2,1)S(1)}, bf16[256,128]{1,0:T(8,128)(2,1)S(1)}, u32[]{:S(2)}, u32[]{:S(2)}) collective-permute-start(bf16[256,128]{1,0:T(8,128)(2,1)S(1)} %get-tuple-element.35), channel_id=1, source_target_pairs={{0,12},{4,0},{8,4},{12,8},{1,13},{5,1},{9,5},{13,9},{2,14},{6,2},{... | collective-permute-start | bytes 196616 | tf_op jit(solution)/shard_map/ppermute | solution.py:21
  13.7 0.0 collective-permute-done.7.refs_2_
  13.7 0.0 collective-permute-done.8.refs_3_
  13.7 0.6 %mix.3 = (bf16[256,128]{1,0:T(8,128)(2,1)S(1)}, bf16[256,128]{1,0:T(8,128)(2,1)S(1)}, bf16[256,128]{1,0:T(8,128)(2,1)S(1)}, bf16[256,128]{1,0:T(8,128)(2,1)S(1)}) custom-call(bf16[256,128]{1,0:T(8,128)(2,1)S(1)} %get-tuple-element.43.refs_0_, bf16[256,128]{1,0:T(8,128)(2,1)S(1)} %collective-permute-done.6.refs_1_, ...), custom_call_target="tpu_custom_call" | custom-call | tf_op jit(solution)/shard_map/mix/pallas_call | solution.py:191
  14.3 0.1 collective-permute-start.9
  14.5 2.5 %collective-permute-start.10 = (bf16[256,128]{1,0:T(8,128)(2,1)S(1)}, bf16[256,128]{1,0:T(8,128)(2,1)S(1)}, u32[]{:S(2)}, u32[]{:S(2)}) collective-permute-start(bf16[256,128]{1,0:T(8,128)(2,1)S(1)} %get-tuple-element.49), channel_id=1, source_target_pairs={{0,8},{4,12},{8,0},{12,4},{1,9},{5,13},{9,1},{13,5},{2,10},{6,14},... | collective-permute-start | bytes 196616 | tf_op jit(solution)/shard_map/ppermute | solution.py:27
  17.0 0.0 collective-permute-done.refs_1_
  17.0 2.5 %collective-permute-start.11 = (bf16[256,128]{1,0:T(8,128)(2,1)S(1)}, bf16[256,128]{1,0:T(8,128)(2,1)S(1)}, u32[]{:S(2)}, u32[]{:S(2)}) collective-permute-start(bf16[256,128]{1,0:T(8,128)(2,1)S(1)} %get-tuple-element.50), channel_id=1, source_target_pairs={{0,12},{4,0},{8,4},{12,8},{1,13},{5,1},{9,5},{13,9},{2,14},{6,2},{... | collective-permute-start | bytes 196616 | tf_op jit(solution)/shard_map/ppermute | solution.py:27
  19.5 0.0 collective-permute-done.1.refs_2_
  19.5 0.0 collective-permute-done.2.refs_3_
  19.5 0.6 %mix.2 = (bf16[256,128]{1,0:T(8,128)(2,1)S(1)}, bf16[256,128]{1,0:T(8,128)(2,1)S(1)}, bf16[256,128]{1,0:T(8,128)(2,1)S(1)}, bf16[256,128]{1,0:T(8,128)(2,1)S(1)}) custom-call(bf16[256,128]{1,0:T(8,128)(2,1)S(1)} %get-tuple-element.32.refs_0_, bf16[256,128]{1,0:T(8,128)(2,1)S(1)} %collective-permute-done.refs_1_, ...), custom_call_target="tpu_custom_call" | custom-call | tf_op jit(solution)/shard_map/mix/pallas_call | solution.py:191
  20.1 1.4 %collective-permute-start.3 = (bf16[256,128]{1,0:T(8,128)(2,1)S(1)}, bf16[256,128]{1,0:T(8,128)(2,1)S(1)}, u32[]{:S(2)}, u32[]{:S(2)}) collective-permute-start(bf16[256,128]{1,0:T(8,128)(2,1)S(1)} %get-tuple-element.40), channel_id=1, source_target_pairs={{0,8},{4,12},{8,0},{12,4},{1,9},{5,13},{9,1},{13,5},{2,10},{6,14},... | collective-permute-start | bytes 196616 | tf_op jit(solution)/shard_map/ppermute | solution.py:27
  21.5 0.1 collective-permute-start.4
  21.6 0.0 collective-permute-done.9.refs_1_
  21.6 3.7 %collective-permute-start.5 = (bf16[256,128]{1,0:T(8,128)(2,1)S(1)}, bf16[256,128]{1,0:T(8,128)(2,1)S(1)}, u32[]{:S(2)}, u32[]{:S(2)}) collective-permute-start(bf16[256,128]{1,0:T(8,128)(2,1)S(1)} %get-tuple-element.42), channel_id=1, source_target_pairs={{0,12},{4,0},{8,4},{12,8},{1,13},{5,1},{9,5},{13,9},{2,14},{6,2},{... | collective-permute-start | bytes 196616 | tf_op jit(solution)/shard_map/ppermute | solution.py:27
  25.3 0.0 collective-permute-done.10.refs_2_
  25.4 0.0 collective-permute-done.11.refs_3_
  25.4 0.0 copy-done.1
  25.4 0.8 %gate.2.refs_4_ = bf16[256,1024]{1,0:T(8,128)(2,1)} custom-call(bf16[256,1024]{1,0:T(8,128)(2,1)S(1)} %copy-done.1, bf16[256,128]{1,0:T(8,128)(2,1)S(1)} %get-tuple-element.47.refs_0_, bf16[256,128]{1,0:T(8,128)(2,1)S(1)} %collective-permute-done.9.refs_1_, bf16[256,128]{1,0:T(8,128)(2,1)S(1)} %collective-permute-done.10.refs_2_, ...), custom_call_target="tpu_custom_call" | custom-call | tf_op jit(solution)/shard_map/gate/pallas_call | solution.py:204
  26.1 0.9 %collective-permute-done.3.refs_1_ = bf16[256,128]{1,0:T(8,128)(2,1)S(1)} collective-permute-done((bf16[256,128]{1,0:T(8,128)(2,1)S(1)}, bf16[256,128]{1,0:T(8,128)(2,1)S(1)}, u32[]{:S(2)}, u32[]{:S(2)}) %collective-permute-start.3) | collective-permute-done | bytes 65568 | tf_op jit(solution)/shard_map/ppermute | solution.py:27
  27.0 0.7 %collective-permute-done.4.refs_2_ = bf16[256,128]{1,0:T(8,128)(2,1)S(1)} collective-permute-done((bf16[256,128]{1,0:T(8,128)(2,1)S(1)}, bf16[256,128]{1,0:T(8,128)(2,1)S(1)}, u32[]{:S(2)}, u32[]{:S(2)}) %collective-permute-start.4) | collective-permute-done | bytes 65568 | tf_op jit(solution)/shard_map/ppermute | solution.py:27
  27.7 0.1 collective-permute-done.5.refs_3_
  27.9 0.8 %gate.3 = bf16[256,1024]{1,0:T(8,128)(2,1)} custom-call(bf16[256,1024]{1,0:T(8,128)(2,1)S(1)} %copy-done.1, bf16[256,128]{1,0:T(8,128)(2,1)S(1)} %get-tuple-element.39.refs_0_, bf16[256,128]{1,0:T(8,128)(2,1)S(1)} %collective-permute-done.3.refs_1_, bf16[256,128]{1,0:T(8,128)(2,1)S(1)} %collective-permute-done.4.refs_2_, ...), custom_call_target="tpu_custom_call", output_to_operand_aliasing={{}: (5, {})} | custom-call | tf_op jit(solution)/shard_map/gate/pallas_call | solution.py:204
  (3 shorter events, 0.0 us)
Async XLA Ops:
  0.0 5.1 %copy-start = (bf16[256,1024]{1,0:T(8,128)(2,1)S(1)}, bf16[256,1024]{1,0:T(8,128)(2,1)}, u32[]{:S(2)}) copy-start(bf16[256,1024]{1,0:T(8,128)(2,1)} %x_ref.5) | copy-start | bytes 1572868
  1.0 9.4 %collective-permute-start.6 = (bf16[256,128]{1,0:T(8,128)(2,1)S(1)}, bf16[256,128]{1,0:T(8,128)(2,1)S(1)}, u32[]{:S(2)}, u32[]{:S(2)}) collective-permute-start(bf16[256,128]{1,0:T(8,128)(2,1)S(1)} %get-tuple-element.44), channel_id=1, source_target_pairs={{0,8},{4,12},{8,0},{12,4},{1,9},{5,13},{9,1},{13,5},{2,10},{6,14},... | collective-permute-start | bytes 196616 | tf_op jit(solution)/shard_map/ppermute | solution.py:21
  5.2 8.5 %collective-permute-start.7 = (bf16[256,128]{1,0:T(8,128)(2,1)S(1)}, bf16[256,128]{1,0:T(8,128)(2,1)S(1)}, u32[]{:S(2)}, u32[]{:S(2)}) collective-permute-start(bf16[256,128]{1,0:T(8,128)(2,1)S(1)} %get-tuple-element.45), channel_id=1, source_target_pairs={{0,4},{4,8},{8,12},{12,0},{1,5},{5,9},{9,13},{13,1},{2,6},{6,10},{... | collective-permute-start | bytes 196616 | tf_op jit(solution)/shard_map/ppermute | solution.py:21
  6.8 6.9 %collective-permute-start.8 = (bf16[256,128]{1,0:T(8,128)(2,1)S(1)}, bf16[256,128]{1,0:T(8,128)(2,1)S(1)}, u32[]{:S(2)}, u32[]{:S(2)}) collective-permute-start(bf16[256,128]{1,0:T(8,128)(2,1)S(1)} %get-tuple-element.46), channel_id=1, source_target_pairs={{0,12},{4,0},{8,4},{12,8},{1,13},{5,1},{9,5},{13,9},{2,14},{6,2},{... | collective-permute-start | bytes 196616 | tf_op jit(solution)/shard_map/ppermute | solution.py:21
  9.1 7.9 %collective-permute-start = (bf16[256,128]{1,0:T(8,128)(2,1)S(1)}, bf16[256,128]{1,0:T(8,128)(2,1)S(1)}, u32[]{:S(2)}, u32[]{:S(2)}) collective-permute-start(bf16[256,128]{1,0:T(8,128)(2,1)S(1)} %get-tuple-element.33), channel_id=1, source_target_pairs={{0,8},{4,12},{8,0},{12,4},{1,9},{5,13},{9,1},{13,5},{2,10},{6,14},... | collective-permute-start | bytes 196616 | tf_op jit(solution)/shard_map/ppermute | solution.py:21
  9.1 10.4 %collective-permute-start.1 = (bf16[256,128]{1,0:T(8,128)(2,1)S(1)}, bf16[256,128]{1,0:T(8,128)(2,1)S(1)}, u32[]{:S(2)}, u32[]{:S(2)}) collective-permute-start(bf16[256,128]{1,0:T(8,128)(2,1)S(1)} %get-tuple-element.34), channel_id=1, source_target_pairs={{0,4},{4,8},{8,12},{12,0},{1,5},{5,9},{9,13},{13,1},{2,6},{6,10},{... | collective-permute-start | bytes 196616 | tf_op jit(solution)/shard_map/ppermute | solution.py:21
  10.4 9.1 %collective-permute-start.2 = (bf16[256,128]{1,0:T(8,128)(2,1)S(1)}, bf16[256,128]{1,0:T(8,128)(2,1)S(1)}, u32[]{:S(2)}, u32[]{:S(2)}) collective-permute-start(bf16[256,128]{1,0:T(8,128)(2,1)S(1)} %get-tuple-element.35), channel_id=1, source_target_pairs={{0,12},{4,0},{8,4},{12,8},{1,13},{5,1},{9,5},{13,9},{2,14},{6,2},{... | collective-permute-start | bytes 196616 | tf_op jit(solution)/shard_map/ppermute | solution.py:21
  14.3 7.3 %collective-permute-start.9 = (bf16[256,128]{1,0:T(8,128)(2,1)S(1)}, bf16[256,128]{1,0:T(8,128)(2,1)S(1)}, u32[]{:S(2)}, u32[]{:S(2)}) collective-permute-start(bf16[256,128]{1,0:T(8,128)(2,1)S(1)} %get-tuple-element.48), channel_id=1, source_target_pairs={{0,4},{4,8},{8,12},{12,0},{1,5},{5,9},{9,13},{13,1},{2,6},{6,10},{... | collective-permute-start | bytes 196616 | tf_op jit(solution)/shard_map/ppermute | solution.py:27
  14.5 10.9 %collective-permute-start.10 = (bf16[256,128]{1,0:T(8,128)(2,1)S(1)}, bf16[256,128]{1,0:T(8,128)(2,1)S(1)}, u32[]{:S(2)}, u32[]{:S(2)}) collective-permute-start(bf16[256,128]{1,0:T(8,128)(2,1)S(1)} %get-tuple-element.49), channel_id=1, source_target_pairs={{0,8},{4,12},{8,0},{12,4},{1,9},{5,13},{9,1},{13,5},{2,10},{6,14},... | collective-permute-start | bytes 196616 | tf_op jit(solution)/shard_map/ppermute | solution.py:27
  17.0 8.4 %collective-permute-start.11 = (bf16[256,128]{1,0:T(8,128)(2,1)S(1)}, bf16[256,128]{1,0:T(8,128)(2,1)S(1)}, u32[]{:S(2)}, u32[]{:S(2)}) collective-permute-start(bf16[256,128]{1,0:T(8,128)(2,1)S(1)} %get-tuple-element.50), channel_id=1, source_target_pairs={{0,12},{4,0},{8,4},{12,8},{1,13},{5,1},{9,5},{13,9},{2,14},{6,2},{... | collective-permute-start | bytes 196616 | tf_op jit(solution)/shard_map/ppermute | solution.py:27
  19.5 5.9 %copy-start.1 = (bf16[256,1024]{1,0:T(8,128)(2,1)S(1)}, bf16[256,1024]{1,0:T(8,128)(2,1)}, u32[]{:S(2)}) copy-start(bf16[256,1024]{1,0:T(8,128)(2,1)} %gate_ref.3) | copy-start | bytes 1572868
  20.1 6.9 %collective-permute-start.3 = (bf16[256,128]{1,0:T(8,128)(2,1)S(1)}, bf16[256,128]{1,0:T(8,128)(2,1)S(1)}, u32[]{:S(2)}, u32[]{:S(2)}) collective-permute-start(bf16[256,128]{1,0:T(8,128)(2,1)S(1)} %get-tuple-element.40), channel_id=1, source_target_pairs={{0,8},{4,12},{8,0},{12,4},{1,9},{5,13},{9,1},{13,5},{2,10},{6,14},... | collective-permute-start | bytes 196616 | tf_op jit(solution)/shard_map/ppermute | solution.py:27
  21.5 6.2 %collective-permute-start.4 = (bf16[256,128]{1,0:T(8,128)(2,1)S(1)}, bf16[256,128]{1,0:T(8,128)(2,1)S(1)}, u32[]{:S(2)}, u32[]{:S(2)}) collective-permute-start(bf16[256,128]{1,0:T(8,128)(2,1)S(1)} %get-tuple-element.41), channel_id=1, source_target_pairs={{0,4},{4,8},{8,12},{12,0},{1,5},{5,9},{9,13},{13,1},{2,6},{6,10},{... | collective-permute-start | bytes 196616 | tf_op jit(solution)/shard_map/ppermute | solution.py:27
  21.6 6.2 %collective-permute-start.5 = (bf16[256,128]{1,0:T(8,128)(2,1)S(1)}, bf16[256,128]{1,0:T(8,128)(2,1)S(1)}, u32[]{:S(2)}, u32[]{:S(2)}) collective-permute-start(bf16[256,128]{1,0:T(8,128)(2,1)S(1)} %get-tuple-element.42), channel_id=1, source_target_pairs={{0,12},{4,0},{8,4},{12,8},{1,13},{5,1},{9,5},{13,9},{2,14},{6,2},{... | collective-permute-start | bytes 196616 | tf_op jit(solution)/shard_map/ppermute | solution.py:27
